TPU v7x, 32 devices: a whole 2x2x4 slice. The times are simulated.
32 devices in a mesh: grp: 2 (over y), pool: 4 (over z), tp: 2 (over x), sub: 2 (over core).
Axes of the slice: x: 2, y: 2, z: 4, core: 2. Of those that a mesh axis runs over, the one named last changes fastest.
Arguments:
- queries: bfloat16 [128, 4096], P(('grp', 'pool', 'tp', 'sub')), parts along dimension 0, may hold values from -48 to 48
- keys_cache: bfloat16 [128, 512, 256], P(('grp', 'pool', 'tp', 'sub')), parts along dimension 0, may hold values from -6 to 6
- values_cache: bfloat16 [128, 512, 256], P(('grp', 'pool', 'tp', 'sub')), parts along dimension 0, may hold values from -6 to 6
- lengths: int32 [128], P(('grp', 'pool', 'tp', 'sub')), parts along dimension 0, may hold values from 2 to 512
- out_weight: bfloat16 [4096, 2048], P(('tp', 'sub')), may hold values from -0.75 to 0.75
- routes: int32 [128, 8], P(('grp', 'pool')), parts along dimension 0, may hold values from 0 to 63, all different within a row; in each aligned block of 16 rows (0 to 15, 16 to 31, ...) at most 14 rows name the same one
- route_weight: float32 [128, 8], P(('grp', 'pool')), parts along dimension 0, may hold values from 0.1 to 0.5
- expert_table: int32 [64], replicated, may hold values from 0 to 63, each once
- w_gate: bfloat16 [64, 768, 2048], P('pool', 'sub', 'tp'), may hold values from -0.125 to 0.125
- w_up: bfloat16 [64, 768, 2048], P('pool', 'sub', 'tp'), may hold values from -0.125 to 0.125
- w_down: bfloat16 [64, 768, 2048], P('pool', 'sub', 'tp'), may hold values from -0.875 to 0.875
Outputs:
- attended: bfloat16 [128, 2048], P(('grp', 'pool', 'tp', 'sub')), parts along dimension 0
- expert_out: bfloat16 [128, 2048], P(('grp', 'pool'), ('tp', 'sub')), parts along dimension 0
There are 2 independent parts, one for each index of `grp`. A program takes and returns all parts, laid end to end along the dimension named above; an argument that names none is the same for every part. Nothing has to cross between parts.
Inputs may be any that keep to these rules, and one draw needn't show every extreme that they name: `routes`: in each aligned block of 16 rows (the rows of one pool index) no expert is named by more than 14 rows, and in some block one expert is named by exactly 14 rows; each row names 8 different experts. `expert_table`: a permutation of the experts.
All inputs are finite; a program needn't handle non-finite values.
Results may differ from a plain program's by a relative error of at most 0.0086.
Values may be sent and summed in bfloat16 or wider, within the bound.
No kernel may reach another device: no remote copies, remote signals or barrier semaphores. Data moves between devices by JAX's collectives and lax.ppermute only.
A program may use at most 128 MiB of HBM per device.

v0:
```python
import math

import jax
import jax.numpy as jnp
from jax import lax
from jax.sharding import PartitionSpec as P

D = 2048
HEADS = 32
KV_HEADS = 2
HEAD_DIM = 128
EXPERTS = 64
TOP_K = 8
CAPACITY = 14


masked_low = -1e30


def body(
    queries,
    keys_cache,
    values_cache,
    lengths,
    out_weight,
    routes,
    route_weight,
    expert_table,
    w_gate,
    w_up,
    w_down,
):
    shard_index = lax.axis_index(("tp", "sub"))
    pool_count = lax.axis_size("pool")
    tp_count = lax.axis_size("tp")
    tp_index = lax.axis_index("tp")
    sub_count = lax.axis_size("sub")
    sub_index = lax.axis_index("sub")
    row_count = queries.shape[0]
    positions = keys_cache.shape[1]
    group_size = HEADS // KV_HEADS
    query_four = queries.reshape(row_count, KV_HEADS, group_size, HEAD_DIM)
    key_four = keys_cache.reshape(row_count, positions, KV_HEADS, HEAD_DIM)
    value_four = values_cache.reshape(row_count, positions, KV_HEADS, HEAD_DIM)
    scores = jnp.einsum(
        "rkgd,rlkd->rkgl", query_four, key_four, preferred_element_type=jnp.float32
    ) * (1.0 / math.sqrt(HEAD_DIM))
    in_range = (lax.iota(jnp.int32, positions)[None, :] < lengths[:, None])[:, None, None, :]
    masked = jnp.where(in_range, scores, masked_low)
    row_max = jnp.max(masked, axis=3, keepdims=True)
    exp_terms = jnp.where(in_range, jnp.exp(masked - row_max), 0.0)
    exp_sum = jnp.sum(exp_terms, axis=3)
    weights = exp_terms.astype(jnp.bfloat16)
    weighted = jnp.einsum(
        "rkgl,rlkd->rkgd", weights, value_four, preferred_element_type=jnp.float32
    )
    attention = (
        (weighted / exp_sum[..., None]).reshape(row_count, HEADS * HEAD_DIM).astype(jnp.bfloat16)
    )
    head_rows = lax.all_to_all(attention, ("tp", "sub"), split_axis=1, concat_axis=0, tiled=True)
    partial_value = jnp.dot(head_rows, out_weight, preferred_element_type=jnp.float32)
    summed = lax.psum(partial_value, ("tp", "sub"))
    attended_all = summed.astype(jnp.bfloat16)
    attended = lax.dynamic_slice_in_dim(attended_all, shard_index * row_count, row_count, 0)
    pool_rows = attended_all.shape[0]
    pair_count = pool_rows * TOP_K
    expert_ids = lax.iota(jnp.int32, EXPERTS)
    flat_routes = routes.reshape(pair_count)
    entry_index = jnp.sum(
        jnp.where(flat_routes[:, None] == expert_ids[None, :], expert_table[None, :], 0), axis=1
    )
    entry_hot = (entry_index[:, None] == expert_ids[None, :]).astype(jnp.int32)
    slot_rank = jnp.sum((jnp.cumsum(entry_hot, axis=0) - entry_hot) * entry_hot, axis=1)
    slot_index = entry_index * CAPACITY + slot_rank
    slot_total = EXPERTS * CAPACITY
    slot_hot = (slot_index[:, None] == lax.iota(jnp.int32, slot_total)[None, :]).astype(
        jnp.bfloat16
    )
    row_hot = (
        (lax.iota(jnp.int32, pair_count) // TOP_K)[:, None]
        == lax.iota(jnp.int32, pool_rows)[None, :]
    ).astype(jnp.bfloat16)
    placing = jnp.einsum("ps,pr->sr", slot_hot, row_hot, preferred_element_type=jnp.float32).astype(
        jnp.bfloat16
    )
    outgoing = jnp.dot(placing, attended_all, preferred_element_type=jnp.float32).astype(
        jnp.bfloat16
    )
    outgoing = outgoing.reshape(pool_count, EXPERTS // pool_count, CAPACITY, D)
    block_width = D // tp_count
    half_width = block_width // sub_count
    own_slice = lax.dynamic_slice_in_dim(
        outgoing, tp_index * block_width + sub_index * half_width, half_width, 3
    )
    arrived = lax.all_to_all(own_slice, "pool", split_axis=0, concat_axis=0, tiled=True)
    incoming = lax.all_gather(arrived, "sub", axis=3, tiled=True)
    gate_part = jnp.einsum("pjcd,jfd->pjcf", incoming, w_gate, preferred_element_type=jnp.float32)
    up_part = jnp.einsum("pjcd,jfd->pjcf", incoming, w_up, preferred_element_type=jnp.float32)
    gate_value, up_value = lax.psum((gate_part, up_part), "tp")
    hidden = (jax.nn.silu(gate_value) * up_value).astype(jnp.bfloat16)
    partial_rows = jnp.einsum("pjcf,jfd->pjcd", hidden, w_down, preferred_element_type=jnp.float32)
    expert_rows = lax.psum_scatter(partial_rows, "sub", scatter_dimension=3, tiled=True).astype(
        jnp.bfloat16
    )
    returned = lax.all_to_all(expert_rows, "pool", split_axis=0, concat_axis=0, tiled=True)
    flat_back = returned.reshape(slot_total, returned.shape[3])
    picked = jnp.take(flat_back, slot_index, axis=0).astype(jnp.float32)
    scaled = picked * route_weight.reshape(pair_count)[:, None]
    expert_out = jnp.sum(scaled.reshape(pool_rows, TOP_K, returned.shape[3]), axis=1).astype(
        jnp.bfloat16
    )
    return (attended, expert_out)


def solution(mesh):
    in_specs = (
        P(("grp", "pool", "tp", "sub"), None),
        P(("grp", "pool", "tp", "sub"), None, None),
        P(("grp", "pool", "tp", "sub"), None, None),
        P(("grp", "pool", "tp", "sub")),
        P(("tp", "sub"), None),
        P(("grp", "pool"), None),
        P(("grp", "pool"), None),
        P(),
        P("pool", "sub", "tp"),
        P("pool", "sub", "tp"),
        P("pool", "sub", "tp"),
    )
    out_specs = (P(("grp", "pool", "tp", "sub"), None), P(("grp", "pool"), ("tp", "sub")))
    return jax.shard_map(body, mesh=mesh, in_specs=in_specs, out_specs=out_specs, check_vma=False)
```

profile of v0, /device:TPU:0, one launch (start us, length us, event | category | flops | bytes accessed | tf_op | source)
XLA Modules:
  0.0 255.0 jit_solution(3014672523360081864)
XLA Ops:
  7.2 0.0 copy-start
  7.2 0.0 copy-start.3
  7.2 0.0 copy-start.5
  7.2 0.8 copy.48
  8.1 0.7 iota_compare_fusion.8
  8.8 0.0 copy-done
  8.8 0.4 fusion.16
  9.2 0.2 fusion.33
  9.4 1.5 fusion.17
  11.0 0.6 copy.36
  11.6 4.2 %all-to-all-start = ((bf16[4,4,1024]{2,0,1:T(4,128)(2,1)}), bf16[4,4,1024]{2,0,1:T(4,128)(2,1)S(1)}, u32[]{:S(2)}, u32[]{:S(2)}) async-start(bf16[4,4,1024]{2,0,1:T(4,128)(2,1)} %copy.36), calls=%async_computation | async-start | bytes 65536 | tf_op jit(solution)/shard_map/all_to_all | solution.py:60
  15.8 0.0 all-gather.2.cloned.1.call-start
  15.8 0.0 copy-done.3
  15.8 0.1 copy.37
  15.9 0.1 eq.26
  16.0 0.0 copy-done.5
  16.0 0.2 select_reduce_fusion.1
  16.1 0.1 fusion.26
  16.2 0.2 reduce_window_sum.11
  16.4 0.2 select_reduce_fusion
  16.6 3.1 %all-to-all-done = bf16[4,4,1024]{2,0,1:T(4,128)(2,1)S(1)} async-done(((bf16[4,4,1024]{2,0,1:T(4,128)(2,1)}), bf16[4,4,1024]{2,0,1:T(4,128)(2,1)S(1)}, u32[]{:S(2)}, u32[]{:S(2)}) %all-to-all-start) | async-done | bytes 32800 | tf_op jit(solution)/shard_map/all_to_all | solution.py:60
  19.7 2.8 %fusion.34 = f32[16,2048]{1,0:T(8,128)S(1)} fusion(bf16[16,1024]{1,0:T(8,128)(2,1)S(1)} %all_to_all.20, bf16[1024,2048]{1,0:T(8,128)(2,1)} %param.15), kind=kOutput, calls=%fused_computation.55 | convolution fusion | flops 67108864 | bytes 4358144 | tf_op jit(solution)/shard_map/dot_general | solution.py:61
  22.6 11.7 %all-reduce.5 = bf16[16,2048]{1,0:T(8,128)(2,1)S(1)} all-reduce(f32[16,2048]{1,0:T(8,128)S(1)} %fusion.34), channel_id=1, replica_groups=mesh['grp'=2,'pool'=4,'tp'=2,'sub'=2] {'tp','sub'}, use_global_device_ids=true, to_apply=%region_2.3 | all-reduce | flops 32768 | bytes 196608 | tf_op jit(solution)/shard_map/psum | solution.py:62
  34.3 3.2 %convolution_convert_fusion = bf16[896,2048]{1,0:T(8,128)(2,1)} fusion(bf16[16,2048]{1,0:T(8,128)(2,1)S(1)} %all-reduce.5, s32[128]{0:T(128)S(1)} %get-tuple-element.5, s32[128]{0:T(128)S(1)} %and_select_fusion), kind=kOutput, calls=%fused_computation.9 | convolution fusion | flops 64356352 | bytes 3736576 | tf_op jit(solution)/shard_map/dot_general | solution.py:86
  37.5 6.0 %reshape.116 = bf16[4,16,14,2048]{3,2,1,0:T(8,128)(2,1)} reshape(bf16[896,2048]{1,0:T(8,128)(2,1)} %convolution_convert_fusion) | data formatting | bytes 7340032 | tf_op jit(solution)/shard_map/reshape | solution.py:89
  43.5 1.3 constant_dynamic-slice_fusion
  44.8 0.5 copy.38
  45.4 28.3 %all_to_all.26 = bf16[4,16,14,512]{3,1,2,0:T(8,128)(2,1)S(1)} all-to-all(bf16[4,16,14,512]{3,1,2,0:T(8,128)(2,1)S(1)} %copy.38), channel_id=1, replica_groups=mesh['grp'=2,'pool'=4,'tp'=2,'sub'=2] {'pool'}, dimensions={0} | all-to-all | bytes 1835008 | tf_op jit(solution)/shard_map/all_to_all | solution.py:95
  73.7 1.5 copy.39
  75.2 0.0 all-gather.2.cloned.1.call-update
  75.2 0.0 all-reduce.4.cloned.1.call-start
  75.3 8.9 %all-gather.2.cloned.1.call-done = bf16[4,16,14,1024]{3,2,0,1:T(8,128)(2,1)} async-done(((bf16[4,16,14,512]{3,2,0,1:T(8,128)(2,1)}), bf16[4,16,14,1024]{3,2,0,1:T(8,128)(2,1)}) %all-gather.2.cloned.1.call-update) | async-done | bytes 1835024 | tf_op jit(solution)/shard_map/all_gather | solution.py:96
  84.1 0.0 copy-start.2
  84.1 10.5 %fusion.10 = f32[4,16,14,384]{3,2,0,1:T(8,128)} fusion(bf16[4,16,14,1024]{3,2,0,1:T(8,128)(2,1)} %all-gather.2.cloned.1.call-done, bf16[16,384,1024]{2,1,0:T(8,128)(2,1)} %param.20), kind=kOutput, calls=%fused_computation.12 | convolution fusion | flops 704643072 | bytes 15794176 | tf_op jit(solution)/shard_map/pjcd,jfd->pjcf/dot_general | solution.py:98
  94.6 0.0 copy-done.2
  94.6 9.8 %fusion.7 = f32[4,16,14,384]{3,2,0,1:T(8,128)} fusion(bf16[4,16,14,1024]{3,2,0,1:T(8,128)(2,1)S(1)} %copy-done.2, bf16[16,384,1024]{2,1,0:T(8,128)(2,1)} %param.19), kind=kOutput, calls=%fused_computation.11 | convolution fusion | flops 704643072 | bytes 15794176 | tf_op jit(solution)/shard_map/pjcd,jfd->pjcf/dot_general | solution.py:97
  104.4 0.0 all-reduce.4.cloned.1.call-update
  104.4 0.2 reduce-scatter.2.cloned.1.call-start
  104.7 87.0 %all-reduce.4.cloned.1.call-done = (f32[4,16,14,384]{3,2,0,1:T(8,128)}, f32[4,16,14,384]{3,2,0,1:T(8,128)}) async-done(((f32[4,16,14,384]{3,2,0,1:T(8,128)}, f32[4,16,14,384]{3,2,0,1:T(8,128)}), (f32[4,16,14,384]{3,2,0,1:T(8,128)}, f32[4,16,14,384]{3,2,0,1:T(8,128)})) %all-reduce.4.cloned.1.call-update) | async-done | bytes 2752528 | tf_op jit(solution)/shard_map/psum | solution.py:99
  191.7 7.9 %fusion.1 = f32[16,4,14,1024]{3,2,1,0:T(8,128)S(1)} fusion(bf16[16,384,1024]{2,1,0:T(8,128)(2,1)} %param.21, f32[4,16,14,384]{3,2,0,1:T(8,128)} %get-tuple-element.2, f32[4,16,14,384]{3,2,0,1:T(8,128)} %get-tuple-element.3), kind=kOutput, calls=%fused_computation.2 | convolution fusion | flops 706707456 | bytes 19005440 | tf_op jit(solution)/shard_map/pjcf,jfd->pjcd/dot_general | solution.py:101
  199.6 3.9 %copy.58 = f32[16,4,14,1024]{3,0,2,1:T(8,128)} copy(f32[16,4,14,1024]{3,2,1,0:T(8,128)S(1)} %fusion.1) | data formatting | bytes 7340032 | tf_op jit(solution)/shard_map/pjcf,jfd->pjcd/dot_general | solution.py:101
  203.5 0.0 reduce-scatter.2.cloned.1.call-update
  203.6 0.0 copy-start.4
  203.6 11.7 %reduce-scatter.2.cloned.1.call-done = f32[4,16,14,512]{3,1,2,0:T(8,128)} async-done(((f32[4,16,14,1024]{3,1,2,0:T(8,128)}), f32[4,16,14,512]{3,1,2,0:T(8,128)}) %reduce-scatter.2.cloned.1.call-update) | async-done | bytes 1835024 | tf_op jit(solution)/shard_map/reduce_scatter | solution.py:102
  215.3 2.6 %convert_element_type.45 = bf16[4,16,14,512]{3,1,2,0:T(8,128)(2,1)} convert(f32[4,16,14,512]{3,1,2,0:T(8,128)} %reduce-scatter.2.cloned.1.call-done) | non-fusion elementwise | flops 458752 | bytes 2752512 | tf_op jit(solution)/shard_map/convert_element_type | solution.py:102
  217.8 4.8 %all-to-all-start.2 = ((bf16[4,16,14,512]{3,1,2,0:T(8,128)(2,1)}), bf16[4,16,14,512]{3,1,2,0:T(8,128)(2,1)S(1)}, u32[]{:S(2)}, u32[]{:S(2)}) async-start(bf16[4,16,14,512]{3,1,2,0:T(8,128)(2,1)} %convert_element_type.45), calls=%async_computation.3 | async-start | bytes 1835008 | tf_op jit(solution)/shard_map/all_to_all | solution.py:105
  222.7 0.1 add.76
  222.7 0.0 copy-done.4
  222.7 0.1 copy.42
  222.8 0.6 constant_dynamic-slice_fusion.1
  223.5 22.6 %all-to-all-done.2 = bf16[4,16,14,512]{3,1,2,0:T(8,128)(2,1)S(1)} async-done(((bf16[4,16,14,512]{3,1,2,0:T(8,128)(2,1)}), bf16[4,16,14,512]{3,1,2,0:T(8,128)(2,1)S(1)}, u32[]{:S(2)}, u32[]{:S(2)}) %all-to-all-start.2) | async-done | bytes 917536 | tf_op jit(solution)/shard_map/all_to_all | solution.py:105
  246.1 0.0 copy-start.1
  246.1 0.5 copy.41
  246.6 0.3 reshape.117
  246.9 0.8 gather_fusion
  247.7 0.8 multiply_reduce_fusion
  248.5 0.0 copy-done.1
  (6 shorter events, 0.1 us)
Async XLA Ops:
  7.2 1.6 copy-start
  7.2 8.6 %copy-start.3 = (s32[16,8]{0,1:T(8,128)S(1)}, s32[16,8]{0,1:T(8,128)}, u32[]{:S(2)}) copy-start(s32[16,8]{0,1:T(8,128)} %param.16) | copy-start | bytes 1540
  7.2 8.8 %copy-start.5 = (s32[64]{0:T(128)S(1)}, s32[64]{0:T(128)}, u32[]{:S(2)}) copy-start(s32[64]{0:T(128)} %param.18) | copy-start | bytes 772
  11.6 8.2 %all-to-all-start = ((bf16[4,4,1024]{2,0,1:T(4,128)(2,1)}), bf16[4,4,1024]{2,0,1:T(4,128)(2,1)S(1)}, u32[]{:S(2)}, u32[]{:S(2)}) async-start(bf16[4,4,1024]{2,0,1:T(4,128)(2,1)} %copy.36), calls=%async_computation | async-start | bytes 65536 | tf_op jit(solution)/shard_map/all_to_all | solution.py:60
  15.8 68.3 %all-gather.2.cloned.1.call-start = ((), (), s32[]{:S(2)}) async-start(), calls=%async_computation.4 | async-start | bytes 3145728 | tf_op jit(solution)/shard_map/all_gather | solution.py:96
  75.2 116.5 %all-reduce.4.cloned.1.call-start = ((), (), s32[]{:S(2)}) async-start(), calls=%async_computation.6 | async-start | bytes 6291456 | tf_op jit(solution)/shard_map/psum | solution.py:99
  84.1 10.5 %copy-start.2 = (bf16[4,16,14,1024]{3,2,0,1:T(8,128)(2,1)S(1)}, bf16[4,16,14,1024]{3,2,0,1:T(8,128)(2,1)}, u32[]{:S(2)}) copy-start(bf16[4,16,14,1024]{3,2,0,1:T(8,128)(2,1)} %all-gather.2.cloned.1.call-done) | copy-start | bytes 5505028
  104.4 110.8 %reduce-scatter.2.cloned.1.call-start = ((), (), s32[]{:S(2)}) async-start(), calls=%async_computation.5 | async-start | bytes 5505024 | tf_op jit(solution)/shard_map/reduce_scatter | solution.py:102
  203.6 19.2 %copy-start.4 = (f32[16,8]{0,1:T(8,128)S(1)}, f32[16,8]{0,1:T(8,128)}, u32[]{:S(2)}) copy-start(f32[16,8]{0,1:T(8,128)} %param.17) | copy-start | bytes 1540
  217.8 28.2 %all-to-all-start.2 = ((bf16[4,16,14,512]{3,1,2,0:T(8,128)(2,1)}), bf16[4,16,14,512]{3,1,2,0:T(8,128)(2,1)S(1)}, u32[]{:S(2)}, u32[]{:S(2)}) async-start(bf16[4,16,14,512]{3,1,2,0:T(8,128)(2,1)} %convert_element_type.45), calls=%async_computation.3 | async-start | bytes 1835008 | tf_op jit(solution)/shard_map/all_to_all | solution.py:105
  246.1 2.4 copy-start.1
Sparse Core Ops, SparseCore 0:
  75.3 8.7 all-gather.1
  104.6 87.1 all-reduce.3
  203.7 11.5 reduce-scatter.1
where the time goes:
time: 256 us; the launch traced here: 255 us
  waiting for transfers between devices  133 us (52%)
  blocking collectives  40 us (16%)
  matrix products  36.2 us (14%)
  local copies, waits for them, and re-layouts  17.3 us (7%)
  between operations  13.9 us (5%)
  starting transfers between devices  9.29 us (4%)
  other arithmetic  4.91 us (2%)
    psum x1, waiting for transfers between devices, body(): gate_value, up_value = lax.psum((gate_part, up_part), 'tp')  87 us
    all_to_all x1, blocking collectives, body(): lax.all_to_all(own_slice, 'pool', split_axis=0, concat_axis=0, tiled=True)  28.3 us
    all_to_all x1, waiting for transfers between devices, body(): lax.all_to_all(expert_rows, 'pool', split_axis=0, concat_axis=0, tiled=True)  22.6 us
    psum x1, blocking collectives, body(): summed = lax.psum(partial_value, ('tp', 'sub'))  11.7 us
    reduce_scatter x1, waiting for transfers between devices, body(): lax.psum_scatter(partial_rows, 'sub', scatter_dimension=3, tiled=True)  11.7 us
    dot_general x1, matrix products, body(): jnp.einsum('pjcd,jfd->pjcf', incoming, w_up, preferred_element_type=jnp.f...  10.5 us
    dot_general x1, matrix products, body(): jnp.einsum('pjcd,jfd->pjcf', incoming, w_gate, preferred_element_type=jnp...  9.77 us
    all_gather x1, waiting for transfers between devices, body(): incoming = lax.all_gather(arrived, 'sub', axis=3, tiled=True)  8.87 us
  transfers between devices with their start and end apart: 5, of which 5 were waited for; matrix products, arithmetic and copies ran while one was open for 1% of the time, Pallas kernels for 0%

commit v1 on v0

v1 whole, which is shorter than its diff:
```python
import functools
import math

import jax
import jax.numpy as jnp
from jax import lax
from jax.experimental import pallas as pl
from jax.experimental.pallas import tpu as pltpu
from jax.sharding import PartitionSpec as P

HEAD_DIM = 128
KV_HEADS = 2
CHUNK = 128
VMEM_LIMIT = 56 << 20

F32 = jnp.float32
BF16 = jnp.bfloat16


def dot_nt(a, b):
    return lax.dot_general(a, b, (((1,), (1,)), ((), ())), preferred_element_type=F32)


def dot_tn(a, b):
    return lax.dot_general(a, b, (((0,), (0,)), ((), ())), preferred_element_type=F32)


def dot_nn(a, b):
    return jnp.dot(a, b, preferred_element_type=F32)


def whole_spec(shape):
    return pl.BlockSpec(shape, lambda *_: (0,) * len(shape))


def attention_kernel(lengths, where, q_ref, k_ref, v_ref, *refs, rows, step_rows, heads, pieces):
    outs, (gathered, flat) = refs[:pieces], refs[pieces:]
    step = pl.program_id(0)
    group = heads // KV_HEADS
    positions = k_ref.shape[1]
    column = lax.broadcasted_iota(jnp.int32, (group, positions), 1)
    for r in range(step_rows):
        row = step * step_rows + r
        valid = column < lengths[row]
        for j in range(KV_HEADS):
            lanes = slice(j * HEAD_DIM, (j + 1) * HEAD_DIM)
            scores = dot_nt(q_ref[r, j * group : (j + 1) * group, :], k_ref[r, :, lanes])
            scores = jnp.where(valid, scores * (1.0 / math.sqrt(HEAD_DIM)), -1e30)
            top = jnp.max(scores, axis=1, keepdims=True)
            terms = jnp.where(valid, jnp.exp(scores - top), 0.0)
            total = jnp.sum(terms, axis=1, keepdims=True)
            value = dot_nn(terms.astype(BF16), v_ref[r, :, lanes]) / total
            gathered[row, j * group : (j + 1) * group, :] = value

    @pl.when(step == pl.num_programs(0) - 1)
    def _():
        for h in range(heads):
            flat[:, h * HEAD_DIM : (h + 1) * HEAD_DIM] = gathered[:, h, :]
        width = heads * HEAD_DIM // pieces
        for k in range(pieces):
            start = pl.multiple_of((where[0] ^ k) * width, width)
            outs[k][...] = flat[:, pl.ds(start, width)].astype(BF16)


def attend(queries, keys_cache, values_cache, lengths, where, pieces):
    rows, columns = queries.shape
    heads = columns // HEAD_DIM
    positions, kv_width = keys_cache.shape[1:]
    step_rows = 2
    width = columns // pieces
    cache = pl.BlockSpec((step_rows, positions, kv_width), lambda i, *_: (i, 0, 0))
    return pl.pallas_call(
        functools.partial(
            attention_kernel, rows=rows, step_rows=step_rows, heads=heads, pieces=pieces
        ),
        grid_spec=pltpu.PrefetchScalarGridSpec(
            num_scalar_prefetch=2,
            grid=(rows // step_rows,),
            in_specs=[
                pl.BlockSpec((step_rows, heads, HEAD_DIM), lambda i, *_: (i, 0, 0)),
                cache,
                cache,
            ],
            out_specs=[whole_spec((rows, width))] * pieces,
            scratch_shapes=[
                pltpu.VMEM((rows, heads, HEAD_DIM), F32),
                pltpu.VMEM((rows, columns), F32),
            ],
        ),
        out_shape=[jax.ShapeDtypeStruct((rows, width), BF16)] * pieces,
        compiler_params=pltpu.CompilerParams(vmem_limit_bytes=VMEM_LIMIT),
        name="attention",
    )(lengths, where, queries.reshape(rows, heads, HEAD_DIM), keys_cache, values_cache)


def project_kernel(where, *refs, sources, pieces):
    inputs, w_ref = refs[:sources], refs[sources]
    outs, (x,) = refs[sources + 1 : sources + 1 + pieces], refs[sources + 1 + pieces :]
    step = pl.program_id(0)

    @pl.when(step == 0)
    def _():
        own_rows = inputs[0].shape[0]
        count = sources * own_rows
        stacked = jnp.concatenate([ref[...].astype(F32) for ref in inputs], axis=0).astype(BF16)
        target = lax.broadcasted_iota(jnp.int32, (count, count), 0)
        origin = lax.broadcasted_iota(jnp.int32, (count, count), 1)
        order = (target ^ (where[1] * own_rows)) == origin
        x[...] = dot_nn(jnp.where(order, 1.0, 0.0).astype(BF16), stacked).astype(BF16)

    value = dot_nn(x[...], w_ref[...])
    for k in range(pieces):

        @pl.when(step == k)
        def _(k=k):
            outs[k][...] = value.astype(outs[k].dtype)


def project(inputs, out_weight, where, pieces):
    sources = len(inputs)
    own_rows, depth = inputs[0].shape
    width = out_weight.shape[1] // pieces
    count = sources * own_rows
    return pl.pallas_call(
        functools.partial(project_kernel, sources=sources, pieces=pieces),
        grid_spec=pltpu.PrefetchScalarGridSpec(
            num_scalar_prefetch=1,
            grid=(pieces,),
            in_specs=[whole_spec((own_rows, depth))] * sources
            + [pl.BlockSpec((depth, width), lambda i, where: (0, where[0] ^ i))],
            out_specs=[whole_spec((count, width))] * pieces,
            scratch_shapes=[pltpu.VMEM((count, depth), BF16)],
        ),
        out_shape=[
            jax.ShapeDtypeStruct((count, width), F32 if k == 0 else BF16) for k in range(pieces)
        ],
        compiler_params=pltpu.CompilerParams(vmem_limit_bytes=VMEM_LIMIT),
        name="project",
    )(where, *inputs, out_weight)


def gate_up_kernel(where, own_ref, other_ref, slot_ref, g_ref, u_ref, out_ref, x, total):
    step = pl.program_id(0)
    half = own_ref.shape[1]
    rows = own_ref.shape[0]
    experts, chunk, depth = g_ref.shape
    capacity = out_ref.shape[0]

    @pl.when(step == 0)
    def _():
        x[:, pl.ds(pl.multiple_of(where[2] * half, half), half)] = own_ref[...]
        x[:, pl.ds(pl.multiple_of((1 - where[2]) * half, half), half)] = other_ref[...]
        total[...] = jnp.zeros_like(total)

    gate = dot_nt(x[...], g_ref[...].reshape(experts * chunk, depth)).astype(BF16)
    up = dot_nt(x[...], u_ref[...].reshape(experts * chunk, depth)).astype(BF16)
    blocks = []
    for e in range(experts):
        lanes = slice(e * chunk, (e + 1) * chunk)
        blocks.append(jnp.concatenate([gate[:, lanes], up[:, lanes]], axis=1))
    both = jnp.concatenate(blocks, axis=0)
    place = lax.broadcasted_iota(jnp.int32, (capacity, experts * rows), 0)
    pick = jnp.where(place == slot_ref[0], 1.0, 0.0).astype(BF16)
    total[...] += dot_nn(pick, both)

    @pl.when(step == pl.num_programs(0) - 1)
    def _():
        out_ref[...] = total[...].astype(BF16)


def gate_up(own, other, slots, w_gate, w_up, where, index, group, capacity):
    rows, half = own.shape
    experts, _, depth = w_gate.shape
    weight = pl.BlockSpec((group, CHUNK, depth), lambda i, *_: (i, index, 0))
    return pl.pallas_call(
        gate_up_kernel,
        grid_spec=pltpu.PrefetchScalarGridSpec(
            num_scalar_prefetch=1,
            grid=(experts // group,),
            in_specs=[
                whole_spec((rows, half)),
                whole_spec((rows, half)),
                pl.BlockSpec((1, 1, group * rows), lambda i, *_: (i, 0, 0)),
                weight,
                weight,
            ],
            out_specs=whole_spec((capacity, 2 * CHUNK)),
            scratch_shapes=[
                pltpu.VMEM((rows, 2 * half), BF16),
                pltpu.VMEM((capacity, 2 * CHUNK), F32),
            ],
        ),
        out_shape=jax.ShapeDtypeStruct((capacity, 2 * CHUNK), BF16),
        compiler_params=pltpu.CompilerParams(vmem_limit_bytes=VMEM_LIMIT),
        name=f"gate_up_{index}",
    )(where, own, other, slots, w_gate, w_up)


def down_kernel(where, own_ref, other_ref, weight_ref, slot_ref, d_ref, *refs, pieces, carried):
    before, refs = refs[:carried], refs[carried:]
    outs, (hidden, total) = refs[:-2], refs[-2:]
    step = pl.program_id(0)
    experts, chunk, depth = d_ref.shape
    capacity = own_ref.shape[0]
    rows = total.shape[0]

    @pl.when(step == 0)
    def _():
        both = own_ref[...].astype(F32) + other_ref[...].astype(F32)
        gate, up = both[:, :chunk], both[:, chunk:]
        value = gate / (1.0 + jnp.exp(-gate)) * up * weight_ref[...]
        hidden[...] = value.astype(BF16)
        if carried:
            total[...] = before[0][...]
        else:
            total[...] = jnp.zeros_like(total)

    place = lax.broadcasted_iota(jnp.int32, (capacity, experts * rows), 0)
    pick = jnp.where(place == slot_ref[0], 1.0, 0.0).astype(BF16)
    spread = dot_tn(pick, hidden[...]).astype(BF16)
    left = jnp.concatenate([spread[e * rows : (e + 1) * rows] for e in range(experts)], axis=1)
    total[...] += dot_nn(left, d_ref[...].reshape(experts * chunk, depth))

    @pl.when(step == pl.num_programs(0) - 1)
    def _():
        if pieces == 1:
            outs[0][...] = total[...]
        else:
            count, width = outs[0].shape
            for k in range(pieces):
                row = pl.multiple_of((where[3] ^ (k >> 1)) * count, count)
                lane = pl.multiple_of((where[2] ^ (k & 1)) * width, width)
                outs[k][...] = total[pl.ds(row, count), pl.ds(lane, width)].astype(outs[k].dtype)


def down(own, other, slot_weight, slots, w_down, before, where, index, group, rows, pieces):
    experts, _, depth = w_down.shape
    capacity = own.shape[0]
    if pieces == 1:
        out_shape = [jax.ShapeDtypeStruct((rows, depth), F32)]
    else:
        shape = (rows * 2 // pieces, depth // 2)
        out_shape = [jax.ShapeDtypeStruct(shape, F32 if k == 0 else BF16) for k in range(pieces)]
    carried = [] if before is None else [before]
    return pl.pallas_call(
        functools.partial(down_kernel, pieces=pieces, carried=len(carried)),
        grid_spec=pltpu.PrefetchScalarGridSpec(
            num_scalar_prefetch=1,
            grid=(experts // group,),
            in_specs=[
                whole_spec((capacity, 2 * CHUNK)),
                whole_spec((capacity, 2 * CHUNK)),
                whole_spec((capacity, 1)),
                pl.BlockSpec((1, 1, group * rows), lambda i, *_: (i, 0, 0)),
                pl.BlockSpec((group, CHUNK, depth), lambda i, *_: (i, index, 0)),
            ]
            + [whole_spec((rows, depth))] * len(carried),
            out_specs=[whole_spec(leaf.shape) for leaf in out_shape],
            scratch_shapes=[
                pltpu.VMEM((capacity, CHUNK), BF16),
                pltpu.VMEM((rows, depth), F32),
            ],
        ),
        out_shape=out_shape,
        compiler_params=pltpu.CompilerParams(vmem_limit_bytes=VMEM_LIMIT),
        name=f"down_{index}",
    )(where, own, other, slot_weight, slots, w_down, *carried)


def xor_permute(value, axes, count, k):
    return lax.ppermute(value, axes, [(i, i ^ k) for i in range(count)])


def body(
    queries,
    keys_cache,
    values_cache,
    lengths,
    out_weight,
    routes,
    route_weight,
    expert_table,
    w_gate,
    w_up,
    w_down,
):
    pools, tps, subs = lax.axis_size("pool"), lax.axis_size("tp"), lax.axis_size("sub")
    pool, tp, sub = lax.axis_index("pool"), lax.axis_index("tp"), lax.axis_index("sub")
    shards = tps * subs
    shard = tp * subs + sub
    direct = tps == 2 and subs == 2 and pools == 4
    own_rows = queries.shape[0]
    pool_rows = own_rows * shards
    rows = pool_rows * pools
    experts, hidden_units, half_width = w_gate.shape
    quarter = half_width // subs
    top = routes.shape[1]
    where = jnp.stack([shard, pool * shards + shard, sub, pool]).astype(jnp.int32)

    facts = jnp.concatenate([routes.astype(F32), route_weight], axis=1)
    if direct:
        blocks = [facts] + [xor_permute(facts, "pool", pools, k) for k in range(1, pools)]
        stacked = jnp.stack(blocks)
        order = lax.iota(jnp.int32, pools) ^ pool
        hot = order[:, None] == lax.iota(jnp.int32, pools)[None, :]
        facts = jnp.sum(jnp.where(hot[:, :, None, None], stacked[None], 0.0), axis=1)
        facts = facts.reshape(rows, 2 * top)
    else:
        facts = lax.all_gather(facts, "pool", axis=0, tiled=True)
    all_routes = facts[:, :top].astype(jnp.int32)
    all_weights = facts[:, top:]
    total_experts = expert_table.shape[0]
    ids = lax.iota(jnp.int32, total_experts)
    entry = jnp.sum(
        jnp.where(all_routes[:, :, None] == ids[None, None, :], expert_table[None, None, :], 0),
        axis=2,
    )
    loads = jnp.sum(
        (entry // experts)[:, :, None] == lax.iota(jnp.int32, pools)[None, None, :],
        axis=(0, 1),
        dtype=jnp.int32,
    )
    largest = jnp.max(loads)
    capacity = -(-rows * top * 13 // (8 * pools * 16)) * 16
    group = max(1, min(experts, 256 // rows))
    groups = experts // group
    local = entry - pool * experts
    expert_of = lax.iota(jnp.int32, experts)
    chosen = local.T[:, None, :] == expert_of[None, :, None]
    mask = jnp.any(chosen, axis=0).reshape(groups, group * rows)
    pair_weight = jnp.sum(jnp.where(chosen, all_weights.T[:, None, :], 0.0), axis=0)
    pair_weight = pair_weight.reshape(1, experts * rows)
    lane = lax.iota(jnp.int32, group * rows)
    before = (lane[:, None] < lane[None, :]).astype(BF16)
    rank = jnp.dot(mask.astype(BF16), before, preferred_element_type=F32).astype(jnp.int32)
    counts = jnp.sum(mask, axis=1, dtype=jnp.int32)
    base = jnp.cumsum(counts) - counts
    slots = jnp.where(mask, rank + base[:, None], -1).reshape(groups, 1, group * rows)

    if direct:
        pieces = attend(queries, keys_cache, values_cache, lengths, where, shards)
        part = pools * shards
        axes = ("pool", "tp", "sub")
        inputs = [
            pieces[k % shards] if k == 0 else xor_permute(pieces[k % shards], axes, part, k)
            for k in range(part)
        ]
        sums = project(inputs, out_weight, where, shards)
        x_sum = sums[0]
        for k in range(1, shards):
            x_sum = x_sum + xor_permute(sums[k], ("tp", "sub"), shards, k).astype(F32)
        own_x = x_sum.astype(BF16)
    else:
        attention = attend(queries, keys_cache, values_cache, lengths, where * 0, 1)[0]
        head_rows = lax.all_to_all(
            attention, ("tp", "sub"), split_axis=1, concat_axis=0, tiled=True
        )
        partial = jnp.dot(head_rows, out_weight, preferred_element_type=F32)
        x_sum = lax.psum_scatter(partial, ("tp", "sub"), scatter_dimension=1, tiled=True)
        own_x = lax.all_gather(x_sum.astype(BF16), "pool", axis=0, tiled=True)
    other_x = xor_permute(own_x, "sub", subs, 1)

    if direct:
        first = jnp.where(sub == 0, own_x, other_x)
        second = jnp.where(sub == 0, other_x, own_x)
        x_half = jnp.concatenate([first, second], axis=1)
        start = pool * pool_rows + (shard ^ subs) * own_rows
        theirs = lax.ppermute(
            lax.dynamic_slice_in_dim(x_half, start, own_rows, 0), "tp", [(0, 1), (1, 0)]
        )
        start = pool * pool_rows + shard * own_rows
        mine = lax.dynamic_slice_in_dim(x_half, start, own_rows, 0)
        attended = jnp.where(
            tp == 0,
            jnp.concatenate([mine, theirs], axis=1),
            jnp.concatenate([theirs, mine], axis=1),
        )
    else:
        pool_x = lax.dynamic_slice_in_dim(own_x, pool * pool_rows, pool_rows, 0)
        attended = lax.all_to_all(pool_x, ("tp", "sub"), split_axis=0, concat_axis=1, tiled=True)

    def weights_of(shifted):
        place = lax.iota(jnp.int32, capacity)[:, None]
        hit = place == shifted.reshape(1, experts * rows)
        return jnp.sum(jnp.where(hit, pair_weight, 0.0), axis=1, keepdims=True)

    def run_experts(shifted, pieces):
        slot_weight = weights_of(shifted)
        chunks = hidden_units // CHUNK
        sent = [
            gate_up(own_x, other_x, shifted, w_gate, w_up, where, c, group, capacity)
            for c in range(chunks)
        ]
        if tps == 2:
            both = [(value, lax.ppermute(value, "tp", [(0, 1), (1, 0)])) for value in sent]
        else:
            both = [
                (lax.psum(value.astype(F32), "tp").astype(BF16), jnp.zeros_like(value))
                for value in sent
            ]
        result = [None]
        for c in range(chunks):
            own, other = both[c]
            last = pieces if c == chunks - 1 else 1
            result = down(
                own,
                other,
                slot_weight,
                shifted,
                w_down,
                result[0],
                where,
                c,
                group,
                rows,
                last,
            )
        return result

    def reduce_rows(values):
        total = values[0]
        for k in range(1, len(values)):
            moved = xor_permute(values[k], ("pool", "sub"), pools * subs, k)
            total = total + moved.astype(F32)
        return total

    def finish(shifted):
        if direct:
            return reduce_rows(run_experts(shifted, pools * subs))
        value = run_experts(shifted, 1)[0]
        value = lax.psum_scatter(value, "pool", scatter_dimension=0, tiled=True)
        return lax.psum_scatter(value, "sub", scatter_dimension=1, tiled=True)

    def more(state):
        k, total = state
        return k + 1, total + finish(slots - k * capacity)

    expert_sum = finish(slots)
    _, extra = lax.while_loop(
        lambda state: state[0] * capacity < largest,
        more,
        (jnp.int32(1), jnp.zeros((pool_rows, quarter), F32)),
    )
    return attended, (expert_sum + extra).astype(BF16)


def solution(mesh):
    in_specs = (
        P(("grp", "pool", "tp", "sub"), None),
        P(("grp", "pool", "tp", "sub"), None, None),
        P(("grp", "pool", "tp", "sub"), None, None),
        P(("grp", "pool", "tp", "sub")),
        P(("tp", "sub"), None),
        P(("grp", "pool"), None),
        P(("grp", "pool"), None),
        P(),
        P("pool", "sub", "tp"),
        P("pool", "sub", "tp"),
        P("pool", "sub", "tp"),
    )
    out_specs = (P(("grp", "pool", "tp", "sub"), None), P(("grp", "pool"), ("tp", "sub")))
    return jax.shard_map(body, mesh=mesh, in_specs=in_specs, out_specs=out_specs, check_vma=False)
```

time: 256 us -> 116 us (0.45)
  waiting for transfers between devices: 133 us -> 11.8 us
  Pallas kernels: 0 us -> 48 us
  blocking collectives: 40 us -> 0 us
  matrix products: 36.2 us -> 0.12 us
  starting transfers between devices: 9.29 us -> 39.8 us
  between operations: 13.9 us -> 1.02 us
  local copies, waits for them, and re-layouts: 17.3 us -> 5.37 us
  other arithmetic: 4.91 us -> 7.96 us
    psum x1 -> x0, waiting for transfers between devices: 87 us -> none  [body(): gate_value, up_value = lax.psum((gate_part, up_part), 'tp')]
    pallas_call x0 -> x8, Pallas kernels: none -> 48 us  [the longest x3 22 us: gate_up(): pl.pallas_call(gate_up_kernel, grid_spec=pltpu.PrefetchScalarGridSpec(num...]
    ppermute x0 -> x33, starting transfers between devices: none -> 39.8 us  [the longest x29 35.7 us: xor_permute(): return lax.ppermute(value, axes, [(i, i ^ k) for i in range(count)])]
    dot_general x7 -> x1, matrix products: 36.2 us -> 0.12 us  [body(): jnp.dot(mask.astype(BF16), before, preferred_element_type=F32)]
    all_to_all x1 -> x0, blocking collectives: 28.3 us -> none  [body(): lax.all_to_all(own_slice, 'pool', split_axis=0, concat_axis=0, tiled=True)]
    all_to_all x2 -> x0, waiting for transfers between devices: 25.7 us -> none  [the longest x1 22.6 us: body(): lax.all_to_all(expert_rows, 'pool', split_axis=0, concat_axis=0, tiled=True)]
    ppermute x0 -> x33, waiting for transfers between devices: none -> 11.8 us  [the longest x29 10.5 us: xor_permute(): return lax.ppermute(value, axes, [(i, i ^ k) for i in range(count)])]
    psum x1 -> x0, blocking collectives: 11.7 us -> none  [body(): summed = lax.psum(partial_value, ('tp', 'sub'))]
  transfers between devices with their start and end apart: 5 -> 33, of which waited for: 5 -> 9; matrix products, arithmetic and copies ran while one was open for 1% -> 7% of each run, Pallas kernels for 0% -> 26%
where the time goes in v1:
time: 116 us; the launch traced here: 115 us
  Pallas kernels  48 us (41%)
  starting transfers between devices  39.8 us (34%)
  waiting for transfers between devices  11.8 us (10%)
  other arithmetic  7.96 us (7%)
  local copies, waits for them, and re-layouts  5.37 us (5%)
    ppermute x29, starting transfers between devices, xor_permute(): return lax.ppermute(value, axes, [(i, i ^ k) for i in range(count)])  35.7 us
    pallas_call x3, Pallas kernels, gate_up(): pl.pallas_call(gate_up_kernel, grid_spec=pltpu.PrefetchScalarGridSpec(num...  22 us
    pallas_call x3, Pallas kernels, down(): pl.pallas_call(functools.partial(down_kernel, pieces=pieces, carried=len(...  16.4 us
    ppermute x29, waiting for transfers between devices, xor_permute(): return lax.ppermute(value, axes, [(i, i ^ k) for i in range(count)])  10.5 us
    pallas_call x1, Pallas kernels, project(): pl.pallas_call(functools.partial(project_kernel, sources=sources, pieces=...  5.02 us
    pallas_call x1, Pallas kernels, attend(): pl.pallas_call(functools.partial(attention_kernel, rows=rows, step_rows=s...  4.71 us
    unnamed x58, local copies, waits for them, and re-layouts  3.99 us
    ppermute x3, starting transfers between devices, run_experts(): lax.ppermute(value, 'tp', [(0, 1), (1, 0)])  3.15 us
  transfers between devices with their start and end apart: 33, of which 9 were waited for; matrix products, arithmetic and copies ran while one was open for 7% of the time, Pallas kernels for 26%

profile of v1, /device:TPU:0, one launch (start us, length us, event | category | flops | bytes accessed | tf_op | source)
XLA Modules:
  0.0 114.8 jit_solution(11767704389917161554)
XLA Ops:
  0.6 0.7 convert_element_type.79
  1.3 0.7 fusion.7
  2.0 5.0 %collective-permute-start.32 = (f32[16,16]{0,1:T(8,128)S(1)}, f32[16,16]{0,1:T(8,128)S(1)}, u32[]{:S(2)}, u32[]{:S(2)}) collective-permute-start(f32[16,16]{0,1:T(8,128)S(1)} %get-tuple-element.132), channel_id=1, source_target_pairs={{0,12},{4,8},{8,4},{12,0},{1,13},{5,9},{9,5},{13,1},{2,14},{6,10},... | collective-permute-start | bytes 3080 | tf_op jit(solution)/shard_map/ppermute | solution.py:271
  7.1 0.6 collective-permute-start.31
  7.6 1.4 %copy.38 = bf16[1,4,32,128]{3,2,1,0:T(8,128)(2,1)} copy(bf16[1,4,32,128]{3,1,2,0:T(4,128)(2,1)} %bitcast.39) | data formatting | bytes 65536
  9.1 4.7 %attention.1 = (bf16[4,1024]{1,0:T(4,128)(2,1)}, bf16[4,1024]{1,0:T(4,128)(2,1)}, bf16[4,1024]{1,0:T(4,128)(2,1)}, bf16[4,1024]{1,0:T(4,128)(2,1)}) custom-call(s32[4]{0:T(128)} %lengths.1, s32[4]{0:T(128)S(1)} %pad_add_fusion.where, bf16[4,32,128]{2,1,0:T(8,128)(2,1)} %bitcast.37, bf16[4,512,256]{2,1,0:T(8,128)(2,1)} %k_ref.1, bf16[4,512,256]{2,1,0:T(8,128)(2,1)} %v_ref.1), custom_call_target="tpu_custom_call" | custom-call | tf_op jit(solution)/shard_map/attention/pallas_call | solution.py:72
  13.9 1.6 %collective-permute-start.14 = (bf16[4,1024]{1,0:T(4,128)(2,1)}, bf16[4,1024]{1,0:T(4,128)(2,1)S(1)}, u32[]{:S(2)}, u32[]{:S(2)}) collective-permute-start(bf16[4,1024]{1,0:T(4,128)(2,1)} %get-tuple-element.85), channel_id=1, source_target_pairs={{0,5},{1,4},{2,7},{3,6},{4,1},{5,0},{6,3},{7,2},{8,13},{9,12},{10,... | collective-permute-start | bytes 24584 | tf_op jit(solution)/shard_map/ppermute | solution.py:271
  15.5 1.5 %collective-permute-start.11 = (bf16[4,1024]{1,0:T(4,128)(2,1)}, bf16[4,1024]{1,0:T(4,128)(2,1)S(1)}, u32[]{:S(2)}, u32[]{:S(2)}) collective-permute-start(bf16[4,1024]{1,0:T(4,128)(2,1)} %get-tuple-element.86), channel_id=1, source_target_pairs={{0,2},{1,3},{2,0},{3,1},{4,6},{5,7},{6,4},{7,5},{8,10},{9,11},{10,... | collective-permute-start | bytes 24584 | tf_op jit(solution)/shard_map/ppermute | solution.py:271
  17.1 0.1 select_reduce_fusion.3
  17.2 1.9 %select_reduce_fusion.2 = s32[64,8]{1,0:T(8,128)S(1)} fusion(s32[64]{0:T(128)} %param.20, s32[64,8]{1,0:T(8,128)S(1)} %get-tuple-element.128), kind=kLoop, calls=%fused_computation.10 | loop fusion | flops 97792 | bytes 4352 | tf_op jit(solution)/shard_map/reduce_sum | solution.py:314
  19.3 0.1 convert_reduce_fusion.1
  19.5 0.1 reduce_sum.74
  19.6 0.2 reduce-window.8
  19.8 0.8 collective-permute-start.13
  20.6 2.1 %collective-permute-start.15 = (bf16[4,1024]{1,0:T(4,128)(2,1)}, bf16[4,1024]{1,0:T(4,128)(2,1)S(1)}, u32[]{:S(2)}, u32[]{:S(2)}) collective-permute-start(bf16[4,1024]{1,0:T(4,128)(2,1)} %get-tuple-element.86), channel_id=1, source_target_pairs={{0,6},{1,7},{2,4},{3,5},{4,2},{5,3},{6,0},{7,1},{8,14},{9,15},{10,... | collective-permute-start | bytes 24584 | tf_op jit(solution)/shard_map/ppermute | solution.py:271
  22.7 0.4 collective-permute-start.16
  23.1 2.8 %collective-permute-start.17 = (bf16[4,1024]{1,0:T(4,128)(2,1)}, bf16[4,1024]{1,0:T(4,128)(2,1)S(1)}, u32[]{:S(2)}, u32[]{:S(2)}) collective-permute-start(bf16[4,1024]{1,0:T(4,128)(2,1)} %get-tuple-element.84.refs_0_), channel_id=1, source_target_pairs={{0,8},{1,9},{2,10},{3,11},{4,12},{5,13},{6,14},{7,15},{8,0},{9,1},... | collective-permute-start | bytes 24584 | tf_op jit(solution)/shard_map/ppermute | solution.py:271
  25.9 0.1 collective-permute-start.18
  26.0 3.4 %collective-permute-start.19 = (bf16[4,1024]{1,0:T(4,128)(2,1)}, bf16[4,1024]{1,0:T(4,128)(2,1)S(1)}, u32[]{:S(2)}, u32[]{:S(2)}) collective-permute-start(bf16[4,1024]{1,0:T(4,128)(2,1)} %get-tuple-element.86), channel_id=1, source_target_pairs={{0,10},{1,11},{2,8},{3,9},{4,14},{5,15},{6,12},{7,13},{8,2},{9,3},... | collective-permute-start | bytes 24584 | tf_op jit(solution)/shard_map/ppermute | solution.py:271
  29.4 0.1 fusion.1
  29.6 0.5 collective-permute-start.20
  30.1 3.2 %collective-permute-start.21 = (bf16[4,1024]{1,0:T(4,128)(2,1)}, bf16[4,1024]{1,0:T(4,128)(2,1)S(1)}, u32[]{:S(2)}, u32[]{:S(2)}) collective-permute-start(bf16[4,1024]{1,0:T(4,128)(2,1)} %get-tuple-element.84.refs_0_), channel_id=1, source_target_pairs={{0,12},{1,13},{2,14},{3,15},{4,8},{5,9},{6,10},{7,11},{8,4},{9,5},... | collective-permute-start | bytes 24584 | tf_op jit(solution)/shard_map/ppermute | solution.py:271
  33.4 0.1 collective-permute-start.22
  33.5 4.2 %collective-permute-start.23 = (bf16[4,1024]{1,0:T(4,128)(2,1)}, bf16[4,1024]{1,0:T(4,128)(2,1)S(1)}, u32[]{:S(2)}, u32[]{:S(2)}) collective-permute-start(bf16[4,1024]{1,0:T(4,128)(2,1)} %get-tuple-element.86), channel_id=1, source_target_pairs={{0,14},{1,15},{2,12},{3,13},{4,10},{5,11},{6,8},{7,9},{8,6},{9,7},... | collective-permute-start | bytes 24584 | tf_op jit(solution)/shard_map/ppermute | solution.py:271
  37.8 0.4 collective-permute-start.24
  38.2 0.2 collective-permute-done.22.refs_13_
  38.5 1.6 %collective-permute-done.23.refs_14_ = bf16[4,1024]{1,0:T(4,128)(2,1)S(1)} collective-permute-done((bf16[4,1024]{1,0:T(4,128)(2,1)}, bf16[4,1024]{1,0:T(4,128)(2,1)S(1)}, u32[]{:S(2)}, u32[]{:S(2)}) %collective-permute-start.23) | collective-permute-done | bytes 8224 | tf_op jit(solution)/shard_map/ppermute | solution.py:271
  40.1 3.7 %collective-permute-done.24.refs_15_ = bf16[4,1024]{1,0:T(4,128)(2,1)S(1)} collective-permute-done((bf16[4,1024]{1,0:T(4,128)(2,1)}, bf16[4,1024]{1,0:T(4,128)(2,1)S(1)}, u32[]{:S(2)}, u32[]{:S(2)}) %collective-permute-start.24) | collective-permute-done | bytes 8224 | tf_op jit(solution)/shard_map/ppermute | solution.py:271
  43.9 0.6 copy-done.24
  44.5 5.0 %project.1 = (f32[64,512]{1,0:T(8,128)}, bf16[64,512]{1,0:T(8,128)(2,1)}, bf16[64,512]{1,0:T(8,128)(2,1)}, bf16[64,512]{1,0:T(8,128)(2,1)}) custom-call(s32[4]{0:T(128)S(1)} %pad_add_fusion.where, bf16[4,1024]{1,0:T(4,128)(2,1)} %get-tuple-element.84.refs_0_, bf16[4,1024]{1,0:T(4,128)(2,1)} %copy-done.10, bf16[4,1024]{1,0:T(4,128)(2,1)} %copy-done.12, ...), custom_call_target="tpu_custom_call" | custom-call | tf_op jit(solution)/shard_map/project/pallas_call | solution.py:124
  49.5 0.3 collective-permute-start.25
  49.8 0.5 collective-permute-start.26
  50.3 1.1 collective-permute-start.27
  51.4 0.2 select_reduce_fusion.1
  51.7 0.8 copy.33.weight_ref
  52.5 2.4 %collective-permute-done.26 = bf16[64,512]{1,0:T(8,128)(2,1)S(1)} collective-permute-done((bf16[64,512]{1,0:T(8,128)(2,1)}, bf16[64,512]{1,0:T(8,128)(2,1)S(1)}, u32[]{:S(2)}, u32[]{:S(2)}) %collective-permute-start.26) | collective-permute-done | bytes 65568 | tf_op jit(solution)/shard_map/ppermute | solution.py:271
  55.0 0.9 add_convert_fusion.own_ref
  55.9 0.6 collective-permute-start.28
  56.5 0.2 convert_reduce_fusion
  56.6 0.7 reduce_max.9
  57.4 7.3 %gate_up_0.2.own_ref = bf16[208,256]{1,0:T(8,128)(2,1)} custom-call(s32[4]{0:T(128)S(1)} %pad_add_fusion.where, bf16[64,512]{1,0:T(8,128)(2,1)S(1)} %add_convert_fusion.own_ref, bf16[64,512]{1,0:T(8,128)(2,1)S(1)} %collective-permute-done.28.other_ref, s32[4,1,256]{2,1,0:T(1,128)S(1)} %reshape.115.slot_ref, bf16[16,384,1024]{2,1,0:T(8,128)(2,1)} %g_ref.5, ...), custom_call_target="tpu_custom_call" | custom-call | tf_op jit(solution)/shard_map/gate_up_0/pallas_call | solution.py:175
  64.7 1.1 collective-permute-start.35
  65.8 7.3 %gate_up_1.2.own_ref = bf16[208,256]{1,0:T(8,128)(2,1)} custom-call(s32[4]{0:T(128)S(1)} %pad_add_fusion.where, bf16[64,512]{1,0:T(8,128)(2,1)S(1)} %add_convert_fusion.own_ref, bf16[64,512]{1,0:T(8,128)(2,1)S(1)} %collective-permute-done.28.other_ref, s32[4,1,256]{2,1,0:T(1,128)S(1)} %reshape.115.slot_ref, bf16[16,384,1024]{2,1,0:T(8,128)(2,1)} %g_ref.5, ...), custom_call_target="tpu_custom_call" | custom-call | tf_op jit(solution)/shard_map/gate_up_1/pallas_call | solution.py:175
  73.2 0.9 collective-permute-start.34
  74.1 7.3 %gate_up_2.2.own_ref = bf16[208,256]{1,0:T(8,128)(2,1)} custom-call(s32[4]{0:T(128)S(1)} %pad_add_fusion.where, bf16[64,512]{1,0:T(8,128)(2,1)S(1)} %add_convert_fusion.own_ref, bf16[64,512]{1,0:T(8,128)(2,1)S(1)} %collective-permute-done.28.other_ref, s32[4,1,256]{2,1,0:T(1,128)S(1)} %reshape.115.slot_ref, bf16[16,384,1024]{2,1,0:T(8,128)(2,1)} %g_ref.5, ...), custom_call_target="tpu_custom_call" | custom-call | tf_op jit(solution)/shard_map/gate_up_2/pallas_call | solution.py:175
  81.4 1.1 collective-permute-start.33
  82.5 0.7 broadcast_select_fusion
  83.2 0.6 copy-done.8
  83.8 5.4 %down_0.2.refs_0_ = f32[64,1024]{1,0:T(8,128)} custom-call(s32[4]{0:T(128)S(1)} %pad_add_fusion.where, bf16[208,256]{1,0:T(8,128)(2,1)} %gate_up_0.2.own_ref, bf16[208,256]{1,0:T(8,128)(2,1)} %copy-done.8, f32[208,1]{1,0:T(8,128)} %copy.33.weight_ref, s32[4,1,256]{2,1,0:T(1,128)S(1)} %reshape.115.slot_ref, bf16[16,384,1024]{2,1,0:T(8,128)(2,1)} %d_ref.5), custom_call_target="tpu_custom_call" | custom-call | tf_op jit(solution)/shard_map/down_0/pallas_call | solution.py:245
  89.2 0.7 copy-done.7
  89.8 5.5 %down_1.2.refs_0_ = f32[64,1024]{1,0:T(8,128)} custom-call(s32[4]{0:T(128)S(1)} %pad_add_fusion.where, bf16[208,256]{1,0:T(8,128)(2,1)} %gate_up_1.2.own_ref, bf16[208,256]{1,0:T(8,128)(2,1)} %copy-done.7, f32[208,1]{1,0:T(8,128)} %copy.33.weight_ref, s32[4,1,256]{2,1,0:T(1,128)S(1)} %reshape.115.slot_ref, bf16[16,384,1024]{2,1,0:T(8,128)(2,1)} %d_ref.5, ...), custom_call_target="tpu_custom_call" | custom-call | tf_op jit(solution)/shard_map/down_1/pallas_call | solution.py:245
  95.3 0.6 copy-done.6
  96.0 5.5 %down_2.2 = (f32[16,512]{1,0:T(8,128)}, bf16[16,512]{1,0:T(8,128)(2,1)}, bf16[16,512]{1,0:T(8,128)(2,1)}, bf16[16,512]{1,0:T(8,128)(2,1)}, bf16[16,512]{1,0:T(8,...) custom-call(s32[4]{0:T(128)S(1)} %pad_add_fusion.where, ...), custom_call_target="tpu_custom_call" | custom-call | tf_op jit(solution)/shard_map/down_2/pallas_call | solution.py:245
  101.6 0.7 while.10
  102.5 1.0 collective-permute-start.29
  103.5 1.5 %collective-permute-start.38 = (bf16[16,512]{1,0:T(8,128)(2,1)S(1)}, bf16[16,512]{1,0:T(8,128)(2,1)S(1)}, u32[]{:S(2)}, u32[]{:S(2)}) collective-permute-start(bf16[16,512]{1,0:T(8,128)(2,1)S(1)} %copy-done.29), channel_id=1, source_target_pairs={{0,5},{1,4},{4,1},{5,0},{8,13},{9,12},{12,9},{13,8},{2,7},{3,6},{6... | collective-permute-start | bytes 49160 | tf_op jit(solution)/shard_map/ppermute | solution.py:271
  104.9 1.3 %collective-permute-done.29 = bf16[4,1024]{1,0:T(4,128)(2,1)S(1)} collective-permute-done((bf16[4,1024]{1,0:T(4,128)(2,1)S(1)}, bf16[4,1024]{1,0:T(4,128)(2,1)S(1)}, u32[]{:S(2)}, u32[]{:S(2)}) %collective-permute-start.29) | collective-permute-done | bytes 8224 | tf_op jit(solution)/shard_map/ppermute | solution.py:368
  106.2 1.6 %collective-permute-start.40 = (bf16[16,512]{1,0:T(8,128)(2,1)S(1)}, bf16[16,512]{1,0:T(8,128)(2,1)S(1)}, u32[]{:S(2)}, u32[]{:S(2)}) collective-permute-start(bf16[16,512]{1,0:T(8,128)(2,1)S(1)} %copy-done.27), channel_id=1, source_target_pairs={{0,9},{1,8},{4,13},{5,12},{8,1},{9,0},{12,5},{13,4},{2,11},{3,10},... | collective-permute-start | bytes 49160 | tf_op jit(solution)/shard_map/ppermute | solution.py:271
  107.8 1.4 %collective-permute-start.41 = (bf16[16,512]{1,0:T(8,128)(2,1)S(1)}, bf16[16,512]{1,0:T(8,128)(2,1)S(1)}, u32[]{:S(2)}, u32[]{:S(2)}) collective-permute-start(bf16[16,512]{1,0:T(8,128)(2,1)S(1)} %copy-done.26), channel_id=1, source_target_pairs={{0,12},{1,13},{4,8},{5,9},{8,4},{9,5},{12,0},{13,1},{2,14},{3,15},... | collective-permute-start | bytes 49160 | tf_op jit(solution)/shard_map/ppermute | solution.py:271
  109.2 2.0 %collective-permute-start.42 = (bf16[16,512]{1,0:T(8,128)(2,1)S(1)}, bf16[16,512]{1,0:T(8,128)(2,1)S(1)}, u32[]{:S(2)}, u32[]{:S(2)}) collective-permute-start(bf16[16,512]{1,0:T(8,128)(2,1)S(1)} %copy-done.25), channel_id=1, source_target_pairs={{0,13},{1,12},{4,9},{5,8},{8,5},{9,4},{12,1},{13,0},{2,15},{3,14},... | collective-permute-start | bytes 49160 | tf_op jit(solution)/shard_map/ppermute | solution.py:271
  111.2 0.6 maximum_select_fusion
  111.8 1.6 %collective-permute-done.41 = bf16[16,512]{1,0:T(8,128)(2,1)S(1)} collective-permute-done((bf16[16,512]{1,0:T(8,128)(2,1)S(1)}, bf16[16,512]{1,0:T(8,128)(2,1)S(1)}, u32[]{:S(2)}, u32[]{:S(2)}) %collective-permute-start.41) | collective-permute-done | bytes 16416 | tf_op jit(solution)/shard_map/ppermute | solution.py:271
  113.4 0.8 collective-permute-done.42
  114.2 0.6 add_convert_fusion.1
  (105 shorter events, 1.4 us)
Async XLA Ops:
  2.0 13.5 %collective-permute-start.32 = (f32[16,16]{0,1:T(8,128)S(1)}, f32[16,16]{0,1:T(8,128)S(1)}, u32[]{:S(2)}, u32[]{:S(2)}) collective-permute-start(f32[16,16]{0,1:T(8,128)S(1)} %get-tuple-element.132), channel_id=1, source_target_pairs={{0,12},{4,8},{8,4},{12,0},{1,13},{5,9},{9,5},{13,1},{2,14},{6,10},... | collective-permute-start | bytes 3080 | tf_op jit(solution)/shard_map/ppermute | solution.py:271
  7.1 9.9 %collective-permute-start.30 = (f32[16,16]{0,1:T(8,128)S(1)}, f32[16,16]{0,1:T(8,128)S(1)}, u32[]{:S(2)}, u32[]{:S(2)}) collective-permute-start(f32[16,16]{0,1:T(8,128)S(1)} %get-tuple-element.132), channel_id=1, source_target_pairs={{0,4},{4,0},{8,12},{12,8},{1,5},{5,1},{9,13},{13,9},{2,6},{6,2},{1... | collective-permute-start | bytes 3080 | tf_op jit(solution)/shard_map/ppermute | solution.py:271
  7.1 9.9 %collective-permute-start.31 = (f32[16,16]{0,1:T(8,128)S(1)}, f32[16,16]{0,1:T(8,128)S(1)}, u32[]{:S(2)}, u32[]{:S(2)}) collective-permute-start(f32[16,16]{0,1:T(8,128)S(1)} %get-tuple-element.132), channel_id=1, source_target_pairs={{0,8},{4,12},{8,0},{12,4},{1,9},{5,13},{9,1},{13,5},{2,10},{6,14},... | collective-permute-start | bytes 3080 | tf_op jit(solution)/shard_map/ppermute | solution.py:271
  13.8 6.9 %collective-permute-start.10 = (bf16[4,1024]{1,0:T(4,128)(2,1)}, bf16[4,1024]{1,0:T(4,128)(2,1)S(1)}, u32[]{:S(2)}, u32[]{:S(2)}) collective-permute-start(bf16[4,1024]{1,0:T(4,128)(2,1)} %get-tuple-element.85), channel_id=1, source_target_pairs={{0,1},{1,0},{2,3},{3,2},{4,5},{5,4},{6,7},{7,6},{8,9},{9,8},{10,11... | collective-permute-start | bytes 24584 | tf_op jit(solution)/shard_map/ppermute | solution.py:271
  13.9 12.1 %collective-permute-start.14 = (bf16[4,1024]{1,0:T(4,128)(2,1)}, bf16[4,1024]{1,0:T(4,128)(2,1)S(1)}, u32[]{:S(2)}, u32[]{:S(2)}) collective-permute-start(bf16[4,1024]{1,0:T(4,128)(2,1)} %get-tuple-element.85), channel_id=1, source_target_pairs={{0,5},{1,4},{2,7},{3,6},{4,1},{5,0},{6,3},{7,2},{8,13},{9,12},{10,... | collective-permute-start | bytes 24584 | tf_op jit(solution)/shard_map/ppermute | solution.py:271
  15.5 7.3 %collective-permute-start.11 = (bf16[4,1024]{1,0:T(4,128)(2,1)}, bf16[4,1024]{1,0:T(4,128)(2,1)S(1)}, u32[]{:S(2)}, u32[]{:S(2)}) collective-permute-start(bf16[4,1024]{1,0:T(4,128)(2,1)} %get-tuple-element.86), channel_id=1, source_target_pairs={{0,2},{1,3},{2,0},{3,1},{4,6},{5,7},{6,4},{7,5},{8,10},{9,11},{10,... | collective-permute-start | bytes 24584 | tf_op jit(solution)/shard_map/ppermute | solution.py:271
  17.0 6.1 %collective-permute-start.12 = (bf16[4,1024]{1,0:T(4,128)(2,1)}, bf16[4,1024]{1,0:T(4,128)(2,1)S(1)}, u32[]{:S(2)}, u32[]{:S(2)}) collective-permute-start(bf16[4,1024]{1,0:T(4,128)(2,1)} %get-tuple-element.87), channel_id=1, source_target_pairs={{0,3},{1,2},{2,1},{3,0},{4,7},{5,6},{6,5},{7,4},{8,11},{9,10},{10,... | collective-permute-start | bytes 24584 | tf_op jit(solution)/shard_map/ppermute | solution.py:271
  19.8 6.1 %collective-permute-start.13 = (bf16[4,1024]{1,0:T(4,128)(2,1)}, bf16[4,1024]{1,0:T(4,128)(2,1)S(1)}, u32[]{:S(2)}, u32[]{:S(2)}) collective-permute-start(bf16[4,1024]{1,0:T(4,128)(2,1)} %get-tuple-element.84.refs_0_), channel_id=1, source_target_pairs={{0,4},{1,5},{2,6},{3,7},{4,0},{5,1},{6,2},{7,3},{8,12},{9,13},{10,... | collective-permute-start | bytes 24584 | tf_op jit(solution)/shard_map/ppermute | solution.py:271
  20.6 23.1 %copy-start.10 = (bf16[4,1024]{1,0:T(4,128)(2,1)}, bf16[4,1024]{1,0:T(4,128)(2,1)S(1)}, u32[]{:S(2)}) copy-start(bf16[4,1024]{1,0:T(4,128)(2,1)S(1)} %collective-permute-done.10.refs_1_) | copy-start | bytes 24580
  20.6 9.0 %collective-permute-start.15 = (bf16[4,1024]{1,0:T(4,128)(2,1)}, bf16[4,1024]{1,0:T(4,128)(2,1)S(1)}, u32[]{:S(2)}, u32[]{:S(2)}) collective-permute-start(bf16[4,1024]{1,0:T(4,128)(2,1)} %get-tuple-element.86), channel_id=1, source_target_pairs={{0,6},{1,7},{2,4},{3,5},{4,2},{5,3},{6,0},{7,1},{8,14},{9,15},{10,... | collective-permute-start | bytes 24584 | tf_op jit(solution)/shard_map/ppermute | solution.py:271
  22.7 21.0 %copy-start.12 = (bf16[4,1024]{1,0:T(4,128)(2,1)}, bf16[4,1024]{1,0:T(4,128)(2,1)S(1)}, u32[]{:S(2)}) copy-start(bf16[4,1024]{1,0:T(4,128)(2,1)S(1)} %collective-permute-done.11.refs_2_) | copy-start | bytes 24580
  22.7 7.4 %collective-permute-start.16 = (bf16[4,1024]{1,0:T(4,128)(2,1)}, bf16[4,1024]{1,0:T(4,128)(2,1)S(1)}, u32[]{:S(2)}, u32[]{:S(2)}) collective-permute-start(bf16[4,1024]{1,0:T(4,128)(2,1)} %get-tuple-element.87), channel_id=1, source_target_pairs={{0,7},{1,6},{2,5},{3,4},{4,3},{5,2},{6,1},{7,0},{8,15},{9,14},{10,... | collective-permute-start | bytes 24584 | tf_op jit(solution)/shard_map/ppermute | solution.py:271
  23.1 20.7 %copy-start.13 = (bf16[4,1024]{1,0:T(4,128)(2,1)}, bf16[4,1024]{1,0:T(4,128)(2,1)S(1)}, u32[]{:S(2)}) copy-start(bf16[4,1024]{1,0:T(4,128)(2,1)S(1)} %collective-permute-done.12.refs_3_) | copy-start | bytes 24580
  23.1 10.3 %collective-permute-start.17 = (bf16[4,1024]{1,0:T(4,128)(2,1)}, bf16[4,1024]{1,0:T(4,128)(2,1)S(1)}, u32[]{:S(2)}, u32[]{:S(2)}) collective-permute-start(bf16[4,1024]{1,0:T(4,128)(2,1)} %get-tuple-element.84.refs_0_), channel_id=1, source_target_pairs={{0,8},{1,9},{2,10},{3,11},{4,12},{5,13},{6,14},{7,15},{8,0},{9,1},... | collective-permute-start | bytes 24584 | tf_op jit(solution)/shard_map/ppermute | solution.py:271
  25.9 17.9 %copy-start.14 = (bf16[4,1024]{1,0:T(4,128)(2,1)}, bf16[4,1024]{1,0:T(4,128)(2,1)S(1)}, u32[]{:S(2)}) copy-start(bf16[4,1024]{1,0:T(4,128)(2,1)S(1)} %collective-permute-done.13.refs_4_) | copy-start | bytes 24580
  25.9 7.6 %collective-permute-start.18 = (bf16[4,1024]{1,0:T(4,128)(2,1)}, bf16[4,1024]{1,0:T(4,128)(2,1)S(1)}, u32[]{:S(2)}, u32[]{:S(2)}) collective-permute-start(bf16[4,1024]{1,0:T(4,128)(2,1)} %get-tuple-element.85), channel_id=1, source_target_pairs={{0,9},{1,8},{2,11},{3,10},{4,13},{5,12},{6,15},{7,14},{8,1},{9,0},... | collective-permute-start | bytes 24584 | tf_op jit(solution)/shard_map/ppermute | solution.py:271
  26.0 17.8 %copy-start.11 = (bf16[4,1024]{1,0:T(4,128)(2,1)}, bf16[4,1024]{1,0:T(4,128)(2,1)S(1)}, u32[]{:S(2)}) copy-start(bf16[4,1024]{1,0:T(4,128)(2,1)S(1)} %collective-permute-done.14.refs_5_) | copy-start | bytes 24580
  26.0 11.8 %collective-permute-start.19 = (bf16[4,1024]{1,0:T(4,128)(2,1)}, bf16[4,1024]{1,0:T(4,128)(2,1)S(1)}, u32[]{:S(2)}, u32[]{:S(2)}) collective-permute-start(bf16[4,1024]{1,0:T(4,128)(2,1)} %get-tuple-element.86), channel_id=1, source_target_pairs={{0,10},{1,11},{2,8},{3,9},{4,14},{5,15},{6,12},{7,13},{8,2},{9,3},... | collective-permute-start | bytes 24584 | tf_op jit(solution)/shard_map/ppermute | solution.py:271
  29.6 14.2 %copy-start.15 = (bf16[4,1024]{1,0:T(4,128)(2,1)}, bf16[4,1024]{1,0:T(4,128)(2,1)S(1)}, u32[]{:S(2)}) copy-start(bf16[4,1024]{1,0:T(4,128)(2,1)S(1)} %collective-permute-done.15.refs_6_) | copy-start | bytes 24580
  29.6 8.6 %collective-permute-start.20 = (bf16[4,1024]{1,0:T(4,128)(2,1)}, bf16[4,1024]{1,0:T(4,128)(2,1)S(1)}, u32[]{:S(2)}, u32[]{:S(2)}) collective-permute-start(bf16[4,1024]{1,0:T(4,128)(2,1)} %get-tuple-element.87), channel_id=1, source_target_pairs={{0,11},{1,10},{2,9},{3,8},{4,15},{5,14},{6,13},{7,12},{8,3},{9,2},... | collective-permute-start | bytes 24584 | tf_op jit(solution)/shard_map/ppermute | solution.py:271
  30.1 13.7 %copy-start.16 = (bf16[4,1024]{1,0:T(4,128)(2,1)}, bf16[4,1024]{1,0:T(4,128)(2,1)S(1)}, u32[]{:S(2)}) copy-start(bf16[4,1024]{1,0:T(4,128)(2,1)S(1)} %collective-permute-done.16.refs_7_) | copy-start | bytes 24580
  30.1 8.1 %collective-permute-start.21 = (bf16[4,1024]{1,0:T(4,128)(2,1)}, bf16[4,1024]{1,0:T(4,128)(2,1)S(1)}, u32[]{:S(2)}, u32[]{:S(2)}) collective-permute-start(bf16[4,1024]{1,0:T(4,128)(2,1)} %get-tuple-element.84.refs_0_), channel_id=1, source_target_pairs={{0,12},{1,13},{2,14},{3,15},{4,8},{5,9},{6,10},{7,11},{8,4},{9,5},... | collective-permute-start | bytes 24584 | tf_op jit(solution)/shard_map/ppermute | solution.py:271
  33.4 10.4 %copy-start.17 = (bf16[4,1024]{1,0:T(4,128)(2,1)}, bf16[4,1024]{1,0:T(4,128)(2,1)S(1)}, u32[]{:S(2)}) copy-start(bf16[4,1024]{1,0:T(4,128)(2,1)S(1)} %collective-permute-done.17.refs_8_) | copy-start | bytes 24580
  33.4 5.1 %collective-permute-start.22 = (bf16[4,1024]{1,0:T(4,128)(2,1)}, bf16[4,1024]{1,0:T(4,128)(2,1)S(1)}, u32[]{:S(2)}, u32[]{:S(2)}) collective-permute-start(bf16[4,1024]{1,0:T(4,128)(2,1)} %get-tuple-element.85), channel_id=1, source_target_pairs={{0,13},{1,12},{2,15},{3,14},{4,9},{5,8},{6,11},{7,10},{8,5},{9,4},... | collective-permute-start | bytes 24584 | tf_op jit(solution)/shard_map/ppermute | solution.py:271
  33.5 10.3 %copy-start.18 = (bf16[4,1024]{1,0:T(4,128)(2,1)}, bf16[4,1024]{1,0:T(4,128)(2,1)S(1)}, u32[]{:S(2)}) copy-start(bf16[4,1024]{1,0:T(4,128)(2,1)S(1)} %collective-permute-done.18.refs_9_) | copy-start | bytes 24580
  33.5 6.6 %collective-permute-start.23 = (bf16[4,1024]{1,0:T(4,128)(2,1)}, bf16[4,1024]{1,0:T(4,128)(2,1)S(1)}, u32[]{:S(2)}, u32[]{:S(2)}) collective-permute-start(bf16[4,1024]{1,0:T(4,128)(2,1)} %get-tuple-element.86), channel_id=1, source_target_pairs={{0,14},{1,15},{2,12},{3,13},{4,10},{5,11},{6,8},{7,9},{8,6},{9,7},... | collective-permute-start | bytes 24584 | tf_op jit(solution)/shard_map/ppermute | solution.py:271
  37.8 6.1 %copy-start.19 = (bf16[4,1024]{1,0:T(4,128)(2,1)}, bf16[4,1024]{1,0:T(4,128)(2,1)S(1)}, u32[]{:S(2)}) copy-start(bf16[4,1024]{1,0:T(4,128)(2,1)S(1)} %collective-permute-done.19.refs_10_) | copy-start | bytes 24580
  37.8 6.0 %collective-permute-start.24 = (bf16[4,1024]{1,0:T(4,128)(2,1)}, bf16[4,1024]{1,0:T(4,128)(2,1)S(1)}, u32[]{:S(2)}, u32[]{:S(2)}) collective-permute-start(bf16[4,1024]{1,0:T(4,128)(2,1)} %get-tuple-element.87), channel_id=1, source_target_pairs={{0,15},{1,14},{2,13},{3,12},{4,11},{5,10},{6,9},{7,8},{8,7},{9,6},... | collective-permute-start | bytes 24584 | tf_op jit(solution)/shard_map/ppermute | solution.py:271
  38.2 5.6 %copy-start.20 = (bf16[4,1024]{1,0:T(4,128)(2,1)}, bf16[4,1024]{1,0:T(4,128)(2,1)S(1)}, u32[]{:S(2)}) copy-start(bf16[4,1024]{1,0:T(4,128)(2,1)S(1)} %collective-permute-done.20.refs_11_) | copy-start | bytes 24580
  38.2 5.6 %copy-start.21 = (bf16[4,1024]{1,0:T(4,128)(2,1)}, bf16[4,1024]{1,0:T(4,128)(2,1)S(1)}, u32[]{:S(2)}) copy-start(bf16[4,1024]{1,0:T(4,128)(2,1)S(1)} %collective-permute-done.21.refs_12_) | copy-start | bytes 24580
  38.5 5.4 %copy-start.22 = (bf16[4,1024]{1,0:T(4,128)(2,1)}, bf16[4,1024]{1,0:T(4,128)(2,1)S(1)}, u32[]{:S(2)}) copy-start(bf16[4,1024]{1,0:T(4,128)(2,1)S(1)} %collective-permute-done.22.refs_13_) | copy-start | bytes 24580
  40.1 3.8 %copy-start.23 = (bf16[4,1024]{1,0:T(4,128)(2,1)}, bf16[4,1024]{1,0:T(4,128)(2,1)S(1)}, u32[]{:S(2)}) copy-start(bf16[4,1024]{1,0:T(4,128)(2,1)S(1)} %collective-permute-done.23.refs_14_) | copy-start | bytes 24580
  43.9 0.6 copy-start.24
  49.5 3.0 %collective-permute-start.25 = (bf16[64,512]{1,0:T(8,128)(2,1)}, bf16[64,512]{1,0:T(8,128)(2,1)S(1)}, u32[]{:S(2)}, u32[]{:S(2)}) collective-permute-start(bf16[64,512]{1,0:T(8,128)(2,1)} %get-tuple-element.89), channel_id=1, source_target_pairs={{0,1},{1,0},{2,3},{3,2},{4,5},{5,4},{6,7},{7,6},{8,9},{9,8},{10,11... | collective-permute-start | bytes 196616 | tf_op jit(solution)/shard_map/ppermute | solution.py:271
  49.8 5.1 %collective-permute-start.26 = (bf16[64,512]{1,0:T(8,128)(2,1)}, bf16[64,512]{1,0:T(8,128)(2,1)S(1)}, u32[]{:S(2)}, u32[]{:S(2)}) collective-permute-start(bf16[64,512]{1,0:T(8,128)(2,1)} %get-tuple-element.90), channel_id=1, source_target_pairs={{0,2},{1,3},{2,0},{3,1},{4,6},{5,7},{6,4},{7,5},{8,10},{9,11},{10,... | collective-permute-start | bytes 196616 | tf_op jit(solution)/shard_map/ppermute | solution.py:271
  50.3 4.7 %collective-permute-start.27 = (bf16[64,512]{1,0:T(8,128)(2,1)}, bf16[64,512]{1,0:T(8,128)(2,1)S(1)}, u32[]{:S(2)}, u32[]{:S(2)}) collective-permute-start(bf16[64,512]{1,0:T(8,128)(2,1)} %get-tuple-element.91), channel_id=1, source_target_pairs={{0,3},{1,2},{2,1},{3,0},{4,7},{5,6},{6,5},{7,4},{8,11},{9,10},{10,... | collective-permute-start | bytes 196616 | tf_op jit(solution)/shard_map/ppermute | solution.py:271
  55.9 1.5 %collective-permute-start.28 = (bf16[64,512]{1,0:T(8,128)(2,1)S(1)}, bf16[64,512]{1,0:T(8,128)(2,1)S(1)}, u32[]{:S(2)}, u32[]{:S(2)}) collective-permute-start(bf16[64,512]{1,0:T(8,128)(2,1)S(1)} %add_convert_fusion.own_ref), channel_id=1, source_target_pairs={{0,1},{1,0},{2,3},{3,2},{4,5},{5,4},{6,7},{7,6},{8,9},{9,8},{10,11... | collective-permute-start | bytes 196616 | tf_op jit(solution)/shard_map/ppermute | solution.py:271
  64.7 18.5 %collective-permute-start.35 = (bf16[208,256]{1,0:T(8,128)(2,1)}, bf16[208,256]{1,0:T(8,128)(2,1)S(1)}, u32[]{:S(2)}, u32[]{:S(2)}) collective-permute-start(bf16[208,256]{1,0:T(8,128)(2,1)} %gate_up_0.2.own_ref), channel_id=1, source_target_pairs={{0,2},{2,0},{1,3},{3,1},{4,6},{6,4},{5,7},{7,5},{8,10},{10,8},{9,1... | collective-permute-start | bytes 319496 | tf_op jit(solution)/shard_map/ppermute | solution.py:395
  73.2 16.0 %collective-permute-start.34 = (bf16[208,256]{1,0:T(8,128)(2,1)}, bf16[208,256]{1,0:T(8,128)(2,1)S(1)}, u32[]{:S(2)}, u32[]{:S(2)}) collective-permute-start(bf16[208,256]{1,0:T(8,128)(2,1)} %gate_up_1.2.own_ref), channel_id=1, source_target_pairs={{0,2},{2,0},{1,3},{3,1},{4,6},{6,4},{5,7},{7,5},{8,10},{10,8},{9,1... | collective-permute-start | bytes 319496 | tf_op jit(solution)/shard_map/ppermute | solution.py:395
  81.4 14.0 %collective-permute-start.33 = (bf16[208,256]{1,0:T(8,128)(2,1)}, bf16[208,256]{1,0:T(8,128)(2,1)S(1)}, u32[]{:S(2)}, u32[]{:S(2)}) collective-permute-start(bf16[208,256]{1,0:T(8,128)(2,1)} %gate_up_2.2.own_ref), channel_id=1, source_target_pairs={{0,2},{2,0},{1,3},{3,1},{4,6},{6,4},{5,7},{7,5},{8,10},{10,8},{9,1... | collective-permute-start | bytes 319496 | tf_op jit(solution)/shard_map/ppermute | solution.py:395
  83.2 0.6 copy-start.8
  89.2 0.7 copy-start.7
  95.3 0.6 copy-start.6
  101.5 0.8 copy-start.31
  101.5 0.9 copy-start.30
  101.5 1.0 copy-start.4
  101.5 1.0 copy-start.5
  101.5 2.0 %copy-start.29 = (bf16[16,512]{1,0:T(8,128)(2,1)S(1)}, bf16[16,512]{1,0:T(8,128)(2,1)}, u32[]{:S(2)}) copy-start(bf16[16,512]{1,0:T(8,128)(2,1)} %get-tuple-element.95) | copy-start | bytes 49156
  101.5 3.4 %copy-start.28 = (bf16[16,512]{1,0:T(8,128)(2,1)S(1)}, bf16[16,512]{1,0:T(8,128)(2,1)}, u32[]{:S(2)}) copy-start(bf16[16,512]{1,0:T(8,128)(2,1)} %get-tuple-element.96) | copy-start | bytes 49156
  101.5 4.7 %copy-start.27 = (bf16[16,512]{1,0:T(8,128)(2,1)S(1)}, bf16[16,512]{1,0:T(8,128)(2,1)}, u32[]{:S(2)}) copy-start(bf16[16,512]{1,0:T(8,128)(2,1)} %get-tuple-element.97) | copy-start | bytes 49156
  101.5 6.3 %copy-start.26 = (bf16[16,512]{1,0:T(8,128)(2,1)S(1)}, bf16[16,512]{1,0:T(8,128)(2,1)}, u32[]{:S(2)}) copy-start(bf16[16,512]{1,0:T(8,128)(2,1)} %get-tuple-element.98) | copy-start | bytes 49156
  101.5 7.7 %copy-start.25 = (bf16[16,512]{1,0:T(8,128)(2,1)S(1)}, bf16[16,512]{1,0:T(8,128)(2,1)}, u32[]{:S(2)}) copy-start(bf16[16,512]{1,0:T(8,128)(2,1)} %get-tuple-element.99) | copy-start | bytes 49156
  101.6 12.6 %copy-start.9 = (f32[16,512]{1,0:T(8,128)S(1)}, f32[16,512]{1,0:T(8,128)}, u32[]{:S(2)}) copy-start(f32[16,512]{1,0:T(8,128)} %get-tuple-element.92) | copy-start | bytes 98308
  102.3 5.6 %collective-permute-start.36 = (bf16[16,512]{1,0:T(8,128)(2,1)S(1)}, bf16[16,512]{1,0:T(8,128)(2,1)S(1)}, u32[]{:S(2)}, u32[]{:S(2)}) collective-permute-start(bf16[16,512]{1,0:T(8,128)(2,1)S(1)} %copy-done.31), channel_id=1, source_target_pairs={{0,1},{1,0},{4,5},{5,4},{8,9},{9,8},{12,13},{13,12},{2,3},{3,2},{6... | collective-permute-start | bytes 49160 | tf_op jit(solution)/shard_map/ppermute | solution.py:271
  102.4 6.8 %collective-permute-start.37 = (bf16[16,512]{1,0:T(8,128)(2,1)S(1)}, bf16[16,512]{1,0:T(8,128)(2,1)S(1)}, u32[]{:S(2)}, u32[]{:S(2)}) collective-permute-start(bf16[16,512]{1,0:T(8,128)(2,1)S(1)} %copy-done.30), channel_id=1, source_target_pairs={{0,4},{1,5},{4,0},{5,1},{8,12},{9,13},{12,8},{13,9},{2,6},{3,7},{6... | collective-permute-start | bytes 49160 | tf_op jit(solution)/shard_map/ppermute | solution.py:271
  102.5 3.7 %collective-permute-start.29 = (bf16[4,1024]{1,0:T(4,128)(2,1)S(1)}, bf16[4,1024]{1,0:T(4,128)(2,1)S(1)}, u32[]{:S(2)}, u32[]{:S(2)}) collective-permute-start(bf16[4,1024]{1,0:T(4,128)(2,1)S(1)} %get-tuple-element.124), channel_id=1, source_target_pairs={{0,2},{2,0},{1,3},{3,1},{4,6},{6,4},{5,7},{7,5},{8,10},{10,8},{9,1... | collective-permute-start | bytes 24584 | tf_op jit(solution)/shard_map/ppermute | solution.py:368
  103.5 8.3 %collective-permute-start.38 = (bf16[16,512]{1,0:T(8,128)(2,1)S(1)}, bf16[16,512]{1,0:T(8,128)(2,1)S(1)}, u32[]{:S(2)}, u32[]{:S(2)}) collective-permute-start(bf16[16,512]{1,0:T(8,128)(2,1)S(1)} %copy-done.29), channel_id=1, source_target_pairs={{0,5},{1,4},{4,1},{5,0},{8,13},{9,12},{12,9},{13,8},{2,7},{3,6},{6... | collective-permute-start | bytes 49160 | tf_op jit(solution)/shard_map/ppermute | solution.py:271
  104.9 6.8 %collective-permute-start.39 = (bf16[16,512]{1,0:T(8,128)(2,1)S(1)}, bf16[16,512]{1,0:T(8,128)(2,1)S(1)}, u32[]{:S(2)}, u32[]{:S(2)}) collective-permute-start(bf16[16,512]{1,0:T(8,128)(2,1)S(1)} %copy-done.28), channel_id=1, source_target_pairs={{0,8},{1,9},{4,12},{5,13},{8,0},{9,1},{12,4},{13,5},{2,10},{3,11},... | collective-permute-start | bytes 49160 | tf_op jit(solution)/shard_map/ppermute | solution.py:271
  106.2 5.6 %collective-permute-start.40 = (bf16[16,512]{1,0:T(8,128)(2,1)S(1)}, bf16[16,512]{1,0:T(8,128)(2,1)S(1)}, u32[]{:S(2)}, u32[]{:S(2)}) collective-permute-start(bf16[16,512]{1,0:T(8,128)(2,1)S(1)} %copy-done.27), channel_id=1, source_target_pairs={{0,9},{1,8},{4,13},{5,12},{8,1},{9,0},{12,5},{13,4},{2,11},{3,10},... | collective-permute-start | bytes 49160 | tf_op jit(solution)/shard_map/ppermute | solution.py:271
  107.8 5.5 %collective-permute-start.41 = (bf16[16,512]{1,0:T(8,128)(2,1)S(1)}, bf16[16,512]{1,0:T(8,128)(2,1)S(1)}, u32[]{:S(2)}, u32[]{:S(2)}) collective-permute-start(bf16[16,512]{1,0:T(8,128)(2,1)S(1)} %copy-done.26), channel_id=1, source_target_pairs={{0,12},{1,13},{4,8},{5,9},{8,4},{9,5},{12,0},{13,1},{2,14},{3,15},... | collective-permute-start | bytes 49160 | tf_op jit(solution)/shard_map/ppermute | solution.py:271
  109.2 5.0 %collective-permute-start.42 = (bf16[16,512]{1,0:T(8,128)(2,1)S(1)}, bf16[16,512]{1,0:T(8,128)(2,1)S(1)}, u32[]{:S(2)}, u32[]{:S(2)}) collective-permute-start(bf16[16,512]{1,0:T(8,128)(2,1)S(1)} %copy-done.25), channel_id=1, source_target_pairs={{0,13},{1,12},{4,9},{5,8},{8,5},{9,4},{12,1},{13,0},{2,15},{3,14},... | collective-permute-start | bytes 49160 | tf_op jit(solution)/shard_map/ppermute | solution.py:271

commit v2 on v0

v2 whole, which is shorter than its diff:
```python
import functools
import math

import jax
import jax.numpy as jnp
from jax import lax
from jax.experimental import pallas as pl
from jax.experimental.pallas import tpu as pltpu
from jax.sharding import PartitionSpec as P

HEAD_DIM = 128
KV_HEADS = 2
CHUNK = 128
VMEM_LIMIT = 16 << 20

F32 = jnp.float32
BF16 = jnp.bfloat16


def dot_nt(a, b):
    return lax.dot_general(a, b, (((1,), (1,)), ((), ())), preferred_element_type=F32)


def dot_tn(a, b):
    return lax.dot_general(a, b, (((0,), (0,)), ((), ())), preferred_element_type=F32)


def dot_nn(a, b):
    return jnp.dot(a, b, preferred_element_type=F32)


def cost(microseconds):
    return pl.CostEstimate(
        flops=0, transcendentals=0, bytes_accessed=int(microseconds * 3_000_000)
    )


VMEM = pl.BlockSpec(memory_space=pltpu.VMEM)
SMEM = pl.BlockSpec(memory_space=pltpu.SMEM)
HBM = pl.BlockSpec(memory_space=pltpu.HBM)
ANY = pl.BlockSpec(memory_space=pl.ANY)


def in_hbm(value):
    return pltpu.with_memory_space_constraint(value, pltpu.HBM)


def call(kernel, name, inputs, specs, outs, out_specs=None, scratch=(), loads=(), anchors=(), us=2):
    count_in, count_out, count_load = len(inputs), len(outs), len(loads)

    def source(ref, first):
        return ref if first is None else ref.at[:, first : first + CHUNK, :]

    def run(*refs):
        refs = list(refs)
        given = [refs.pop(0) for _ in range(count_in)]
        sources = [refs.pop(0) for _ in range(count_load)]
        del refs[: len(anchors)]
        results = [refs.pop(0) for _ in range(count_out)]
        targets = [refs.pop(0) for _ in range(count_load)]
        copies = []
        if loads:
            sems = refs.pop()
            for i, (_, first) in enumerate(loads):
                copies.append(
                    pltpu.make_async_copy(source(sources[i], first), targets[i], sems.at[i])
                )
                copies[-1].start()
        kernel(*given, *results, *refs)
        for copy in copies:
            copy.wait()

    def loaded(array, first):
        shape = array.shape if first is None else (array.shape[0], CHUNK, array.shape[2])
        return pltpu.VMEM(shape, array.dtype)

    scratch = list(scratch) + ([pltpu.SemaphoreType.DMA((count_load,))] if loads else [])
    results = pl.pallas_call(
        run,
        in_specs=list(specs) + [HBM] * count_load + [ANY] * len(anchors),
        out_specs=list(out_specs or [VMEM] * count_out) + [VMEM] * count_load,
        out_shape=list(outs) + [loaded(*leaf) for leaf in loads],
        scratch_shapes=scratch,
        compiler_params=pltpu.CompilerParams(vmem_limit_bytes=VMEM_LIMIT),
        cost_estimate=cost(us),
        name=name,
    )(*inputs, *[in_hbm(leaf[0]) for leaf in loads], *anchors)
    return list(results[:count_out]), list(results[count_out:])


def attention_kernel(lengths, where, q_ref, k_hbm, v_hbm, *refs, pieces):
    outs, (k_ref, v_ref, sems, gathered, flat) = refs[:pieces], refs[pieces:]
    rows, heads, _ = q_ref.shape
    positions = k_ref.shape[1]
    group = heads // KV_HEADS
    copies = []
    for row in range(rows):
        pair = [
            pltpu.make_async_copy(k_hbm.at[row], k_ref.at[row], sems.at[row, 0]),
            pltpu.make_async_copy(v_hbm.at[row], v_ref.at[row], sems.at[row, 1]),
        ]
        pair[0].start()
        pair[1].start()
        copies.append(pair)
    column = lax.broadcasted_iota(jnp.int32, (group, positions), 1)
    for row in range(rows):
        valid = column < lengths[row]
        copies[row][0].wait()
        copies[row][1].wait()
        for j in range(KV_HEADS):
            lanes = slice(j * HEAD_DIM, (j + 1) * HEAD_DIM)
            scores = dot_nt(q_ref[row, j * group : (j + 1) * group, :], k_ref[row, :, lanes])
            scores = jnp.where(valid, scores * (1.0 / math.sqrt(HEAD_DIM)), -1e30)
            top = jnp.max(scores, axis=1, keepdims=True)
            terms = jnp.where(valid, jnp.exp(scores - top), 0.0)
            total = jnp.sum(terms, axis=1, keepdims=True)
            value = dot_nn(terms.astype(BF16), v_ref[row, :, lanes]) / total
            gathered[row, j * group : (j + 1) * group, :] = value
    for h in range(heads):
        flat[:, h * HEAD_DIM : (h + 1) * HEAD_DIM] = gathered[:, h, :]
    width = heads * HEAD_DIM // pieces
    for k in range(pieces):
        start = pl.multiple_of((where[0] ^ k) * width, width)
        outs[k][...] = flat[:, pl.ds(start, width)].astype(BF16)


def attend(queries, keys_cache, values_cache, lengths, where, pieces, loads):
    rows, columns = queries.shape
    heads = columns // HEAD_DIM
    return call(
        functools.partial(attention_kernel, pieces=pieces),
        "attention",
        [lengths, where, queries.reshape(rows, heads, HEAD_DIM), in_hbm(keys_cache), in_hbm(values_cache)],
        [SMEM, SMEM, VMEM, HBM, HBM],
        [jax.ShapeDtypeStruct((rows, columns // pieces), BF16)] * pieces,
        scratch=[
            pltpu.VMEM(keys_cache.shape, BF16),
            pltpu.VMEM(values_cache.shape, BF16),
            pltpu.SemaphoreType.DMA((rows, 2)),
            pltpu.VMEM((rows, heads, HEAD_DIM), F32),
            pltpu.VMEM((rows, columns), F32),
        ],
        loads=loads,
        us=4,
    )


def route_kernel(where, table_ref, facts_ref, slot_ref, weight_ref, largest_ref, *, experts, swapped):
    pools, double, pool_rows = facts_ref.shape
    top = double // 2
    rows = pools * pool_rows
    total = table_ref.shape[1]
    groups, _, lanes = slot_ref.shape
    group = lanes // rows
    own = where[3] if swapped else 0
    facts = jnp.concatenate([facts_ref[own ^ p] for p in range(pools)], axis=1)
    routes = jnp.concatenate([facts[i : i + 1] for i in range(top)], axis=1).astype(jnp.int32)
    ids = lax.broadcasted_iota(jnp.int32, (total, top * rows), 0)
    hot = jnp.where(ids == routes, 1.0, 0.0).astype(BF16)
    table = jnp.broadcast_to(table_ref[...].astype(F32), (8, total)).astype(BF16)
    entry = dot_nn(table, hot)[0:1].astype(jnp.int32)

    largest = jnp.int32(0)
    for p in range(pools):
        inside = (entry >= p * experts) & (entry < (p + 1) * experts)
        largest = jnp.maximum(largest, jnp.sum(jnp.where(inside, 1.0, 0.0)).astype(jnp.int32))
    largest_ref[0] = largest

    lane = lax.broadcasted_iota(jnp.int32, (groups, lanes), 1)
    block = lax.broadcasted_iota(jnp.int32, (groups, lanes), 0)
    wanted = where[3] * experts + block * group + lane // rows
    weight = jnp.zeros((groups, lanes), F32)
    mask = jnp.zeros((groups, lanes), F32)
    for i in range(top):
        named = jnp.concatenate([entry[:, i * rows : (i + 1) * rows]] * group, axis=1)
        value = jnp.concatenate([facts[top + i : top + i + 1]] * group, axis=1)
        match = wanted == named
        mask = mask + jnp.where(match, 1.0, 0.0)
        weight = weight + jnp.where(match, value, 0.0)
    earlier = lax.broadcasted_iota(jnp.int32, (lanes, lanes), 0)
    later = lax.broadcasted_iota(jnp.int32, (lanes, lanes), 1)
    before = jnp.where(earlier < later, 1.0, 0.0).astype(BF16)
    rank = dot_nn(mask.astype(BF16), before)
    base = jnp.zeros((1, 1), F32)
    for g in range(groups):
        slot = jnp.where(mask[g : g + 1] > 0.0, rank[g : g + 1] + base, -1.0)
        slot_ref[g] = slot.astype(jnp.int32)
        weight_ref[g] = weight[g : g + 1]
        base = base + jnp.sum(mask[g : g + 1], axis=1, keepdims=True)


def route(facts, expert_table, where, experts, rows, swapped, loads):
    group = max(1, min(experts, 256 // rows))
    shape = (experts // group, 1, group * rows)
    return call(
        functools.partial(route_kernel, experts=experts, swapped=swapped),
        "route",
        [where, expert_table.reshape(1, -1), facts],
        [SMEM, VMEM, VMEM],
        [
            jax.ShapeDtypeStruct(shape, jnp.int32),
            jax.ShapeDtypeStruct(shape, F32),
            jax.ShapeDtypeStruct((1,), jnp.int32),
        ],
        out_specs=[VMEM, VMEM, SMEM],
        loads=loads,
    )


def pick_kernel(shift, slot_ref, weight_ref, pick_ref, spread_ref, slot_weight_ref):
    groups, _, lanes = slot_ref.shape
    capacity = pick_ref.shape[0]
    total = jnp.zeros((capacity, 1), F32)
    place = lax.broadcasted_iota(jnp.int32, (capacity, lanes), 0)
    for g in range(groups):
        hit = place == slot_ref[g] - shift[0]
        one = jnp.where(hit, 1.0, 0.0)
        part = slice(g * lanes, (g + 1) * lanes)
        pick_ref[:, part] = one.astype(BF16)
        spread_ref[part, :] = one.T.astype(BF16)
        total = total + jnp.sum(jnp.where(hit, weight_ref[g], 0.0), axis=1, keepdims=True)
    slot_weight_ref[...] = total


def pick_slots(shift, slots, weights, capacity, loads=()):
    pairs = slots.shape[0] * slots.shape[2]
    return call(
        pick_kernel,
        "pick",
        [shift.reshape(1), slots, weights],
        [SMEM, VMEM, VMEM],
        [
            jax.ShapeDtypeStruct((capacity, pairs), BF16),
            jax.ShapeDtypeStruct((pairs, capacity), BF16),
            jax.ShapeDtypeStruct((capacity, 1), F32),
        ],
        loads=loads,
    )


def project_kernel(where, *refs, sources):
    inputs, w_ref = refs[:sources], refs[sources]
    outs = refs[sources + 1 :]
    own_rows = inputs[0].shape[0]
    count = sources * own_rows
    half = outs[0].shape[1]
    stacked = jnp.concatenate([ref[...].astype(F32) for ref in inputs], axis=0).astype(BF16)
    target = lax.broadcasted_iota(jnp.int32, (count, count), 0)
    origin = lax.broadcasted_iota(jnp.int32, (count, count), 1)
    order = (target ^ (where[0] * own_rows)) == origin
    x = dot_nn(jnp.where(order, 1.0, 0.0).astype(BF16), stacked).astype(BF16)
    for k in range(2):
        start = pl.multiple_of((where[1] ^ k) * half, half)
        value = dot_nn(x, w_ref[:, pl.ds(start, half)])
        if k == 0:
            outs[0][...] = value
            outs[1][...] = value.astype(BF16)
        else:
            outs[2][...] = value.astype(BF16)


def project(inputs, out_weight, where, loads, anchors):
    sources = len(inputs)
    shape = (sources * inputs[0].shape[0], out_weight.shape[1] // 2)
    return call(
        functools.partial(project_kernel, sources=sources),
        "project",
        [where, *inputs, out_weight],
        [SMEM] + [VMEM] * (sources + 1),
        [
            jax.ShapeDtypeStruct(shape, F32),
            jax.ShapeDtypeStruct(shape, BF16),
            jax.ShapeDtypeStruct(shape, BF16),
        ],
        loads=loads,
        anchors=anchors,
    )


def gate_up_kernel(where, *refs, sources, group):
    inputs = refs[:sources]
    pick_ref, g_ref, u_ref, out_ref, x, both = refs[sources:]
    count = inputs[0].shape[0]
    rows = x.shape[0]
    experts, _, depth = g_ref.shape
    if sources == 1:
        x[...] = inputs[0][...]
    else:
        for k in range(sources):
            start = pl.multiple_of((where[3] ^ k) * count, count)
            x[pl.ds(start, count), :] = inputs[k][...]
    for i in range(experts // group):
        part = slice(i * group, (i + 1) * group)
        gate = dot_nt(x[...], g_ref[part].reshape(group * CHUNK, depth)).astype(BF16)
        up = dot_nt(x[...], u_ref[part].reshape(group * CHUNK, depth)).astype(BF16)
        for e in range(group):
            first = (i * group + e) * rows
            lanes = slice(e * CHUNK, (e + 1) * CHUNK)
            both[first : first + rows, :CHUNK] = gate[:, lanes]
            both[first : first + rows, CHUNK:] = up[:, lanes]
    out_ref[...] = dot_nn(pick_ref[...], both[...]).astype(BF16)


def gate_up(xs, pick, w_gate, w_up, where, index, group, loads):
    sources = len(xs)
    rows = xs[0].shape[0] * sources
    experts, _, depth = w_gate.shape
    (sent,), held = call(
        functools.partial(gate_up_kernel, sources=sources, group=group),
        f"gate_up_{index}",
        [where, *xs, pick, w_gate, w_up],
        [SMEM] + [VMEM] * (sources + 3),
        [jax.ShapeDtypeStruct((pick.shape[0], 2 * CHUNK), BF16)],
        scratch=[
            pltpu.VMEM((rows, depth), BF16),
            pltpu.VMEM((experts * rows, 2 * CHUNK), BF16),
        ],
        loads=loads,
        us=4,
    )
    return sent, held


def down_kernel(own_ref, other_ref, weight_ref, spread_ref, d_ref, *refs, carried):
    before, outs = refs[:carried], refs[carried:]
    experts, _, depth = d_ref.shape
    rows = spread_ref.shape[0] // experts
    both = own_ref[...].astype(F32) + other_ref[...].astype(F32)
    gate, up = both[:, :CHUNK], both[:, CHUNK:]
    hidden = (gate / (1.0 + jnp.exp(-gate)) * up * weight_ref[...]).astype(BF16)
    spread = dot_nn(spread_ref[...], hidden).astype(BF16)
    left = jnp.concatenate([spread[e * rows : (e + 1) * rows] for e in range(experts)], axis=1)
    total = dot_nn(left, d_ref[...].reshape(experts * CHUNK, depth))
    if carried:
        total = total + before[0][...]
    outs[0][...] = total


def down(own, other, slot_weight, spread, w_down, before, index):
    experts, _, depth = w_down.shape
    rows = spread.shape[0] // experts
    carried = [] if before is None else [before]
    (total,), _ = call(
        functools.partial(down_kernel, carried=len(carried)),
        f"down_{index}",
        [own, other, slot_weight, spread, w_down, *carried],
        [VMEM] * (5 + len(carried)),
        [jax.ShapeDtypeStruct((rows, depth), F32)],
        us=3,
    )
    return total


def load(loads, anchors, name):
    return call(lambda: None, name, [], [], [], loads=loads, anchors=anchors, us=2 * len(loads))[1]


def halves_kernel(where, value_ref, own_ref, other_ref):
    width = own_ref.shape[1]
    own_ref[...] = value_ref[:, pl.ds(pl.multiple_of(where[2] * width, width), width)]
    other_ref[...] = value_ref[:, pl.ds(pl.multiple_of((1 - where[2]) * width, width), width)]


def halves(value, where):
    rows, depth = value.shape
    vmem = pl.BlockSpec(memory_space=pltpu.VMEM)
    return pl.pallas_call(
        halves_kernel,
        in_specs=[pl.BlockSpec(memory_space=pltpu.SMEM), vmem],
        out_specs=[vmem] * 2,
        out_shape=[jax.ShapeDtypeStruct((rows, depth // 2), F32)] * 2,
        name="halves",
    )(where, value)


def split_kernel(where, own_ref, other_ref, *outs):
    count = outs[0].shape[0]
    for k in range(len(outs)):
        row = pl.ds(pl.multiple_of((where[3] ^ k) * count, count), count)
        outs[k][...] = (own_ref[row, :] + other_ref[row, :]).astype(outs[k].dtype)


def split(own, other, where, pieces):
    rows, width = own.shape
    vmem = pl.BlockSpec(memory_space=pltpu.VMEM)
    return pl.pallas_call(
        split_kernel,
        in_specs=[pl.BlockSpec(memory_space=pltpu.SMEM), vmem, vmem],
        out_specs=[vmem] * pieces,
        out_shape=[
            jax.ShapeDtypeStruct((rows // pieces, width), F32 if k == 0 else BF16)
            for k in range(pieces)
        ],
        name="split",
    )(where, own, other)


def xor_permute(value, axes, count, k):
    return lax.ppermute(value, axes, [(i, i ^ k) for i in range(count)])


def body(
    queries,
    keys_cache,
    values_cache,
    lengths,
    out_weight,
    routes,
    route_weight,
    expert_table,
    w_gate,
    w_up,
    w_down,
):
    pools, tps, subs = lax.axis_size("pool"), lax.axis_size("tp"), lax.axis_size("sub")
    pool, tp, sub = lax.axis_index("pool"), lax.axis_index("tp"), lax.axis_index("sub")
    shards = tps * subs
    shard = tp * subs + sub
    direct = tps == 2 and subs == 2 and pools == 4
    own_rows = queries.shape[0]
    pool_rows = own_rows * shards
    rows = pool_rows * pools
    experts, hidden_units, half_width = w_gate.shape
    top = routes.shape[1]
    where = jnp.stack([shard, tp, sub, pool]).astype(jnp.int32)

    facts = jnp.concatenate([routes.astype(F32), route_weight], axis=1).T
    capacity = -(-rows * top * 13 // (8 * pools * 16)) * 16
    group = max(1, min(experts, 256 // rows))
    gates, ups, downs = [[(w, c) for c in range(0, hidden_units, CHUNK)] for w in (w_gate, w_up, w_down)]
    chunks = len(gates)

    if direct:
        axes = ("tp", "sub")
        pieces, (out_held, gate_0) = attend(
            queries,
            keys_cache,
            values_cache,
            lengths,
            where,
            shards,
            [(out_weight, None), gates[0]],
        )
        facts, pieces = lax.optimization_barrier((facts, pieces))
        inputs = [pieces[0]] + [xor_permute(pieces[k], axes, shards, k) for k in range(1, shards)]
        blocks = [facts] + [xor_permute(facts, "pool", pools, k) for k in range(1, pools)]
        (up_0,) = load([ups[0]], [pieces[0]], "load_a")
        (kept, near, far), (gate_1,) = project(inputs, out_held, where, [gates[1]], [up_0])
        (up_1,) = load([ups[1]], [near], "load_b")
        x_sum = kept
        for k in range(1, shards):
            value = near if k < subs else far
            x_sum = x_sum + xor_permute(value, axes, shards, k).astype(F32)
        x_half, up_1 = lax.optimization_barrier((x_sum.astype(BF16), up_1))
        xs = [x_half] + [xor_permute(x_half, "pool", pools, k) for k in range(1, pools)]
        blocks, _ = lax.optimization_barrier((blocks, x_half))
        (slots, weights, largest), (gate_2,) = route(
            jnp.stack(blocks), expert_table, where, experts, rows, True, [gates[2]]
        )
        (pick, spread, slot_weight), (up_2,) = pick_slots(
            jnp.int32(0), slots, weights, capacity, [ups[2]]
        )
        (down_0,) = load([downs[0]], [pick], "load_c")
        held = [(gate_0, up_0), (gate_1, up_1), (gate_2, up_2)]
        theirs = lax.ppermute(
            lax.dynamic_slice_in_dim(x_half, (shard ^ subs) * own_rows, own_rows, 0),
            "tp",
            [(0, 1), (1, 0)],
        )
        mine = lax.dynamic_slice_in_dim(x_half, shard * own_rows, own_rows, 0)
        attended = jnp.where(
            tp == 0,
            jnp.concatenate([mine, theirs], axis=1),
            jnp.concatenate([theirs, mine], axis=1),
        )
        held_down, sent = [down_0], []
        for c in range(chunks):
            value, more_held = gate_up(
                xs, pick, *held[c], where, c, group, downs[c + 1 : c + 2]
            )
            sent.append(value)
            held_down += more_held
    else:
        blocks = lax.all_gather(facts, "pool", axis=0)
        (slots, weights, largest), _ = route(blocks, expert_table, where, experts, rows, False, [])
        (pick, spread, slot_weight), _ = pick_slots(jnp.int32(0), slots, weights, capacity)
        (attention,), _ = attend(queries, keys_cache, values_cache, lengths, where * 0, 1, [])
        head_rows = lax.all_to_all(
            attention, ("tp", "sub"), split_axis=1, concat_axis=0, tiled=True
        )
        partial = jnp.dot(head_rows, out_weight, preferred_element_type=F32)
        x_sum = lax.psum_scatter(partial, ("tp", "sub"), scatter_dimension=1, tiled=True)
        x_pool = x_sum.astype(BF16)
        attended = lax.all_to_all(x_pool, ("tp", "sub"), split_axis=0, concat_axis=1, tiled=True)
        x_part = lax.all_gather(x_pool, "pool", axis=0, tiled=True)
        xs = [lax.all_gather(x_part, "sub", axis=1, tiled=True)]
        held = load(gates + ups + downs, [], "load")
        held_down = held[2 * chunks :]
        sent = [
            gate_up(xs, pick, held[c], held[chunks + c], where, c, group, [])[0]
            for c in range(chunks)
        ]

    def exchange(value):
        if tps == 2:
            return value, lax.ppermute(value, "tp", [(0, 1), (1, 0)])
        return lax.psum(value.astype(F32), "tp").astype(BF16), jnp.zeros_like(value)

    result = None
    both = [exchange(value) for value in sent]
    for c in range(chunks):
        result = down(*both[c], slot_weight, spread, held_down[c], result, c)

    def combine(value):
        if not direct:
            value = lax.psum_scatter(value, "pool", scatter_dimension=0, tiled=True)
            return lax.psum_scatter(value, "sub", scatter_dimension=1, tiled=True)
        own, other = halves(value, where)
        pieces = split(own, xor_permute(other, "sub", subs, 1), where, pools)
        total = pieces[0]
        for k in range(1, pools):
            total = total + xor_permute(pieces[k], "pool", pools, k).astype(F32)
        return total

    def more(state):
        k, total = state
        k, *held = lax.optimization_barrier((k, *xs))
        order = lax.iota(jnp.int32, len(held)) ^ (pool if direct else 0)
        x = jnp.take(jnp.stack(held), order, axis=0).reshape(rows, half_width)
        (pick, spread, slot_weight), _ = pick_slots(k * capacity, slots, weights, capacity)
        gate = jnp.einsum("rd,efd->erf", x, w_gate, preferred_element_type=F32)
        up = jnp.einsum("rd,efd->erf", x, w_up, preferred_element_type=F32)
        both = jnp.concatenate([gate, up], axis=2).astype(BF16)
        both = both.reshape(experts * rows, 2 * hidden_units)
        sent = jnp.dot(pick, both, preferred_element_type=F32).astype(BF16)
        if tps == 2:
            both = sent.astype(F32) + lax.ppermute(sent, "tp", [(0, 1), (1, 0)]).astype(F32)
        else:
            both = lax.psum(sent.astype(F32), "tp")
        hidden = jax.nn.silu(both[:, :hidden_units]) * both[:, hidden_units:] * slot_weight
        spread = jnp.dot(spread, hidden.astype(BF16), preferred_element_type=F32).astype(BF16)
        spread = spread.reshape(experts, rows, hidden_units)
        value = jnp.einsum("erf,efd->rd", spread, w_down, preferred_element_type=F32)
        return k + 1, total + combine(value)

    expert_sum = combine(result)
    _, extra = lax.while_loop(
        lambda state: state[0] * capacity < largest[0],
        more,
        (jnp.int32(1), jnp.zeros((pool_rows, half_width // subs), F32)),
    )
    return attended, (expert_sum + extra).astype(BF16)


def solution(mesh):
    in_specs = (
        P(("grp", "pool", "tp", "sub"), None),
        P(("grp", "pool", "tp", "sub"), None, None),
        P(("grp", "pool", "tp", "sub"), None, None),
        P(("grp", "pool", "tp", "sub")),
        P(("tp", "sub"), None),
        P(("grp", "pool"), None),
        P(("grp", "pool"), None),
        P(),
        P("pool", "sub", "tp"),
        P("pool", "sub", "tp"),
        P("pool", "sub", "tp"),
    )
    out_specs = (P(("grp", "pool", "tp", "sub"), None), P(("grp", "pool"), ("tp", "sub")))
    return jax.shard_map(body, mesh=mesh, in_specs=in_specs, out_specs=out_specs, check_vma=False)
```

time: 256 us -> 76.3 us (0.30)
  waiting for transfers between devices: 133 us -> 4.6 us
  Pallas kernels: 0 us -> 41.1 us
  blocking collectives: 40 us -> 0 us
  matrix products: 36.2 us -> 0 us
  local copies, waits for them, and re-layouts: 17.3 us -> 2.79 us
  starting transfers between devices: 9.29 us -> 22.7 us
  between operations: 13.9 us -> 0.88 us
    psum x1 -> x0, waiting for transfers between devices: 87 us -> none  [body(): gate_value, up_value = lax.psum((gate_part, up_part), 'tp')]
    pallas_call x0 -> x15, Pallas kernels: none -> 41.1 us  [the longest x13 37.8 us: call(): pl.pallas_call(run, in_specs=list(specs) + [HBM] * count_load + [ANY] * l...]
    dot_general x7 -> x0, matrix products: 36.2 us -> none  [the longest x1 10.5 us: body(): jnp.einsum('pjcd,jfd->pjcf', incoming, w_up, preferred_element_type=jnp.f...]
    all_to_all x1 -> x0, blocking collectives: 28.3 us -> none  [body(): lax.all_to_all(own_slice, 'pool', split_axis=0, concat_axis=0, tiled=True)]
    all_to_all x2 -> x0, waiting for transfers between devices: 25.7 us -> none  [the longest x1 22.6 us: body(): lax.all_to_all(expert_rows, 'pool', split_axis=0, concat_axis=0, tiled=True)]
    ppermute x0 -> x20, starting transfers between devices: none -> 22.7 us  [the longest x16 18.4 us: xor_permute(): return lax.ppermute(value, axes, [(i, i ^ k) for i in range(count)])]
    psum x1 -> x0, blocking collectives: 11.7 us -> none  [body(): summed = lax.psum(partial_value, ('tp', 'sub'))]
    reduce_scatter x1 -> x0, waiting for transfers between devices: 11.7 us -> none  [body(): lax.psum_scatter(partial_rows, 'sub', scatter_dimension=3, tiled=True)]
  transfers between devices with their start and end apart: 5 -> 20, of which waited for: 5 -> 4; matrix products, arithmetic and copies ran while one was open for 1% -> 1% of each run, Pallas kernels for 0% -> 33%
where the time goes in v2:
time: 76.3 us; the launch traced here: 75.7 us
  Pallas kernels  41.1 us (54%)
  starting transfers between devices  22.7 us (30%)
  waiting for transfers between devices  4.6 us (6%)
  local copies, waits for them, and re-layouts  2.79 us (4%)
  other arithmetic  2.72 us (4%)
  between operations  0.88 us (1%)
  loops' own time  0.84 us (1%)
    pallas_call x13, Pallas kernels, call(): pl.pallas_call(run, in_specs=list(specs) + [HBM] * count_load + [ANY] * l...  37.8 us
    ppermute x16, starting transfers between devices, xor_permute(): return lax.ppermute(value, axes, [(i, i ^ k) for i in range(count)])  18.4 us
    ppermute x16, waiting for transfers between devices, xor_permute(): return lax.ppermute(value, axes, [(i, i ^ k) for i in range(count)])  4.59 us
    ppermute x3, starting transfers between devices, exchange(): return (value, lax.ppermute(value, 'tp', [(0, 1), (1, 0)]))  3.29 us
    unnamed x15, local copies, waits for them, and re-layouts  2.77 us
    pallas_call x1, Pallas kernels, halves(): pl.pallas_call(halves_kernel, in_specs=[pl.BlockSpec(memory_space=pltpu.S...  1.69 us
    pallas_call x1, Pallas kernels, split(): pl.pallas_call(split_kernel, in_specs=[pl.BlockSpec(memory_space=pltpu.SM...  1.62 us
  transfers between devices with their start and end apart: 20, of which 4 were waited for; matrix products, arithmetic and copies ran while one was open for 1% of the time, Pallas kernels for 33%

profile of v2, /device:TPU:0, one launch (start us, length us, event | category | flops | bytes accessed | tf_op | source)
XLA Modules:
  0.0 75.7 jit_solution(7159274913554686581)
XLA Ops:
  0.6 0.7 convert_element_type.53
  1.3 0.8 %copy.15 = bf16[1,4,32,128]{3,2,1,0:T(8,128)(2,1)S(1)} copy(bf16[1,4,32,128]{3,1,2,0:T(4,128)(2,1)} %bitcast.93) | data formatting | bytes 65536
  2.1 0.7 maximum_bitcast_fusion
  2.8 0.1 pad_add_fusion.refs_1_.refs_0_.where
  2.9 0.7 copy-done.1
  3.5 5.2 %attention.1 = (bf16[4,1024]{1,0:T(4,128)(2,1)S(1)}, bf16[4,1024]{1,0:T(4,128)(2,1)S(1)}, bf16[4,1024]{1,0:T(4,128)(2,1)S(1)}, bf16[4,1024]{1,0:T(4,128)(2,1)S(1...) custom-call(s32[4]{0:T(128)S(1)} %copy-done.1, s32[4]{0:T(128)S(1)} %pad_add_fusion.refs_1_.refs_0_.where, ...), custom_call_target="tpu_custom_call" | custom-call | bytes 12000000 | tf_op jit(solution)/shard_map/attention/pallas_call | solution.py:78
  8.7 0.5 collective-permute-start.5
  9.2 2.6 %collective-permute-start.6 = (bf16[4,1024]{1,0:T(4,128)(2,1)S(1)}, bf16[4,1024]{1,0:T(4,128)(2,1)S(1)}, u32[]{:S(2)}, u32[]{:S(2)}) collective-permute-start(bf16[4,1024]{1,0:T(4,128)(2,1)S(1)} %get-tuple-element.134), channel_id=1, source_target_pairs={{0,2},{1,3},{2,0},{3,1},{4,6},{5,7},{6,4},{7,5},{8,10},{9,11},{10,... | collective-permute-start | bytes 24584 | tf_op jit(solution)/shard_map/ppermute | solution.py:399
  11.8 0.1 collective-permute-start.7
  11.9 2.2 %load_a.1.refs_7_ = bf16[16,128,1024]{2,1,0:T(8,128)(2,1)S(1)} custom-call(bf16[16,384,1024]{2,1,0:T(8,128)(2,1)} %refs_3_.5, bf16[4,1024]{1,0:T(4,128)(2,1)S(1)} %get-tuple-element.132.refs_1_), custom_call_target="tpu_custom_call" | custom-call | bytes 6000000 | tf_op jit(solution)/shard_map/load_a/pallas_call | solution.py:78
  14.1 0.0 collective-permute-done.5.refs_2_
  14.1 0.0 collective-permute-done.6.refs_3_
  14.1 0.8 %collective-permute-done.7.refs_4_ = bf16[4,1024]{1,0:T(4,128)(2,1)S(1)} collective-permute-done((bf16[4,1024]{1,0:T(4,128)(2,1)S(1)}, bf16[4,1024]{1,0:T(4,128)(2,1)S(1)}, u32[]{:S(2)}, u32[]{:S(2)}) %collective-permute-start.7) | collective-permute-done | bytes 8224 | tf_op jit(solution)/shard_map/ppermute | solution.py:399
  14.9 2.7 %project.1 = (f32[16,1024]{1,0:T(8,128)S(1)}, bf16[16,1024]{1,0:T(8,128)(2,1)S(1)}, bf16[16,1024]{1,0:T(8,128)(2,1)S(1)}, bf16[16,128,1024]{2,1,0:T(8,128)(2,1)S(1)}) custom-call(s32[4]{0:T(128)S(1)} %pad_add_fusion.refs_1_.refs_0_.where, bf16[4,1024]{1,0:T(4,128)(2,1)S(1)} %get-tuple-element.132.refs_1_, ...), custom_call_target="tpu_custom_call" | custom-call | bytes 6000000 | tf_op jit(solution)/shard_map/project/pallas_call | solution.py:78
  17.6 1.0 %collective-permute-start.10 = (bf16[16,1024]{1,0:T(8,128)(2,1)S(1)}, bf16[16,1024]{1,0:T(8,128)(2,1)S(1)}, u32[]{:S(2)}, u32[]{:S(2)}) collective-permute-start(bf16[16,1024]{1,0:T(8,128)(2,1)S(1)} %get-tuple-element.139), channel_id=1, source_target_pairs={{0,3},{1,2},{2,1},{3,0},{4,7},{5,6},{6,5},{7,4},{8,11},{9,10},{10,... | collective-permute-start | bytes 98312 | tf_op jit(solution)/shard_map/ppermute | solution.py:399
  18.6 0.9 %collective-permute-start.9 = (bf16[16,1024]{1,0:T(8,128)(2,1)S(1)}, bf16[16,1024]{1,0:T(8,128)(2,1)S(1)}, u32[]{:S(2)}, u32[]{:S(2)}) collective-permute-start(bf16[16,1024]{1,0:T(8,128)(2,1)S(1)} %get-tuple-element.139), channel_id=1, source_target_pairs={{0,2},{1,3},{2,0},{3,1},{4,6},{5,7},{6,4},{7,5},{8,10},{9,11},{10,... | collective-permute-start | bytes 98312 | tf_op jit(solution)/shard_map/ppermute | solution.py:399
  19.5 0.1 collective-permute-start.8
  19.5 1.6 %collective-permute-start.15 = (f32[16,16]{1,0:T(8,128)S(1)}, f32[16,16]{1,0:T(8,128)S(1)}, u32[]{:S(2)}, u32[]{:S(2)}) collective-permute-start(f32[16,16]{1,0:T(8,128)S(1)} %maximum_bitcast_fusion), channel_id=1, source_target_pairs={{0,4},{4,0},{8,12},{12,8},{1,5},{5,1},{9,13},{13,9},{2,6},{6,2},{1... | collective-permute-start | bytes 3080 | tf_op jit(solution)/shard_map/ppermute | solution.py:399
  21.1 2.2 %load_b.1.refs_7_ = bf16[16,128,1024]{2,1,0:T(8,128)(2,1)S(1)} custom-call(bf16[16,384,1024]{2,1,0:T(8,128)(2,1)} %refs_3_.5, bf16[16,1024]{1,0:T(8,128)(2,1)S(1)} %get-tuple-element.138.refs_1_), custom_call_target="tpu_custom_call" | custom-call | bytes 6000000 | tf_op jit(solution)/shard_map/load_b/pallas_call | solution.py:78
  23.3 2.7 %collective-permute-start.16 = (f32[16,16]{1,0:T(8,128)S(1)}, f32[16,16]{1,0:T(8,128)S(1)}, u32[]{:S(2)}, u32[]{:S(2)}) collective-permute-start(f32[16,16]{1,0:T(8,128)S(1)} %maximum_bitcast_fusion), channel_id=1, source_target_pairs={{0,8},{4,12},{8,0},{12,4},{1,9},{5,13},{9,1},{13,5},{2,10},{6,14},... | collective-permute-start | bytes 3080 | tf_op jit(solution)/shard_map/ppermute | solution.py:399
  26.0 0.0 collective-permute-done.10
  26.0 0.2 collective-permute-start.17
  26.2 0.0 collective-permute-done.9
  26.2 0.0 collective-permute-done.8
  26.2 0.7 collective-permute-start.12
  27.0 3.5 %collective-permute-start.13 = (bf16[16,1024]{1,0:T(8,128)(2,1)S(1)}, bf16[16,1024]{1,0:T(8,128)(2,1)S(1)}, u32[]{:S(2)}, u32[]{:S(2)}) collective-permute-start(bf16[16,1024]{1,0:T(8,128)(2,1)S(1)} %add_convert_fusion.refs_1_), channel_id=1, source_target_pairs={{0,8},{4,12},{8,0},{12,4},{1,9},{5,13},{9,1},{13,5},{2,10},{6,14},... | collective-permute-start | bytes 98312 | tf_op jit(solution)/shard_map/ppermute | solution.py:399
  30.5 0.0 collective-permute-done.15
  30.5 0.2 collective-permute-start.14
  30.7 0.0 collective-permute-done.16
  30.7 0.7 collective-permute-done.17
  31.4 3.4 %route.1 = (s32[4,1,256]{2,1,0:T(1,128)S(1)}, f32[4,1,256]{2,1,0:T(1,128)S(1)}, s32[1]{0:T(128)}, bf16[16,128,1024]{2,1,0:T(8,128)(2,1)S(1)}) custom-call(s32[4]{0:T(128)S(1)} %pad_add_fusion.refs_1_.refs_0_.where, s32[1,64]{1,0:T(1,128)S(1)} %bitcast.85, f32[4,16,16]{2,1,0:T(8,128)S(1)} %pad_maximum_fusion.1.refs_2_, bf16[16,384,1024]{2,1,0:T(8,128)(2,1)} %refs_3_.4), custom_call_target="tpu_custom_call" | custom-call | bytes 6000000 | tf_op jit(solution)/shard_map/route/pallas_call | solution.py:78
  34.9 2.3 %pick.2 = (bf16[208,1024]{1,0:T(8,128)(2,1)S(1)}, bf16[1024,208]{1,0:T(8,128)(2,1)S(1)}, f32[208,1]{1,0:T(8,128)S(1)}, bf16[16,128,1024]{2,1,0:T(8,128)(2,1)S(1)}) custom-call(s32[1]{0:T(128)} %constant.47.clone.1.refs_0_, s32[4,1,256]{2,1,0:T(1,128)S(1)} %get-tuple-element.319.refs_1_, f32[4,1,256]{2,1,0:T(1,128)S(1)} %get-tuple-element.320.refs_2_, ...), custom_call_target="tpu_custom_call" | custom-call | bytes 6000000 | tf_op jit(solution)/shard_map/pick/pallas_call | solution.py:78
  37.1 0.0 collective-permute-done.12.refs_2_
  37.1 0.0 collective-permute-done.13.refs_3_
  37.2 0.0 collective-permute-done.14.refs_4_
  37.2 5.5 %gate_up_0.1 = (bf16[208,256]{1,0:T(8,128)(2,1)S(1)}, bf16[16,128,1024]{2,1,0:T(8,128)(2,1)S(1)}) custom-call(s32[4]{0:T(128)S(1)} %pad_add_fusion.refs_1_.refs_0_.where, bf16[16,1024]{1,0:T(8,128)(2,1)S(1)} %add_convert_fusion.refs_1_, bf16[16,1024]{1,0:T(8,128)(2,1)S(1)} %collective-permute-done.12.refs_2_, ...), custom_call_target="tpu_custom_call" | custom-call | bytes 12000000 | tf_op jit(solution)/shard_map/gate_up_0/pallas_call | solution.py:78
  42.7 1.1 %collective-permute-start.20 = (bf16[208,256]{1,0:T(8,128)(2,1)S(1)}, bf16[208,256]{1,0:T(8,128)(2,1)S(1)}, u32[]{:S(2)}, u32[]{:S(2)}) collective-permute-start(bf16[208,256]{1,0:T(8,128)(2,1)S(1)} %get-tuple-element.159.refs_0_), channel_id=1, source_target_pairs={{0,2},{2,0},{1,3},{3,1},{4,6},{6,4},{5,7},{7,5},{8,10},{10,8},{9,1... | collective-permute-start | bytes 319496 | tf_op jit(solution)/shard_map/ppermute | solution.py:506
  43.8 5.5 %gate_up_1.1 = (bf16[208,256]{1,0:T(8,128)(2,1)S(1)}, bf16[16,128,1024]{2,1,0:T(8,128)(2,1)S(1)}) custom-call(s32[4]{0:T(128)S(1)} %pad_add_fusion.refs_1_.refs_0_.where, bf16[16,1024]{1,0:T(8,128)(2,1)S(1)} %add_convert_fusion.refs_1_, bf16[16,1024]{1,0:T(8,128)(2,1)S(1)} %collective-permute-done.12.refs_2_, ...), custom_call_target="tpu_custom_call" | custom-call | bytes 12000000 | tf_op jit(solution)/shard_map/gate_up_1/pallas_call | solution.py:78
  49.3 1.0 %collective-permute-start.19 = (bf16[208,256]{1,0:T(8,128)(2,1)S(1)}, bf16[208,256]{1,0:T(8,128)(2,1)S(1)}, u32[]{:S(2)}, u32[]{:S(2)}) collective-permute-start(bf16[208,256]{1,0:T(8,128)(2,1)S(1)} %get-tuple-element.156.refs_0_), channel_id=1, source_target_pairs={{0,2},{2,0},{1,3},{3,1},{4,6},{6,4},{5,7},{7,5},{8,10},{10,8},{9,1... | collective-permute-start | bytes 319496 | tf_op jit(solution)/shard_map/ppermute | solution.py:506
  50.3 3.4 %gate_up_2.1.refs_0_ = bf16[208,256]{1,0:T(8,128)(2,1)S(1)} custom-call(s32[4]{0:T(128)S(1)} %pad_add_fusion.refs_1_.refs_0_.where, bf16[16,1024]{1,0:T(8,128)(2,1)S(1)} %add_convert_fusion.refs_1_, bf16[16,1024]{1,0:T(8,128)(2,1)S(1)} %collective-permute-done.12.refs_2_, bf16[16,1024]{1,0:T(8,128)(2,1)S(1)} %collective-permute-done.13.refs_3_, ...), custom_call_target="tpu_custom_call" | custom-call | bytes 12000000 | tf_op jit(solution)/shard_map/gate_up_2/pallas_call | solution.py:78
  53.7 1.1 %collective-permute-start.18 = (bf16[208,256]{1,0:T(8,128)(2,1)S(1)}, bf16[208,256]{1,0:T(8,128)(2,1)S(1)}, u32[]{:S(2)}, u32[]{:S(2)}) collective-permute-start(bf16[208,256]{1,0:T(8,128)(2,1)S(1)} %gate_up_2.1.refs_0_), channel_id=1, source_target_pairs={{0,2},{2,0},{1,3},{3,1},{4,6},{6,4},{5,7},{7,5},{8,10},{10,8},{9,1... | collective-permute-start | bytes 319496 | tf_op jit(solution)/shard_map/ppermute | solution.py:506
  54.9 2.2 %load_c.1.refs_4_ = bf16[16,128,1024]{2,1,0:T(8,128)(2,1)S(1)} custom-call(bf16[16,384,1024]{2,1,0:T(8,128)(2,1)} %refs_0_.7, bf16[208,1024]{1,0:T(8,128)(2,1)S(1)} %get-tuple-element.148.refs_5_.refs_1_), custom_call_target="tpu_custom_call" | custom-call | bytes 6000000 | tf_op jit(solution)/shard_map/load_c/pallas_call | solution.py:78
  57.1 0.0 collective-permute-done.20.refs_1_
  57.1 1.1 %down_0.1.refs_5_ = f32[64,1024]{1,0:T(8,128)S(1)} custom-call(bf16[208,256]{1,0:T(8,128)(2,1)S(1)} %get-tuple-element.159.refs_0_, bf16[208,256]{1,0:T(8,128)(2,1)S(1)} %collective-permute-done.20.refs_1_, f32[208,1]{1,0:T(8,128)S(1)} %get-tuple-element.151.refs_2_, bf16[1024,208]{1,0:T(8,128)(2,1)S(1)} %get-tuple-element.152.refs_3_, ...), custom_call_target="tpu_custom_call" | custom-call | bytes 9000000 | tf_op jit(solution)/shard_map/down_0/pallas_call | solution.py:78
  58.2 0.0 collective-permute-done.19.refs_1_
  58.2 1.1 %down_1.1.refs_5_ = f32[64,1024]{1,0:T(8,128)S(1)} custom-call(bf16[208,256]{1,0:T(8,128)(2,1)S(1)} %get-tuple-element.156.refs_0_, bf16[208,256]{1,0:T(8,128)(2,1)S(1)} %collective-permute-done.19.refs_1_, f32[208,1]{1,0:T(8,128)S(1)} %get-tuple-element.151.refs_2_, bf16[1024,208]{1,0:T(8,128)(2,1)S(1)} %get-tuple-element.152.refs_3_, ...), custom_call_target="tpu_custom_call" | custom-call | bytes 9000000 | tf_op jit(solution)/shard_map/down_1/pallas_call | solution.py:78
  59.3 0.0 collective-permute-done.18.refs_1_
  59.3 1.1 %down_2.1.value_ref = f32[64,1024]{1,0:T(8,128)S(1)} custom-call(bf16[208,256]{1,0:T(8,128)(2,1)S(1)} %gate_up_2.1.refs_0_, bf16[208,256]{1,0:T(8,128)(2,1)S(1)} %collective-permute-done.18.refs_1_, f32[208,1]{1,0:T(8,128)S(1)} %get-tuple-element.151.refs_2_, bf16[1024,208]{1,0:T(8,128)(2,1)S(1)} %get-tuple-element.152.refs_3_, ...), custom_call_target="tpu_custom_call" | custom-call | bytes 9000000 | tf_op jit(solution)/shard_map/down_2/pallas_call | solution.py:78
  60.4 0.7 copy-done
  61.0 1.7 %halves.2 = (f32[64,512]{1,0:T(8,128)}, f32[64,512]{1,0:T(8,128)}) custom-call(s32[4]{0:T(128)S(1)} %pad_add_fusion.refs_1_.refs_0_.where, f32[64,1024]{1,0:T(8,128)} %copy-done), custom_call_target="tpu_custom_call" | custom-call | tf_op jit(solution)/shard_map/halves/pallas_call | solution.py:367
  62.7 0.0 collective-permute-start.21
  62.8 1.0 %collective-permute-start.11 = (bf16[4,1024]{1,0:T(4,128)(2,1)S(1)}, bf16[4,1024]{1,0:T(4,128)(2,1)S(1)}, u32[]{:S(2)}, u32[]{:S(2)}) collective-permute-start(bf16[4,1024]{1,0:T(4,128)(2,1)S(1)} %get-tuple-element.197), channel_id=1, source_target_pairs={{0,2},{2,0},{1,3},{3,1},{4,6},{6,4},{5,7},{7,5},{8,10},{10,8},{9,1... | collective-permute-start | bytes 24584 | tf_op jit(solution)/shard_map/ppermute | solution.py:465
  63.8 0.5 collective-permute-done.21.other_ref
  64.3 0.7 copy-done.5
  64.9 1.6 %split.2 = (f32[16,512]{1,0:T(8,128)}, bf16[16,512]{1,0:T(8,128)(2,1)}, bf16[16,512]{1,0:T(8,128)(2,1)}, bf16[16,512]{1,0:T(8,128)(2,1)}) custom-call(s32[4]{0:T(128)S(1)} %pad_add_fusion.refs_1_.refs_0_.where, f32[64,512]{1,0:T(8,128)} %get-tuple-element.160.own_ref, f32[64,512]{1,0:T(8,128)} %copy-done.5), custom_call_target="tpu_custom_call" | custom-call | tf_op jit(solution)/shard_map/split/pallas_call | solution.py:386
  66.6 2.9 %collective-permute-start.24 = (bf16[16,512]{1,0:T(8,128)(2,1)}, bf16[16,512]{1,0:T(8,128)(2,1)S(1)}, u32[]{:S(2)}, u32[]{:S(2)}) collective-permute-start(bf16[16,512]{1,0:T(8,128)(2,1)} %get-tuple-element.165), channel_id=1, source_target_pairs={{0,12},{4,8},{8,4},{12,0},{1,13},{5,9},{9,5},{13,1},{2,14},{6,10},... | collective-permute-start | bytes 49160 | tf_op jit(solution)/shard_map/ppermute | solution.py:399
  69.5 0.8 %while.10 = (s32[]{:T(128)}, f32[16,512]{1,0:T(8,128)S(1)}, s32[1]{0:T(128)}, bf16[16,1024]{1,0:T(8,128)(2,1)S(1)}, bf16[16,1024]{1,0:T(8,128)(2,1)S(1)}, /*inde...) while((s32[]{:T(128)}, f32[16,512]{1,0:T(8,128)S(1)}, ...), condition=%wide.region_1.2_spmd, body=%wide.region_0.1_spmd.sunk | while | flops 2912496640 | bytes 105876032 | solution.py:547
  70.3 0.1 collective-permute-start.23
  70.4 1.5 %collective-permute-start.22 = (bf16[16,512]{1,0:T(8,128)(2,1)S(1)}, bf16[16,512]{1,0:T(8,128)(2,1)S(1)}, u32[]{:S(2)}, u32[]{:S(2)}) collective-permute-start(bf16[16,512]{1,0:T(8,128)(2,1)S(1)} %copy-done.7), channel_id=1, source_target_pairs={{0,4},{4,0},{8,12},{12,8},{1,5},{5,1},{9,13},{13,9},{2,6},{6,2},{1... | collective-permute-start | bytes 49160 | tf_op jit(solution)/shard_map/ppermute | solution.py:399
  71.9 0.0 collective-permute-done.11
  71.9 0.6 maximum_select_fusion
  72.5 0.0 collective-permute-done.24
  72.5 2.5 %collective-permute-done.23 = bf16[16,512]{1,0:T(8,128)(2,1)S(1)} collective-permute-done((bf16[16,512]{1,0:T(8,128)(2,1)S(1)}, bf16[16,512]{1,0:T(8,128)(2,1)S(1)}, u32[]{:S(2)}, u32[]{:S(2)}) %collective-permute-start.23) | collective-permute-done | bytes 16416 | tf_op jit(solution)/shard_map/ppermute | solution.py:399
  75.0 0.6 add_convert_fusion.1
  (16 shorter events, 0.1 us)
Async XLA Ops:
  2.9 0.7 copy-start.1
  8.7 5.4 %collective-permute-start.5 = (bf16[4,1024]{1,0:T(4,128)(2,1)S(1)}, bf16[4,1024]{1,0:T(4,128)(2,1)S(1)}, u32[]{:S(2)}, u32[]{:S(2)}) collective-permute-start(bf16[4,1024]{1,0:T(4,128)(2,1)S(1)} %get-tuple-element.133), channel_id=1, source_target_pairs={{0,1},{1,0},{2,3},{3,2},{4,5},{5,4},{6,7},{7,6},{8,9},{9,8},{10,11... | collective-permute-start | bytes 24584 | tf_op jit(solution)/shard_map/ppermute | solution.py:399
  9.2 4.9 %collective-permute-start.6 = (bf16[4,1024]{1,0:T(4,128)(2,1)S(1)}, bf16[4,1024]{1,0:T(4,128)(2,1)S(1)}, u32[]{:S(2)}, u32[]{:S(2)}) collective-permute-start(bf16[4,1024]{1,0:T(4,128)(2,1)S(1)} %get-tuple-element.134), channel_id=1, source_target_pairs={{0,2},{1,3},{2,0},{3,1},{4,6},{5,7},{6,4},{7,5},{8,10},{9,11},{10,... | collective-permute-start | bytes 24584 | tf_op jit(solution)/shard_map/ppermute | solution.py:399
  11.8 3.1 %collective-permute-start.7 = (bf16[4,1024]{1,0:T(4,128)(2,1)S(1)}, bf16[4,1024]{1,0:T(4,128)(2,1)S(1)}, u32[]{:S(2)}, u32[]{:S(2)}) collective-permute-start(bf16[4,1024]{1,0:T(4,128)(2,1)S(1)} %get-tuple-element.135), channel_id=1, source_target_pairs={{0,3},{1,2},{2,1},{3,0},{4,7},{5,6},{6,5},{7,4},{8,11},{9,10},{10,... | collective-permute-start | bytes 24584 | tf_op jit(solution)/shard_map/ppermute | solution.py:399
  17.6 8.4 %collective-permute-start.10 = (bf16[16,1024]{1,0:T(8,128)(2,1)S(1)}, bf16[16,1024]{1,0:T(8,128)(2,1)S(1)}, u32[]{:S(2)}, u32[]{:S(2)}) collective-permute-start(bf16[16,1024]{1,0:T(8,128)(2,1)S(1)} %get-tuple-element.139), channel_id=1, source_target_pairs={{0,3},{1,2},{2,1},{3,0},{4,7},{5,6},{6,5},{7,4},{8,11},{9,10},{10,... | collective-permute-start | bytes 98312 | tf_op jit(solution)/shard_map/ppermute | solution.py:399
  18.6 7.6 %collective-permute-start.9 = (bf16[16,1024]{1,0:T(8,128)(2,1)S(1)}, bf16[16,1024]{1,0:T(8,128)(2,1)S(1)}, u32[]{:S(2)}, u32[]{:S(2)}) collective-permute-start(bf16[16,1024]{1,0:T(8,128)(2,1)S(1)} %get-tuple-element.139), channel_id=1, source_target_pairs={{0,2},{1,3},{2,0},{3,1},{4,6},{5,7},{6,4},{7,5},{8,10},{9,11},{10,... | collective-permute-start | bytes 98312 | tf_op jit(solution)/shard_map/ppermute | solution.py:399
  19.5 12.0 %copy-start.2 = (s32[64]{0:T(128)S(1)}, s32[64]{0:T(128)}, u32[]{:S(2)}) copy-start(s32[64]{0:T(128)} %param.20) | copy-start | bytes 772
  19.5 6.7 %collective-permute-start.8 = (bf16[16,1024]{1,0:T(8,128)(2,1)S(1)}, bf16[16,1024]{1,0:T(8,128)(2,1)S(1)}, u32[]{:S(2)}, u32[]{:S(2)}) collective-permute-start(bf16[16,1024]{1,0:T(8,128)(2,1)S(1)} %get-tuple-element.138.refs_1_), channel_id=1, source_target_pairs={{0,1},{1,0},{2,3},{3,2},{4,5},{5,4},{6,7},{7,6},{8,9},{9,8},{10,11... | collective-permute-start | bytes 98312 | tf_op jit(solution)/shard_map/ppermute | solution.py:399
  19.5 10.9 %collective-permute-start.15 = (f32[16,16]{1,0:T(8,128)S(1)}, f32[16,16]{1,0:T(8,128)S(1)}, u32[]{:S(2)}, u32[]{:S(2)}) collective-permute-start(f32[16,16]{1,0:T(8,128)S(1)} %maximum_bitcast_fusion), channel_id=1, source_target_pairs={{0,4},{4,0},{8,12},{12,8},{1,5},{5,1},{9,13},{13,9},{2,6},{6,2},{1... | collective-permute-start | bytes 3080 | tf_op jit(solution)/shard_map/ppermute | solution.py:399
  23.3 7.4 %collective-permute-start.16 = (f32[16,16]{1,0:T(8,128)S(1)}, f32[16,16]{1,0:T(8,128)S(1)}, u32[]{:S(2)}, u32[]{:S(2)}) collective-permute-start(f32[16,16]{1,0:T(8,128)S(1)} %maximum_bitcast_fusion), channel_id=1, source_target_pairs={{0,8},{4,12},{8,0},{12,4},{1,9},{5,13},{9,1},{13,5},{2,10},{6,14},... | collective-permute-start | bytes 3080 | tf_op jit(solution)/shard_map/ppermute | solution.py:399
  26.0 5.5 %collective-permute-start.17 = (f32[16,16]{1,0:T(8,128)S(1)}, f32[16,16]{1,0:T(8,128)S(1)}, u32[]{:S(2)}, u32[]{:S(2)}) collective-permute-start(f32[16,16]{1,0:T(8,128)S(1)} %maximum_bitcast_fusion), channel_id=1, source_target_pairs={{0,12},{4,8},{8,4},{12,0},{1,13},{5,9},{9,5},{13,1},{2,14},{6,10},... | collective-permute-start | bytes 3080 | tf_op jit(solution)/shard_map/ppermute | solution.py:399
  26.2 10.9 %collective-permute-start.12 = (bf16[16,1024]{1,0:T(8,128)(2,1)S(1)}, bf16[16,1024]{1,0:T(8,128)(2,1)S(1)}, u32[]{:S(2)}, u32[]{:S(2)}) collective-permute-start(bf16[16,1024]{1,0:T(8,128)(2,1)S(1)} %add_convert_fusion.refs_1_), channel_id=1, source_target_pairs={{0,4},{4,0},{8,12},{12,8},{1,5},{5,1},{9,13},{13,9},{2,6},{6,2},{1... | collective-permute-start | bytes 98312 | tf_op jit(solution)/shard_map/ppermute | solution.py:399
  27.0 10.2 %collective-permute-start.13 = (bf16[16,1024]{1,0:T(8,128)(2,1)S(1)}, bf16[16,1024]{1,0:T(8,128)(2,1)S(1)}, u32[]{:S(2)}, u32[]{:S(2)}) collective-permute-start(bf16[16,1024]{1,0:T(8,128)(2,1)S(1)} %add_convert_fusion.refs_1_), channel_id=1, source_target_pairs={{0,8},{4,12},{8,0},{12,4},{1,9},{5,13},{9,1},{13,5},{2,10},{6,14},... | collective-permute-start | bytes 98312 | tf_op jit(solution)/shard_map/ppermute | solution.py:399
  30.5 6.7 %collective-permute-start.14 = (bf16[16,1024]{1,0:T(8,128)(2,1)S(1)}, bf16[16,1024]{1,0:T(8,128)(2,1)S(1)}, u32[]{:S(2)}, u32[]{:S(2)}) collective-permute-start(bf16[16,1024]{1,0:T(8,128)(2,1)S(1)} %add_convert_fusion.refs_1_), channel_id=1, source_target_pairs={{0,12},{4,8},{8,4},{12,0},{1,13},{5,9},{9,5},{13,1},{2,14},{6,10},... | collective-permute-start | bytes 98312 | tf_op jit(solution)/shard_map/ppermute | solution.py:399
  42.7 14.4 %collective-permute-start.20 = (bf16[208,256]{1,0:T(8,128)(2,1)S(1)}, bf16[208,256]{1,0:T(8,128)(2,1)S(1)}, u32[]{:S(2)}, u32[]{:S(2)}) collective-permute-start(bf16[208,256]{1,0:T(8,128)(2,1)S(1)} %get-tuple-element.159.refs_0_), channel_id=1, source_target_pairs={{0,2},{2,0},{1,3},{3,1},{4,6},{6,4},{5,7},{7,5},{8,10},{10,8},{9,1... | collective-permute-start | bytes 319496 | tf_op jit(solution)/shard_map/ppermute | solution.py:506
  49.3 8.9 %collective-permute-start.19 = (bf16[208,256]{1,0:T(8,128)(2,1)S(1)}, bf16[208,256]{1,0:T(8,128)(2,1)S(1)}, u32[]{:S(2)}, u32[]{:S(2)}) collective-permute-start(bf16[208,256]{1,0:T(8,128)(2,1)S(1)} %get-tuple-element.156.refs_0_), channel_id=1, source_target_pairs={{0,2},{2,0},{1,3},{3,1},{4,6},{6,4},{5,7},{7,5},{8,10},{10,8},{9,1... | collective-permute-start | bytes 319496 | tf_op jit(solution)/shard_map/ppermute | solution.py:506
  53.7 5.5 %collective-permute-start.18 = (bf16[208,256]{1,0:T(8,128)(2,1)S(1)}, bf16[208,256]{1,0:T(8,128)(2,1)S(1)}, u32[]{:S(2)}, u32[]{:S(2)}) collective-permute-start(bf16[208,256]{1,0:T(8,128)(2,1)S(1)} %gate_up_2.1.refs_0_), channel_id=1, source_target_pairs={{0,2},{2,0},{1,3},{3,1},{4,6},{6,4},{5,7},{7,5},{8,10},{10,8},{9,1... | collective-permute-start | bytes 319496 | tf_op jit(solution)/shard_map/ppermute | solution.py:506
  60.3 0.7 copy-start
  62.7 1.6 %collective-permute-start.21 = (f32[64,512]{1,0:T(8,128)}, f32[64,512]{1,0:T(8,128)S(1)}, u32[]{:S(2)}, u32[]{:S(2)}) collective-permute-start(f32[64,512]{1,0:T(8,128)} %get-tuple-element.161), channel_id=1, source_target_pairs={{0,1},{1,0},{2,3},{3,2},{4,5},{5,4},{6,7},{7,6},{8,9},{9,8},{10,11... | collective-permute-start | bytes 393224 | tf_op jit(solution)/shard_map/ppermute | solution.py:399
  62.8 9.1 %collective-permute-start.11 = (bf16[4,1024]{1,0:T(4,128)(2,1)S(1)}, bf16[4,1024]{1,0:T(4,128)(2,1)S(1)}, u32[]{:S(2)}, u32[]{:S(2)}) collective-permute-start(bf16[4,1024]{1,0:T(4,128)(2,1)S(1)} %get-tuple-element.197), channel_id=1, source_target_pairs={{0,2},{2,0},{1,3},{3,1},{4,6},{6,4},{5,7},{7,5},{8,10},{10,8},{9,1... | collective-permute-start | bytes 24584 | tf_op jit(solution)/shard_map/ppermute | solution.py:465
  64.3 0.7 copy-start.5
  66.6 6.0 %collective-permute-start.24 = (bf16[16,512]{1,0:T(8,128)(2,1)}, bf16[16,512]{1,0:T(8,128)(2,1)S(1)}, u32[]{:S(2)}, u32[]{:S(2)}) collective-permute-start(bf16[16,512]{1,0:T(8,128)(2,1)} %get-tuple-element.165), channel_id=1, source_target_pairs={{0,12},{4,8},{8,4},{12,0},{1,13},{5,9},{9,5},{13,1},{2,14},{6,10},... | collective-permute-start | bytes 49160 | tf_op jit(solution)/shard_map/ppermute | solution.py:399
  69.5 0.9 %copy-start.8 = (bf16[16,512]{1,0:T(8,128)(2,1)S(1)}, bf16[16,512]{1,0:T(8,128)(2,1)}, u32[]{:S(2)}) copy-start(bf16[16,512]{1,0:T(8,128)(2,1)} %get-tuple-element.164) | copy-start | bytes 49156
  69.5 0.9 %copy-start.7 = (bf16[16,512]{1,0:T(8,128)(2,1)S(1)}, bf16[16,512]{1,0:T(8,128)(2,1)}, u32[]{:S(2)}) copy-start(bf16[16,512]{1,0:T(8,128)(2,1)} %get-tuple-element.163) | copy-start | bytes 49156
  69.5 5.6 %copy-start.6 = (f32[16,512]{1,0:T(8,128)S(1)}, f32[16,512]{1,0:T(8,128)}, u32[]{:S(2)}) copy-start(f32[16,512]{1,0:T(8,128)} %get-tuple-element.162) | copy-start | bytes 98308
  70.3 4.7 %collective-permute-start.23 = (bf16[16,512]{1,0:T(8,128)(2,1)S(1)}, bf16[16,512]{1,0:T(8,128)(2,1)S(1)}, u32[]{:S(2)}, u32[]{:S(2)}) collective-permute-start(bf16[16,512]{1,0:T(8,128)(2,1)S(1)} %copy-done.8), channel_id=1, source_target_pairs={{0,8},{4,12},{8,0},{12,4},{1,9},{5,13},{9,1},{13,5},{2,10},{6,14},... | collective-permute-start | bytes 49160 | tf_op jit(solution)/shard_map/ppermute | solution.py:399
  70.4 4.6 %collective-permute-start.22 = (bf16[16,512]{1,0:T(8,128)(2,1)S(1)}, bf16[16,512]{1,0:T(8,128)(2,1)S(1)}, u32[]{:S(2)}, u32[]{:S(2)}) collective-permute-start(bf16[16,512]{1,0:T(8,128)(2,1)S(1)} %copy-done.7), channel_id=1, source_target_pairs={{0,4},{4,0},{8,12},{12,8},{1,5},{5,1},{9,13},{13,9},{2,6},{6,2},{1... | collective-permute-start | bytes 49160 | tf_op jit(solution)/shard_map/ppermute | solution.py:399

commit v3 on v2

v3 whole, which is shorter than its diff:
```python
import functools
import math

import jax
import jax.numpy as jnp
from jax import lax
from jax.experimental import pallas as pl
from jax.experimental.pallas import tpu as pltpu
from jax.sharding import PartitionSpec as P

HEAD_DIM = 128
KV_HEADS = 2
CHUNK = 128
FACT_LANES = 128

F32 = jnp.float32
BF16 = jnp.bfloat16


def dot_nt(a, b):
    return lax.dot_general(a, b, (((1,), (1,)), ((), ())), preferred_element_type=F32)


def dot_tn(a, b):
    return lax.dot_general(a, b, (((0,), (0,)), ((), ())), preferred_element_type=F32)


def dot_nn(a, b):
    return jnp.dot(a, b, preferred_element_type=F32)


def cost(microseconds):
    return pl.CostEstimate(
        flops=0, transcendentals=0, bytes_accessed=int(microseconds * 3_000_000)
    )


VMEM = pl.BlockSpec(memory_space=pltpu.VMEM)
SMEM = pl.BlockSpec(memory_space=pltpu.SMEM)
HBM = pl.BlockSpec(memory_space=pltpu.HBM)
ANY = pl.BlockSpec(memory_space=pl.ANY)


def in_hbm(value):
    return pltpu.with_memory_space_constraint(value, pltpu.HBM)


def position():
    tp, sub = lax.axis_index("tp"), lax.axis_index("sub")
    subs = lax.axis_size("sub")
    return tp * subs + sub, tp, sub, lax.axis_index("pool"), subs


def call(kernel, name, inputs, specs, outs, out_specs=None, scratch=(), loads=(), anchors=(), us=2, roomy=False, begins=False):
    count_in, count_out, count_load = len(inputs), len(outs), len(loads)

    def source(ref, first):
        return ref if first is None else ref.at[:, first : first + CHUNK, :]

    def run(*refs):
        refs = list(refs)
        given = [refs.pop(0) for _ in range(count_in)]
        sources = [refs.pop(0) for _ in range(count_load)]
        del refs[: len(anchors)]
        results = [refs.pop(0) for _ in range(count_out)]
        targets = [refs.pop(0) for _ in range(count_load)]
        copies = []
        if loads:
            sems = refs.pop()
            for i, (_, first) in enumerate(loads):
                copies.append(
                    pltpu.make_async_copy(source(sources[i], first), targets[i], sems.at[i])
                )

        def begin():
            if copies:

                @pl.when(lax.axis_index("tp") >= 0)
                def _():
                    for copy in copies:
                        copy.start()

        if begins:
            kernel(begin, *given, *results, *refs)
        else:
            begin()
            kernel(*given, *results, *refs)
        for copy in copies:
            copy.wait()

    def loaded(array, first):
        shape = array.shape if first is None else (array.shape[0], CHUNK, array.shape[2])
        return pltpu.VMEM(shape, array.dtype)

    if not roomy:
        outs = [
            leaf if spec is HBM else pltpu.VMEM(leaf.shape, leaf.dtype)
            for leaf, spec in zip(outs, out_specs or [VMEM] * count_out)
        ]
    scratch = list(scratch) + ([pltpu.SemaphoreType.DMA((count_load,))] if loads else [])
    results = pl.pallas_call(
        run,
        in_specs=list(specs) + [HBM] * count_load + [ANY] * len(anchors),
        out_specs=list(out_specs or [VMEM] * count_out) + [VMEM] * count_load,
        out_shape=list(outs) + [loaded(*leaf) for leaf in loads],
        scratch_shapes=scratch,
        compiler_params=pltpu.CompilerParams(vmem_limit_bytes=(48 if roomy else 12) << 20),
        cost_estimate=cost(us),
        name=name,
    )(*inputs, *[in_hbm(leaf[0]) for leaf in loads], *anchors)
    return list(results[:count_out]), list(results[count_out:])


def attention_kernel(
    begin, q_hbm, lengths_hbm, route_hbm, share_hbm, k_hbm, v_hbm, *refs, pieces
):
    where = position()
    outs, facts_ref = refs[:pieces], refs[pieces]
    lengths, q_ref, route_ref, share_ref, k_ref, v_ref, sems, spread, gathered, flat = refs[
        pieces + 1 :
    ]
    rows, heads, _ = gathered.shape
    positions = k_ref.shape[1]
    group = heads // KV_HEADS
    small = [
        pltpu.make_async_copy(q_hbm, q_ref, sems.at[rows, 0]),
        pltpu.make_async_copy(lengths_hbm, lengths, sems.at[rows, 1]),
        pltpu.make_async_copy(route_hbm, route_ref, sems.at[rows + 1, 0]),
        pltpu.make_async_copy(share_hbm, share_ref, sems.at[rows + 1, 1]),
    ]
    for copy in small:
        copy.start()
    copies = []
    for row in range(rows):
        pair = [
            pltpu.make_async_copy(k_hbm.at[row], k_ref.at[row], sems.at[row, 0]),
            pltpu.make_async_copy(v_hbm.at[row], v_ref.at[row], sems.at[row, 1]),
        ]
        pair[0].start()
        pair[1].start()
        copies.append(pair)
    begin()
    for copy in small:
        copy.wait()
    share = share_ref[...]
    high = share.astype(BF16).astype(F32)
    middle = (share - high).astype(BF16).astype(F32)
    block = jnp.concatenate([route_ref[...].astype(F32), high, middle, share - high - middle], axis=0)
    count, lanes = block.shape[1], facts_ref.shape[1]
    block = jnp.concatenate([block, jnp.zeros((block.shape[0], -count % 128), F32)], axis=1).T
    blank = jnp.zeros((count, lanes - block.shape[1]), F32)
    facts_ref[...] = jnp.concatenate([block[:count], blank], axis=1).astype(BF16)
    queries = q_ref[...].astype(F32)
    for h in range(heads):
        spread[:, h, :] = queries[:, h * HEAD_DIM : (h + 1) * HEAD_DIM]
    column = lax.broadcasted_iota(jnp.int32, (group, positions), 1)
    for row in range(rows):
        valid = column < lengths[row]
        copies[row][0].wait()
        copies[row][1].wait()
        for j in range(KV_HEADS):
            lanes = slice(j * HEAD_DIM, (j + 1) * HEAD_DIM)
            own = spread[row, j * group : (j + 1) * group, :].astype(BF16)
            scores = dot_nt(own, k_ref[row, :, lanes])
            scores = jnp.where(valid, scores * (1.0 / math.sqrt(HEAD_DIM)), -1e30)
            top = jnp.max(scores, axis=1, keepdims=True)
            terms = jnp.where(valid, jnp.exp(scores - top), 0.0)
            total = jnp.sum(terms, axis=1, keepdims=True)
            value = dot_nn(terms.astype(BF16), v_ref[row, :, lanes]) / total
            gathered[row, j * group : (j + 1) * group, :] = value
    for h in range(heads):
        flat[:, h * HEAD_DIM : (h + 1) * HEAD_DIM] = gathered[:, h, :]
    width = heads * HEAD_DIM // pieces
    for k in range(pieces):
        start = pl.multiple_of(((where[0] ^ k) if pieces > 1 else 0) * width, width)
        outs[k][...] = flat[:, pl.ds(start, width)].astype(BF16)


def attend(queries, keys_cache, values_cache, lengths, facts, pieces, loads, roomy):
    rows, columns = queries.shape
    heads = columns // HEAD_DIM
    return call(
        functools.partial(attention_kernel, pieces=pieces),
        "attention",
        [in_hbm(a) for a in (queries, lengths, *facts, keys_cache, values_cache)],
        [HBM] * 6,
        [jax.ShapeDtypeStruct((rows, columns // pieces), BF16)] * pieces
        + [jax.ShapeDtypeStruct((facts[0].shape[1], FACT_LANES), BF16)],
        scratch=[
            pltpu.SMEM((rows,), jnp.int32),
            pltpu.VMEM(queries.shape, BF16),
            pltpu.VMEM(facts[0].shape, jnp.int32),
            pltpu.VMEM(facts[1].shape, F32),
            pltpu.VMEM(keys_cache.shape, BF16),
            pltpu.VMEM(values_cache.shape, BF16),
            pltpu.SemaphoreType.DMA((rows + 2, 2)),
            pltpu.VMEM((rows, heads, HEAD_DIM), F32),
            pltpu.VMEM((rows, heads, HEAD_DIM), F32),
            pltpu.VMEM((rows, columns), F32),
        ],
        loads=loads,
        us=4,
        roomy=roomy,
        begins=True,
    )


def route_kernel(table_ref, *refs, sources, experts, top):
    where = position()
    given, (slot_ref, weight_ref, largest_ref, *picks, held) = refs[:sources], refs[sources:]
    pools, pool_rows, lanes = held.shape
    if sources == 1:
        held[...] = given[0][...].astype(F32)
    else:
        for k in range(sources):
            width = given[k].shape[1]
            held[where[3] ^ where[0] ^ k] = given[k][:, width - lanes :].astype(F32)
    rows = pools * pool_rows
    total = table_ref.shape[1]
    groups, _, lanes = slot_ref.shape
    group = lanes // rows
    facts = held[...].reshape(rows, held.shape[2]).T
    shares = facts[top : 2 * top] + facts[2 * top : 3 * top] + facts[3 * top : 4 * top]
    routes = jnp.concatenate([facts[i : i + 1] for i in range(top)], axis=1).astype(jnp.int32)
    ids = lax.broadcasted_iota(jnp.int32, (total, top * rows), 0)
    hot = jnp.where(ids == routes, 1.0, 0.0).astype(BF16)
    table = jnp.broadcast_to(table_ref[...].astype(F32), (8, total)).astype(BF16)
    entry = dot_nn(table, hot)[0:1].astype(jnp.int32)

    first = lax.broadcasted_iota(jnp.int32, (pools, top * rows), 0) * experts
    inside = jnp.where((entry >= first) & (entry < first + experts), 1.0, 0.0)
    loads = jnp.sum(inside, axis=1, keepdims=True)
    largest_ref[...] = jnp.max(loads, axis=0, keepdims=True).astype(jnp.int32)

    lane = lax.broadcasted_iota(jnp.int32, (groups, lanes), 1)
    block = lax.broadcasted_iota(jnp.int32, (groups, lanes), 0)
    wanted = where[3] * experts + block * group + lane // rows
    weight = jnp.zeros((groups, lanes), F32)
    mask = jnp.zeros((groups, lanes), F32)
    for i in range(top):
        named = jnp.concatenate([entry[:, i * rows : (i + 1) * rows]] * group, axis=1)
        value = jnp.concatenate([shares[i : i + 1]] * group, axis=1)
        match = wanted == named
        mask = mask + jnp.where(match, 1.0, 0.0)
        weight = weight + jnp.where(match, value, 0.0)
    earlier = lax.broadcasted_iota(jnp.int32, (lanes, lanes), 0)
    later = lax.broadcasted_iota(jnp.int32, (lanes, lanes), 1)
    before = jnp.where(earlier < later, 1.0, 0.0).astype(BF16)
    rank = dot_nn(mask.astype(BF16), before)
    base = jnp.zeros((1, 1), F32)
    counts = jnp.sum(mask, axis=1, keepdims=True)
    slots = []
    for g in range(groups):
        slots.append(jnp.where(mask[g : g + 1] > 0.0, rank[g : g + 1] + base, -1.0))
        slot_ref[g] = slots[g].astype(jnp.int32)
        weight_ref[g] = weight[g : g + 1]
        base = base + counts[g : g + 1]
    fill_picks(slots, [weight[g : g + 1] for g in range(groups)], *picks)


def fill_picks(slots, weights, pick_ref, spread_ref, slot_weight_ref):
    groups, lanes = len(slots), slots[0].shape[1]
    capacity = pick_ref.shape[0]
    rows = jnp.concatenate(slots + [slots[0]] * (-groups % 8), axis=0).T
    place = lax.broadcasted_iota(jnp.int32, (capacity, lanes), 0).astype(F32)
    along = lax.broadcasted_iota(jnp.int32, (lanes, capacity), 1).astype(F32)
    total = jnp.zeros((capacity, lanes), F32)
    for g in range(groups):
        hit = place == slots[g]
        part = slice(g * lanes, (g + 1) * lanes)
        pick_ref[:, part] = jnp.where(hit, 1.0, 0.0).astype(BF16)
        spread_ref[part, :] = jnp.where(along == rows[:, g : g + 1], 1.0, 0.0).astype(BF16)
        total = total + jnp.where(hit, weights[g], 0.0)
    slot_weight_ref[...] = jnp.sum(total, axis=1, keepdims=True)


def pick_shapes(capacity, pairs):
    return [
        jax.ShapeDtypeStruct((capacity, pairs), BF16),
        jax.ShapeDtypeStruct((pairs, capacity), BF16),
        jax.ShapeDtypeStruct((capacity, 1), F32),
    ]


def route(blocks, expert_table, experts, rows, top, capacity, pools, loads, roomy):
    group = max(1, min(experts, 256 // rows))
    shape = (experts // group, 1, group * rows)
    results, held = call(
        functools.partial(route_kernel, sources=len(blocks), experts=experts, top=top),
        "route",
        [expert_table.reshape(1, -1), *blocks],
        [VMEM] + [VMEM] * len(blocks),
        [
            jax.ShapeDtypeStruct(shape, jnp.int32),
            jax.ShapeDtypeStruct(shape, F32),
            jax.ShapeDtypeStruct((1, 1), jnp.int32),
            *pick_shapes(capacity, experts * rows),
        ],
        scratch=[pltpu.VMEM((pools, rows // pools, FACT_LANES), F32)],
        loads=loads,
        us=6,
        roomy=roomy,
    )
    return results[:3], results[3:], held


def pick_slots(shift, slots, weights, capacity):
    def kernel(shift_ref, *refs):
        slot_ref, weight_ref, *picks = refs
        groups = range(slot_ref.shape[0])
        shifted = [(slot_ref[g] - shift_ref[0]).astype(F32) for g in groups]
        fill_picks(shifted, [weight_ref[g] for g in groups], *picks)

    return call(
        kernel,
        "pick",
        [shift.reshape(1), slots, weights],
        [SMEM, VMEM, VMEM],
        pick_shapes(capacity, slots.shape[0] * slots.shape[2]),
        roomy=True,
    )[0]


def project_kernel(*refs, sources):
    where = position()
    inputs, (own_ref, sent_ref, w_ref) = refs[:sources], refs[sources : sources + 3]
    kept, near, far, held = refs[sources + 3 :]
    own_rows = inputs[0].shape[0]
    count = sources * own_rows
    half = kept.shape[1]
    facts = jnp.where(where[0] == 0, own_ref[...].astype(F32), sent_ref[...].astype(F32))
    facts = facts.astype(BF16)
    held[...] = facts
    stacked = jnp.concatenate([ref[...].astype(F32) for ref in inputs], axis=0).astype(BF16)
    target = lax.broadcasted_iota(jnp.int32, (count, count), 0)
    origin = lax.broadcasted_iota(jnp.int32, (count, count), 1)
    order = (target ^ (where[0] * own_rows)) == origin
    x = dot_nn(jnp.where(order, 1.0, 0.0).astype(BF16), stacked).astype(BF16)
    for k, out in ((1, far), (0, near)):
        start = pl.multiple_of((where[1] ^ k) * half, half)
        value = dot_nn(x, w_ref[:, pl.ds(start, half)])
        out[:, :half] = value.astype(BF16)
        out[:, half:] = facts
        if k == 0:
            kept[...] = value


def project(inputs, facts, out_weight, loads, anchors):
    sources = len(inputs)
    count, half = sources * inputs[0].shape[0], out_weight.shape[1] // 2
    sent = jax.ShapeDtypeStruct((count, half + FACT_LANES), BF16)
    return call(
        functools.partial(project_kernel, sources=sources),
        "project",
        [*inputs, *facts, out_weight],
        [VMEM] * (sources + 3),
        [
            jax.ShapeDtypeStruct((count, half), F32),
            sent,
            sent,
            jax.ShapeDtypeStruct((count, FACT_LANES), BF16),
        ],
        loads=loads,
        anchors=anchors,
    )


def gate_up_kernel(*refs, sources, first):
    where = position()
    inputs, refs = refs[:sources], refs[sources:]
    pick_ref, g_ref, u_ref, out_ref = refs[:4]
    if first:
        columns_ref, mine_ref, theirs_ref, x, both = refs[4:]
        count = inputs[0].shape[0]
        own_rows = mine_ref.shape[0]
        row = lax.broadcasted_iota(jnp.int32, (own_rows, count), 0)
        place = lax.broadcasted_iota(jnp.int32, (own_rows, count), 1)
        for out, shard in ((mine_ref, where[0]), (theirs_ref, where[0] ^ where[4])):
            chosen = jnp.where(place == row + shard * own_rows, 1.0, 0.0).astype(BF16)
            out[...] = dot_nn(chosen, inputs[0][...]).astype(BF16)
        for k in range(sources):
            start = pl.multiple_of((where[3] ^ k) * count, count) if sources > 1 else 0
            x[pl.ds(start, count), :] = inputs[k][...].astype(F32)
        columns_ref[...] = x[...].T.astype(BF16)
    else:
        (columns_ref,), (both,) = inputs, refs[4:]
    experts, _, depth = g_ref.shape
    rows = columns_ref.shape[1]
    for base, w_ref in ((0, g_ref), (CHUNK, u_ref)):
        value = dot_nn(w_ref[...].reshape(experts * CHUNK, depth), columns_ref[...]).astype(BF16)
        for e in range(experts):
            both[base : base + CHUNK, e * rows : (e + 1) * rows] = value[
                e * CHUNK : (e + 1) * CHUNK
            ]
    out_ref[...] = dot_nt(pick_ref[...], both[...]).astype(BF16)


def gate_up(xs, pick, w_gate, w_up, index, own_rows, loads, roomy, anchors=()):
    first = index == 0
    experts, _, depth = w_gate.shape
    rows = pick.shape[1] // experts
    outs = [jax.ShapeDtypeStruct((pick.shape[0], 2 * CHUNK), BF16)]
    scratch = [pltpu.VMEM((2 * CHUNK, experts * rows), BF16)]
    if first:
        outs.append(jax.ShapeDtypeStruct((depth, rows), BF16))
        outs += [jax.ShapeDtypeStruct((own_rows, depth), BF16)] * 2
        scratch.insert(0, pltpu.VMEM((rows, depth), F32))
    results, held = call(
        functools.partial(gate_up_kernel, sources=len(xs), first=first),
        f"gate_up_{index}",
        [*xs, pick, w_gate, w_up],
        [VMEM] * (len(xs) + 3),
        outs,
        scratch=scratch,
        loads=loads,
        anchors=anchors,
        us=4,
        roomy=roomy,
    )
    return results[0], results[1:2] if first else xs, results[2:], held


def down_kernel(own_ref, other_ref, weight_ref, spread_ref, d_ref, *refs, carried):
    before, outs = refs[:carried], refs[carried:]
    experts, _, depth = d_ref.shape
    rows = spread_ref.shape[0] // experts
    both = own_ref[...].astype(F32) + other_ref[...].astype(F32)
    gate, up = both[:, :CHUNK], both[:, CHUNK:]
    hidden = (gate / (1.0 + jnp.exp(-gate)) * up * weight_ref[...]).astype(BF16)
    spread = dot_nn(spread_ref[...], hidden).astype(BF16)
    left = jnp.concatenate([spread[e * rows : (e + 1) * rows] for e in range(experts)], axis=1)
    total = dot_nn(left, d_ref[...].reshape(experts * CHUNK, depth))
    if carried:
        total = total + before[0][...]
    if len(outs) == 1:
        outs[0][...] = total
    else:
        half = depth // 2
        low, high = total[:, :half], total[:, half:]
        mine = lax.axis_index("sub") == 0
        outs[0][...] = jnp.where(mine, low, high)
        outs[1][...] = jnp.where(mine, high, low)


def down(own, other, slot_weight, spread, w_down, before, index, halved, roomy):
    experts, _, depth = w_down.shape
    rows = spread.shape[0] // experts
    carried = [] if before is None else [before]
    parts = 2 if halved else 1
    return call(
        functools.partial(down_kernel, carried=len(carried)),
        f"down_{index}",
        [own, other, slot_weight, spread, w_down, *carried],
        [VMEM] * (5 + len(carried)),
        [jax.ShapeDtypeStruct((rows, depth // parts), F32)] * parts,
        us=3,
        roomy=roomy,
    )[0]


def load(loads, anchors, name, roomy=False):
    return call(
        lambda: None, name, [], [], [], loads=loads, anchors=anchors, us=2 * len(loads), roomy=roomy
    )[1]


def arrange_kernel(*refs):
    inputs, out_ref = refs[:-1], refs[-1]
    count = inputs[0].shape[0]
    for k, ref in enumerate(inputs):
        start = pl.multiple_of((lax.axis_index("pool") ^ k) * count, count)
        out_ref[pl.ds(start, count), :] = ref[...]


def arrange(blocks):
    shape = (len(blocks) * blocks[0].shape[0], blocks[0].shape[1])
    outs = [jax.ShapeDtypeStruct(shape, BF16)]
    return call(arrange_kernel, "arrange", blocks, [VMEM] * len(blocks), outs, roomy=True)[0][0]


def halves_kernel(value_ref, own_ref, other_ref):
    half = own_ref.shape[1]
    low, high = value_ref[:, :half], value_ref[:, half:]
    mine = lax.axis_index("sub") == 0
    own_ref[...] = jnp.where(mine, low, high)
    other_ref[...] = jnp.where(mine, high, low)


def halves(value):
    outs = [jax.ShapeDtypeStruct((value.shape[0], value.shape[1] // 2), F32)] * 2
    return call(halves_kernel, "halves", [value], [VMEM], outs, roomy=True)[0]


def join_kernel(mine_ref, theirs_ref, out_hbm, out_ref, sem):
    half = mine_ref.shape[1]
    low = lax.axis_index("tp") == 0
    mine, theirs = mine_ref[...].astype(F32), theirs_ref[...].astype(F32)
    out_ref[:, :half] = jnp.where(low, mine, theirs).astype(BF16)
    out_ref[:, half:] = jnp.where(low, theirs, mine).astype(BF16)
    copy = pltpu.make_async_copy(out_ref, out_hbm, sem)
    copy.start()
    copy.wait()


def join(mine, theirs):
    shape = (mine.shape[0], 2 * mine.shape[1])
    return call(
        join_kernel,
        "join",
        [mine, theirs],
        [VMEM, VMEM],
        [jax.ShapeDtypeStruct(shape, BF16)],
        out_specs=[HBM],
        scratch=[pltpu.VMEM(shape, BF16), pltpu.SemaphoreType.DMA],
    )[0][0]


def split_kernel(own_ref, other_ref, *outs):
    count = outs[0].shape[0]
    pool = lax.axis_index("pool")
    for k in range(len(outs)):
        row = pl.ds(pl.multiple_of((pool ^ k) * count, count), count)
        outs[k][...] = (own_ref[row, :] + other_ref[row, :]).astype(outs[k].dtype)


def split(own, other, pieces):
    shape = (own.shape[0] // pieces, own.shape[1])
    return call(
        split_kernel,
        "split",
        [own, other],
        [VMEM, VMEM],
        [jax.ShapeDtypeStruct(shape, F32 if k == 0 else BF16) for k in range(pieces)],
    )[0]


def xor_permute(value, axes, count, k):
    return lax.ppermute(value, axes, [(i, i ^ k) for i in range(count)])


def body(
    queries,
    keys_cache,
    values_cache,
    lengths,
    out_weight,
    routes,
    route_weight,
    expert_table,
    w_gate,
    w_up,
    w_down,
):
    pools, tps, subs = lax.axis_size("pool"), lax.axis_size("tp"), lax.axis_size("sub")
    pool, tp, sub = lax.axis_index("pool"), lax.axis_index("tp"), lax.axis_index("sub")
    shards = tps * subs
    shard = tp * subs + sub
    direct = tps == 2 and subs == 2 and pools == 4
    own_rows = queries.shape[0]
    pool_rows = own_rows * shards
    rows = pool_rows * pools
    experts, hidden_units, half_width = w_gate.shape
    top = routes.shape[1]

    capacity = -(-rows * top * 13 // (8 * pools * 16)) * 16
    gates, ups, downs = [
        [(w, c) for c in range(0, hidden_units, CHUNK)] for w in (w_gate, w_up, w_down)
    ]
    chunks = len(gates)

    if direct:
        axes = ("tp", "sub")
        (*pieces, facts), (out_held, gate_0, up_0) = attend(
            queries,
            keys_cache,
            values_cache,
            lengths,
            (routes.T, route_weight.T),
            shards,
            [(out_weight, None), gates[0], ups[0]],
            False,
        )
        inputs = [pieces[0]] + [xor_permute(pieces[k], axes, shards, k) for k in range(1, shards)]
        pairs = [(i, i ^ (shards * (i % shards))) for i in range(pools * shards) if i % shards]
        other_facts = lax.ppermute(facts, ("pool", "tp", "sub"), pairs)
        gate_1, up_1 = load([gates[1], ups[1]], [pieces[0]], "load_a")
        (kept, near, far, block), (gate_2,) = project(
            inputs, [facts, other_facts], out_held, [gates[2]], [gate_1]
        )
        up_2, down_0 = load([ups[2], downs[0]], [near], "load_b")
        x_sum, blocks = kept, [block]
        for k in range(1, shards):
            blocks.append(xor_permute(near if k < subs else far, axes, shards, k))
            x_sum = x_sum + blocks[k][:, :half_width].astype(F32)
        x_half, up_2 = lax.optimization_barrier((x_sum.astype(BF16), up_2))
        xs = [x_half] + [xor_permute(x_half, "pool", pools, k) for k in range(1, pools)]
        blocks, _ = lax.optimization_barrier((blocks, x_half))
        (slots, weights, largest), (pick, spread, slot_weight), (down_1, down_2) = route(
            blocks,
            expert_table,
            experts,
            rows,
            top,
            capacity,
            pools,
            downs[1:3],
            False,
        )
        held = [(gate_0, up_0), (gate_1, up_1), (gate_2, up_2)]
        held_down, sent, given = [down_0, down_1, down_2], [], xs
        for c in range(chunks):
            value, given, rest, _ = gate_up(
                given, pick, *held[c], c, own_rows, [], False, sent[-1:]
            )
            if c == 0:
                mine, theirs = rest
            sent.append(value)
        theirs, _ = lax.optimization_barrier((theirs, sent[-1]))
        theirs = lax.ppermute(theirs, "tp", [(0, 1), (1, 0)])
    else:
        (attention, facts), _ = attend(
            queries,
            keys_cache,
            values_cache,
            lengths,
            (routes.T, route_weight.T),
            1,
            [],
            True,
        )
        blocks = lax.all_gather(facts, "pool", axis=0)
        (slots, weights, largest), (pick, spread, slot_weight), _ = route(
            [blocks], expert_table, experts, rows, top, capacity, pools, [], True
        )
        head_rows = lax.all_to_all(
            attention, ("tp", "sub"), split_axis=1, concat_axis=0, tiled=True
        )
        partial = jnp.dot(head_rows, out_weight, preferred_element_type=F32)
        x_sum = lax.psum_scatter(partial, ("tp", "sub"), scatter_dimension=1, tiled=True)
        x_pool = x_sum.astype(BF16)
        attended = lax.all_to_all(x_pool, ("tp", "sub"), split_axis=0, concat_axis=1, tiled=True)
        x_part = lax.all_gather(x_pool, "pool", axis=0, tiled=True)
        xs = [lax.all_gather(x_part, "sub", axis=1, tiled=True)]
        held = load(gates + ups + downs, [], "load")
        held_down, sent, given = held[2 * chunks :], [], xs
        for c in range(chunks):
            value, given, *_ = gate_up(
                given, pick, held[c], held[chunks + c], c, own_rows, [], True
            )
            sent.append(value)

    def exchange(value):
        if tps == 2:
            return value, lax.ppermute(value, "tp", [(0, 1), (1, 0)])
        return lax.psum(value.astype(F32), "tp").astype(BF16), jnp.zeros_like(value)

    def combine(halved, extra=None):
        if not direct:
            value = lax.psum_scatter(halved[0], "pool", scatter_dimension=0, tiled=True)
            return lax.psum_scatter(value, "sub", scatter_dimension=1, tiled=True)
        own, other = halved
        received = xor_permute(other, "sub", subs, 1)
        if extra is not None:
            received, extra = lax.optimization_barrier((received, extra))
        pieces = split(own, received, pools)
        total = pieces[0]
        for k in range(1, pools):
            total = total + xor_permute(pieces[k], "pool", pools, k).astype(F32)
        return total if extra is None else total + extra

    def more(state):
        k, total = state
        k, *held_x = lax.optimization_barrier((k, *xs))
        x = arrange(held_x) if direct else held_x[0]
        pick, spread, slot_weight = pick_slots(k * capacity, slots, weights, capacity)
        gate = jnp.einsum("rd,efd->erf", x, w_gate, preferred_element_type=F32)
        up = jnp.einsum("rd,efd->erf", x, w_up, preferred_element_type=F32)
        both = jnp.concatenate([gate, up], axis=2).astype(BF16)
        both = both.reshape(experts * rows, 2 * hidden_units)
        sent = jnp.dot(pick, both, preferred_element_type=F32).astype(BF16)
        if tps == 2:
            both = sent.astype(F32) + lax.ppermute(sent, "tp", [(0, 1), (1, 0)]).astype(F32)
        else:
            both = lax.psum(sent.astype(F32), "tp")
        hidden = jax.nn.silu(both[:, :hidden_units]) * both[:, hidden_units:] * slot_weight
        spread = jnp.dot(spread, hidden.astype(BF16), preferred_element_type=F32).astype(BF16)
        spread = spread.reshape(experts, rows, hidden_units)
        value = jnp.einsum("erf,efd->rd", spread, w_down, preferred_element_type=F32)
        value = halves(value) if direct else [value]
        return k + 1, total + combine(value)

    both = [exchange(value) for value in sent]
    result = [None]
    for c in range(chunks):
        last = direct and c == chunks - 1
        result = down(
            *both[c], slot_weight, spread, held_down[c], result[0], c, last, not direct
        )
    if direct:
        theirs, largest, *result = lax.optimization_barrier((theirs, largest, *result))
        attended = join(mine, theirs)
    _, extra = lax.while_loop(
        lambda state: state[0] * capacity < largest[0, 0],
        more,
        (jnp.minimum(largest[0, 0], 1), jnp.zeros((pool_rows, half_width // subs), F32)),
    )
    if direct:
        return attended, combine(result, extra).astype(BF16)
    return attended, (combine(result) + extra).astype(BF16)


def solution(mesh):
    in_specs = (
        P(("grp", "pool", "tp", "sub"), None),
        P(("grp", "pool", "tp", "sub"), None, None),
        P(("grp", "pool", "tp", "sub"), None, None),
        P(("grp", "pool", "tp", "sub")),
        P(("tp", "sub"), None),
        P(("grp", "pool"), None),
        P(("grp", "pool"), None),
        P(),
        P("pool", "sub", "tp"),
        P("pool", "sub", "tp"),
        P("pool", "sub", "tp"),
    )
    out_specs = (P(("grp", "pool", "tp", "sub"), None), P(("grp", "pool"), ("tp", "sub")))
    return jax.shard_map(body, mesh=mesh, in_specs=in_specs, out_specs=out_specs, check_vma=False)
```

time: 76.3 us -> 61.6 us (0.81)
  Pallas kernels: 41.1 us -> 31.7 us
  local copies, waits for them, and re-layouts: 2.79 us -> 0.01 us
  other arithmetic: 2.72 us -> 0.64 us
  waiting for transfers between devices: 4.6 us -> 3.29 us
  starting transfers between devices: 22.7 us -> 23.5 us
    pallas_call x13, Pallas kernels: 37.8 us -> 31.7 us  [call(): pl.pallas_call(run, in_specs=list(specs) + [HBM] * count_load + [ANY] * l...]
    pallas_call x2 -> x0, Pallas kernels: 3.31 us -> none  [the longest x1 1.69 us: halves(): pl.pallas_call(halves_kernel, in_specs=[pl.BlockSpec(memory_space=pltpu.S...]
    unnamed x15 -> x2, local copies, waits for them, and re-layouts: 2.77 us -> 0.01 us
    ppermute x16 -> x13, waiting for transfers between devices: 4.59 us -> 2.76 us  [xor_permute(): return lax.ppermute(value, axes, [(i, i ^ k) for i in range(count)])]
    ppermute x16 -> x13, starting transfers between devices: 18.4 us -> 18.6 us  [xor_permute(): return lax.ppermute(value, axes, [(i, i ^ k) for i in range(count)])]
  transfers between devices with their start and end apart: 20 -> 18, of which waited for: 4 -> 2; matrix products, arithmetic and copies ran while one was open for 1% -> 0% of each run, Pallas kernels for 33% -> 33%
where the time goes in v3:
time: 61.6 us; the launch traced here: 61.4 us
  Pallas kernels  31.7 us (51%)
  starting transfers between devices  23.5 us (38%)
  waiting for transfers between devices  3.29 us (5%)
  between operations  1.55 us (3%)
  loops' own time  0.84 us (1%)
  other arithmetic  0.64 us (1%)
    pallas_call x13, Pallas kernels, call(): pl.pallas_call(run, in_specs=list(specs) + [HBM] * count_load + [ANY] * l...  31.7 us
    ppermute x13, starting transfers between devices, xor_permute(): return lax.ppermute(value, axes, [(i, i ^ k) for i in range(count)])  18.6 us
    ppermute x3, starting transfers between devices, exchange(): return (value, lax.ppermute(value, 'tp', [(0, 1), (1, 0)]))  3.86 us
    ppermute x13, waiting for transfers between devices, xor_permute(): return lax.ppermute(value, axes, [(i, i ^ k) for i in range(count)])  2.76 us
  transfers between devices with their start and end apart: 18, of which 2 were waited for; matrix products, arithmetic and copies ran while one was open for 0% of the time, Pallas kernels for 33%

profile of v3, /device:TPU:0, one launch (start us, length us, event | category | flops | bytes accessed | tf_op | source)
XLA Modules:
  0.0 61.4 jit_solution(4992479096748887717)
XLA Ops:
  0.6 5.4 %attention.1 = (bf16[4,1024]{1,0:T(4,128)(2,1)S(1)}, bf16[4,1024]{1,0:T(4,128)(2,1)S(1)}, bf16[4,1024]{1,0:T(4,128)(2,1)S(1)}, bf16[4,1024]{1,0:T(4,128)(2,1)S(1...) custom-call(bf16[4,4096]{1,0:T(4,128)(2,1)} %refs_0_.3, ...), custom_call_target="tpu_custom_call" | custom-call | bytes 12000000 | tf_op jit(solution)/shard_map/attention/pallas_call | solution.py:101
  6.1 0.5 collective-permute-start.5
  6.6 2.6 %collective-permute-start.6 = (bf16[4,1024]{1,0:T(4,128)(2,1)S(1)}, bf16[4,1024]{1,0:T(4,128)(2,1)S(1)}, u32[]{:S(2)}, u32[]{:S(2)}) collective-permute-start(bf16[4,1024]{1,0:T(4,128)(2,1)S(1)} %get-tuple-element.129), channel_id=1, source_target_pairs={{0,2},{1,3},{2,0},{3,1},{4,6},{5,7},{6,4},{7,5},{8,10},{9,11},{10,... | collective-permute-start | bytes 24584 | tf_op jit(solution)/shard_map/ppermute | solution.py:538
  9.2 0.1 collective-permute-start.7
  9.2 0.6 %collective-permute-start.8 = (bf16[16,128]{1,0:T(8,128)(2,1)S(1)}, bf16[16,128]{1,0:T(8,128)(2,1)S(1)}, u32[]{:S(2)}, u32[]{:S(2)}) collective-permute-start(bf16[16,128]{1,0:T(8,128)(2,1)S(1)} %get-tuple-element.131.refs_4_), channel_id=1, source_target_pairs={{1,5},{2,10},{3,15},{5,1},{6,14},{7,11},{9,13},{10,2},{11,7},{13,9... | collective-permute-start | bytes 12296 | tf_op jit(solution)/shard_map/ppermute | solution.py:585
  9.9 3.5 %load_a.1 = (bf16[16,128,1024]{2,1,0:T(8,128)(2,1)S(1)}, bf16[16,128,1024]{2,1,0:T(8,128)(2,1)S(1)}) custom-call(bf16[16,384,1024]{2,1,0:T(8,128)(2,1)} %refs_7_.3, bf16[16,384,1024]{2,1,0:T(8,128)(2,1)} %refs_0_.5, bf16[4,1024]{1,0:T(4,128)(2,1)S(1)} %get-tuple-element.127.refs_2_.refs_0_), custom_call_target="tpu_custom_call" | custom-call | bytes 12000000 | tf_op jit(solution)/shard_map/load_a/pallas_call | solution.py:101
  13.4 0.0 collective-permute-done.8.refs_5_
  13.4 0.0 collective-permute-done.5.refs_1_
  13.4 0.0 collective-permute-done.6.refs_2_
  13.4 0.0 collective-permute-done.7.refs_3_
  13.4 2.7 %project.1 = (f32[16,1024]{1,0:T(8,128)S(1)}, bf16[16,1152]{1,0:T(8,128)(2,1)S(1)}, bf16[16,1152]{1,0:T(8,128)(2,1)S(1)}, bf16[16,128]{1,0:T(8,128)(2,1)S(1)}, bf16[16,128,1024]{2,1,0:T(8,128)(2,1)S(1)}) custom-call(bf16[4,1024]{1,0:T(4,128)(2,1)S(1)} %get-tuple-element.127.refs_2_.refs_0_, bf16[4,1024]{1,0:T(4,128)(2,1)S(1)} %collective-permute-done.5.refs_1_, ...), custom_call_target="tpu_custom_call" | custom-call | bytes 6000000 | tf_op jit(solution)/shard_map/project/pallas_call | solution.py:101
  16.1 5.6 %collective-permute-start.10 = (bf16[16,1152]{1,0:T(8,128)(2,1)S(1)}, bf16[16,1152]{1,0:T(8,128)(2,1)S(1)}, u32[]{:S(2)}, u32[]{:S(2)}) collective-permute-start(bf16[16,1152]{1,0:T(8,128)(2,1)S(1)} %get-tuple-element.136), channel_id=1, source_target_pairs={{0,2},{1,3},{2,0},{3,1},{4,6},{5,7},{6,4},{7,5},{8,10},{9,11},{10,... | collective-permute-start | bytes 110600 | tf_op jit(solution)/shard_map/ppermute | solution.py:538
  21.8 0.8 %collective-permute-start.11 = (bf16[16,1152]{1,0:T(8,128)(2,1)S(1)}, bf16[16,1152]{1,0:T(8,128)(2,1)S(1)}, u32[]{:S(2)}, u32[]{:S(2)}) collective-permute-start(bf16[16,1152]{1,0:T(8,128)(2,1)S(1)} %get-tuple-element.136), channel_id=1, source_target_pairs={{0,3},{1,2},{2,1},{3,0},{4,7},{5,6},{6,5},{7,4},{8,11},{9,10},{10,... | collective-permute-start | bytes 110600 | tf_op jit(solution)/shard_map/ppermute | solution.py:538
  22.5 0.0 copy-start
  22.5 0.0 collective-permute-start.9
  22.6 3.5 %load_b.1 = (bf16[16,128,1024]{2,1,0:T(8,128)(2,1)S(1)}, bf16[16,128,1024]{2,1,0:T(8,128)(2,1)S(1)}) custom-call(bf16[16,384,1024]{2,1,0:T(8,128)(2,1)} %refs_0_.5, bf16[16,384,1024]{2,1,0:T(8,128)(2,1)} %refs_6_.3, bf16[16,1152]{1,0:T(8,128)(2,1)S(1)} %get-tuple-element.135.refs_2_), custom_call_target="tpu_custom_call" | custom-call | bytes 12000000 | tf_op jit(solution)/shard_map/load_b/pallas_call | solution.py:101
  26.1 0.0 collective-permute-done.10.refs_3_
  26.1 0.0 collective-permute-done.11.refs_4_
  26.1 0.0 collective-permute-done.9.refs_2_
  26.1 1.0 %collective-permute-start.12 = (bf16[16,1024]{1,0:T(8,128)(2,1)S(1)}, bf16[16,1024]{1,0:T(8,128)(2,1)S(1)}, u32[]{:S(2)}, u32[]{:S(2)}) collective-permute-start(bf16[16,1024]{1,0:T(8,128)(2,1)S(1)} %add_convert_fusion.refs_0_), channel_id=1, source_target_pairs={{0,4},{4,0},{8,12},{12,8},{1,5},{5,1},{9,13},{13,9},{2,6},{6,2},{1... | collective-permute-start | bytes 98312 | tf_op jit(solution)/shard_map/ppermute | solution.py:538
  27.1 1.0 %collective-permute-start.13 = (bf16[16,1024]{1,0:T(8,128)(2,1)S(1)}, bf16[16,1024]{1,0:T(8,128)(2,1)S(1)}, u32[]{:S(2)}, u32[]{:S(2)}) collective-permute-start(bf16[16,1024]{1,0:T(8,128)(2,1)S(1)} %add_convert_fusion.refs_0_), channel_id=1, source_target_pairs={{0,8},{4,12},{8,0},{12,4},{1,9},{5,13},{9,1},{13,5},{2,10},{6,14},... | collective-permute-start | bytes 98312 | tf_op jit(solution)/shard_map/ppermute | solution.py:538
  28.2 2.4 %collective-permute-start.14 = (bf16[16,1024]{1,0:T(8,128)(2,1)S(1)}, bf16[16,1024]{1,0:T(8,128)(2,1)S(1)}, u32[]{:S(2)}, u32[]{:S(2)}) collective-permute-start(bf16[16,1024]{1,0:T(8,128)(2,1)S(1)} %add_convert_fusion.refs_0_), channel_id=1, source_target_pairs={{0,12},{4,8},{8,4},{12,0},{1,13},{5,9},{9,5},{13,1},{2,14},{6,10},... | collective-permute-start | bytes 98312 | tf_op jit(solution)/shard_map/ppermute | solution.py:538
  30.6 0.0 copy-done
  30.6 4.0 %route.1 = (s32[4,1,256]{2,1,0:T(1,128)S(1)}, f32[4,1,256]{2,1,0:T(1,128)S(1)}, s32[1,1]{1,0:T(1,128)}, bf16[208,1024]{1,0:T(8,128)(2,1)S(1)}, bf16[1024,208]{1,...) custom-call(s32[1,64]{1,0:T(1,128)S(1)} %bitcast.53, ...), custom_call_target="tpu_custom_call" | custom-call | bytes 18000000 | tf_op jit(solution)/shard_map/route/pallas_call | solution.py:101
  34.6 0.0 collective-permute-done.12.refs_1_
  34.6 0.0 collective-permute-done.13.refs_2_
  34.6 0.0 collective-permute-done.14.refs_3_
  34.6 3.0 %gate_up_0.1 = (bf16[208,256]{1,0:T(8,128)(2,1)S(1)}, bf16[1024,64]{1,0:T(8,128)(2,1)S(1)}, bf16[4,1024]{1,0:T(4,128)(2,1)S(1)}, bf16[4,1024]{1,0:T(4,128)(2,1)S(1)}) custom-call(bf16[16,1024]{1,0:T(8,128)(2,1)S(1)} %add_convert_fusion.refs_0_, bf16[16,1024]{1,0:T(8,128)(2,1)S(1)} %collective-permute-done.12.refs_1_, ...), custom_call_target="tpu_custom_call" | custom-call | bytes 12000000 | tf_op jit(solution)/shard_map/gate_up_0/pallas_call | solution.py:101
  37.7 1.7 %collective-permute-start.18 = (bf16[208,256]{1,0:T(8,128)(2,1)S(1)}, bf16[208,256]{1,0:T(8,128)(2,1)S(1)}, u32[]{:S(2)}, u32[]{:S(2)}) collective-permute-start(bf16[208,256]{1,0:T(8,128)(2,1)S(1)} %get-tuple-element.153.refs_4_.refs_0_), channel_id=1, source_target_pairs={{0,2},{2,0},{1,3},{3,1},{4,6},{6,4},{5,7},{7,5},{8,10},{10,8},{9,1... | collective-permute-start | bytes 319496 | tf_op jit(solution)/shard_map/ppermute | solution.py:654
  39.4 2.8 %gate_up_1.1.refs_4_.refs_0_ = bf16[208,256]{1,0:T(8,128)(2,1)S(1)} custom-call(bf16[1024,64]{1,0:T(8,128)(2,1)S(1)} %get-tuple-element.149.refs_0_, bf16[208,1024]{1,0:T(8,128)(2,1)S(1)} %get-tuple-element.144.refs_4_.refs_1_, bf16[16,128,1024]{2,1,0:T(8,128)(2,1)S(1)} %get-tuple-element.133.refs_8_.refs_2_, ...), custom_call_target="tpu_custom_call" | custom-call | bytes 12000000 | tf_op jit(solution)/shard_map/gate_up_1/pallas_call | solution.py:101
  42.2 0.5 collective-permute-start.17
  42.7 2.8 %gate_up_2.1.refs_0_ = bf16[208,256]{1,0:T(8,128)(2,1)S(1)} custom-call(bf16[1024,64]{1,0:T(8,128)(2,1)S(1)} %get-tuple-element.149.refs_0_, bf16[208,1024]{1,0:T(8,128)(2,1)S(1)} %get-tuple-element.144.refs_4_.refs_1_, bf16[16,128,1024]{2,1,0:T(8,128)(2,1)S(1)} %get-tuple-element.150.refs_2_, bf16[16,128,1024]{2,1,0:T(8,128)(2,1)S(1)} %get-tuple-element.151.refs_3_, ...), custom_call_target="tpu_custom_call" | custom-call | bytes 12000000 | tf_op jit(solution)/shard_map/gate_up_2/pallas_call | solution.py:101
  45.5 1.7 %collective-permute-start.16 = (bf16[208,256]{1,0:T(8,128)(2,1)S(1)}, bf16[208,256]{1,0:T(8,128)(2,1)S(1)}, u32[]{:S(2)}, u32[]{:S(2)}) collective-permute-start(bf16[208,256]{1,0:T(8,128)(2,1)S(1)} %gate_up_2.1.refs_0_), channel_id=1, source_target_pairs={{0,2},{2,0},{1,3},{3,1},{4,6},{6,4},{5,7},{7,5},{8,10},{10,8},{9,1... | collective-permute-start | bytes 319496 | tf_op jit(solution)/shard_map/ppermute | solution.py:654
  47.2 0.4 collective-permute-start.15
  47.6 0.0 collective-permute-done.18.refs_1_
  47.6 1.1 %down_0.1.refs_5_ = f32[64,1024]{1,0:T(8,128)S(1)} custom-call(bf16[208,256]{1,0:T(8,128)(2,1)S(1)} %get-tuple-element.153.refs_4_.refs_0_, bf16[208,256]{1,0:T(8,128)(2,1)S(1)} %collective-permute-done.18.refs_1_, f32[208,1]{1,0:T(8,128)S(1)} %get-tuple-element.156.refs_2_, bf16[1024,208]{1,0:T(8,128)(2,1)S(1)} %get-tuple-element.157.refs_3_, ...), custom_call_target="tpu_custom_call" | custom-call | bytes 9000000 | tf_op jit(solution)/shard_map/down_0/pallas_call | solution.py:101
  48.7 0.0 collective-permute-done.17.refs_1_
  48.7 1.1 %down_1.1.refs_5_ = f32[64,1024]{1,0:T(8,128)S(1)} custom-call(bf16[208,256]{1,0:T(8,128)(2,1)S(1)} %gate_up_1.1.refs_4_.refs_0_, bf16[208,256]{1,0:T(8,128)(2,1)S(1)} %collective-permute-done.17.refs_1_, f32[208,1]{1,0:T(8,128)S(1)} %get-tuple-element.156.refs_2_, bf16[1024,208]{1,0:T(8,128)(2,1)S(1)} %get-tuple-element.157.refs_3_, ...), custom_call_target="tpu_custom_call" | custom-call | bytes 9000000 | tf_op jit(solution)/shard_map/down_1/pallas_call | solution.py:101
  49.7 0.5 collective-permute-done.16.refs_1_
  50.3 1.1 %down_2.1 = (f32[64,512]{1,0:T(8,128)S(1)}, f32[64,512]{1,0:T(8,128)S(1)}) custom-call(bf16[208,256]{1,0:T(8,128)(2,1)S(1)} %gate_up_2.1.refs_0_, bf16[208,256]{1,0:T(8,128)(2,1)S(1)} %collective-permute-done.16.refs_1_, f32[208,1]{1,0:T(8,128)S(1)} %get-tuple-element.156.refs_2_, bf16[1024,208]{1,0:T(8,128)(2,1)S(1)} %get-tuple-element.157.refs_3_, ...), custom_call_target="tpu_custom_call" | custom-call | bytes 9000000 | tf_op jit(solution)/shard_map/down_2/pallas_call | solution.py:101
  51.3 0.0 collective-permute-done.15.refs_1_
  51.3 0.1 collective-permute-start.19
  52.1 0.8 %while.10 = (s32[]{:T(128)}, f32[16,512]{1,0:T(8,128)S(1)}, s32[1,1]{1,0:T(1,128)}, bf16[16,1024]{1,0:T(8,128)(2,1)S(1)}, bf16[16,1024]{1,0:T(8,128)(2,1)S(1)}, ...) while((s32[]{:T(128)}, f32[16,512]{1,0:T(8,128)S(1)}, ...), condition=%wide.region_1.2_spmd, body=%wide.region_0.1_spmd.sunk | while | flops 2912233472 | bytes 72229176 | solution.py:702
  52.9 0.0 collective-permute-done.19.refs_1_
  53.0 0.1 collective-permute-start.20
  53.1 2.2 %collective-permute-start.21 = (bf16[16,512]{1,0:T(8,128)(2,1)S(1)}, bf16[16,512]{1,0:T(8,128)(2,1)S(1)}, u32[]{:S(2)}, u32[]{:S(2)}) collective-permute-start(bf16[16,512]{1,0:T(8,128)(2,1)S(1)} %get-tuple-element.173), channel_id=1, source_target_pairs={{0,8},{4,12},{8,0},{12,4},{1,9},{5,13},{9,1},{13,5},{2,10},{6,14},... | collective-permute-start | bytes 49160 | tf_op jit(solution)/shard_map/ppermute | solution.py:538
  55.3 2.2 %collective-permute-start.22 = (bf16[16,512]{1,0:T(8,128)(2,1)S(1)}, bf16[16,512]{1,0:T(8,128)(2,1)S(1)}, u32[]{:S(2)}, u32[]{:S(2)}) collective-permute-start(bf16[16,512]{1,0:T(8,128)(2,1)S(1)} %get-tuple-element.174), channel_id=1, source_target_pairs={{0,12},{4,8},{8,4},{12,0},{1,13},{5,9},{9,5},{13,1},{2,14},{6,10},... | collective-permute-start | bytes 49160 | tf_op jit(solution)/shard_map/ppermute | solution.py:538
  57.4 0.6 %join.1 = bf16[4,2048]{1,0:T(4,128)(2,1)} custom-call(bf16[4,1024]{1,0:T(4,128)(2,1)S(1)} %get-tuple-element.147.refs_0_, bf16[4,1024]{1,0:T(4,128)(2,1)S(1)} %collective-permute-done.15.refs_1_), custom_call_target="tpu_custom_call" | custom-call | bytes 6000000 | tf_op jit(solution)/shard_map/join/pallas_call | solution.py:101
  58.1 0.0 collective-permute-done.20
  58.1 0.0 collective-permute-done.21
  58.1 2.7 %collective-permute-done.22 = bf16[16,512]{1,0:T(8,128)(2,1)S(1)} collective-permute-done((bf16[16,512]{1,0:T(8,128)(2,1)S(1)}, bf16[16,512]{1,0:T(8,128)(2,1)S(1)}, u32[]{:S(2)}, u32[]{:S(2)}) %collective-permute-start.22) | collective-permute-done | bytes 16416 | tf_op jit(solution)/shard_map/ppermute | solution.py:538
  60.8 0.6 %add_convert_fusion.1 = bf16[16,512]{1,0:T(8,128)(2,1)} fusion(f32[16,512]{1,0:T(8,128)S(1)} %get-tuple-element.175, bf16[16,512]{1,0:T(8,128)(2,1)S(1)} %collective-permute-done.22, bf16[16,512]{1,0:T(8,128)(2,1)S(1)} %collective-permute-done.21, f32[16,512]{1,0:T(8,128)S(1)} %get-tuple-element.171, bf16[16,512]{1,0:T(8,128)(2,1)S(1)} %collective-permute-done.20), kind=kLoop, calls=%fused_computation.21 | loop fusion | flops 65536 | bytes 131072 | tf_op jit(solution)/shard_map/convert_element_type | solution.py:708
  (3 shorter events, 0.1 us)
Async XLA Ops:
  6.1 7.3 %collective-permute-start.5 = (bf16[4,1024]{1,0:T(4,128)(2,1)S(1)}, bf16[4,1024]{1,0:T(4,128)(2,1)S(1)}, u32[]{:S(2)}, u32[]{:S(2)}) collective-permute-start(bf16[4,1024]{1,0:T(4,128)(2,1)S(1)} %get-tuple-element.128), channel_id=1, source_target_pairs={{0,1},{1,0},{2,3},{3,2},{4,5},{5,4},{6,7},{7,6},{8,9},{9,8},{10,11... | collective-permute-start | bytes 24584 | tf_op jit(solution)/shard_map/ppermute | solution.py:538
  6.6 6.8 %collective-permute-start.6 = (bf16[4,1024]{1,0:T(4,128)(2,1)S(1)}, bf16[4,1024]{1,0:T(4,128)(2,1)S(1)}, u32[]{:S(2)}, u32[]{:S(2)}) collective-permute-start(bf16[4,1024]{1,0:T(4,128)(2,1)S(1)} %get-tuple-element.129), channel_id=1, source_target_pairs={{0,2},{1,3},{2,0},{3,1},{4,6},{5,7},{6,4},{7,5},{8,10},{9,11},{10,... | collective-permute-start | bytes 24584 | tf_op jit(solution)/shard_map/ppermute | solution.py:538
  9.2 4.3 %collective-permute-start.7 = (bf16[4,1024]{1,0:T(4,128)(2,1)S(1)}, bf16[4,1024]{1,0:T(4,128)(2,1)S(1)}, u32[]{:S(2)}, u32[]{:S(2)}) collective-permute-start(bf16[4,1024]{1,0:T(4,128)(2,1)S(1)} %get-tuple-element.130), channel_id=1, source_target_pairs={{0,3},{1,2},{2,1},{3,0},{4,7},{5,6},{6,5},{7,4},{8,11},{9,10},{10,... | collective-permute-start | bytes 24584 | tf_op jit(solution)/shard_map/ppermute | solution.py:538
  9.2 4.2 %collective-permute-start.8 = (bf16[16,128]{1,0:T(8,128)(2,1)S(1)}, bf16[16,128]{1,0:T(8,128)(2,1)S(1)}, u32[]{:S(2)}, u32[]{:S(2)}) collective-permute-start(bf16[16,128]{1,0:T(8,128)(2,1)S(1)} %get-tuple-element.131.refs_4_), channel_id=1, source_target_pairs={{1,5},{2,10},{3,15},{5,1},{6,14},{7,11},{9,13},{10,2},{11,7},{13,9... | collective-permute-start | bytes 12296 | tf_op jit(solution)/shard_map/ppermute | solution.py:585
  16.1 9.9 %collective-permute-start.10 = (bf16[16,1152]{1,0:T(8,128)(2,1)S(1)}, bf16[16,1152]{1,0:T(8,128)(2,1)S(1)}, u32[]{:S(2)}, u32[]{:S(2)}) collective-permute-start(bf16[16,1152]{1,0:T(8,128)(2,1)S(1)} %get-tuple-element.136), channel_id=1, source_target_pairs={{0,2},{1,3},{2,0},{3,1},{4,6},{5,7},{6,4},{7,5},{8,10},{9,11},{10,... | collective-permute-start | bytes 110600 | tf_op jit(solution)/shard_map/ppermute | solution.py:538
  21.8 4.3 %collective-permute-start.11 = (bf16[16,1152]{1,0:T(8,128)(2,1)S(1)}, bf16[16,1152]{1,0:T(8,128)(2,1)S(1)}, u32[]{:S(2)}, u32[]{:S(2)}) collective-permute-start(bf16[16,1152]{1,0:T(8,128)(2,1)S(1)} %get-tuple-element.136), channel_id=1, source_target_pairs={{0,3},{1,2},{2,1},{3,0},{4,7},{5,6},{6,5},{7,4},{8,11},{9,10},{10,... | collective-permute-start | bytes 110600 | tf_op jit(solution)/shard_map/ppermute | solution.py:538
  22.5 8.0 %copy-start = (s32[64]{0:T(128)S(1)}, s32[64]{0:T(128)}, u32[]{:S(2)}) copy-start(s32[64]{0:T(128)} %param.20) | copy-start | bytes 772
  22.5 3.6 %collective-permute-start.9 = (bf16[16,1152]{1,0:T(8,128)(2,1)S(1)}, bf16[16,1152]{1,0:T(8,128)(2,1)S(1)}, u32[]{:S(2)}, u32[]{:S(2)}) collective-permute-start(bf16[16,1152]{1,0:T(8,128)(2,1)S(1)} %get-tuple-element.135.refs_2_), channel_id=1, source_target_pairs={{0,1},{1,0},{2,3},{3,2},{4,5},{5,4},{6,7},{7,6},{8,9},{9,8},{10,11... | collective-permute-start | bytes 110600 | tf_op jit(solution)/shard_map/ppermute | solution.py:538
  26.1 8.5 %collective-permute-start.12 = (bf16[16,1024]{1,0:T(8,128)(2,1)S(1)}, bf16[16,1024]{1,0:T(8,128)(2,1)S(1)}, u32[]{:S(2)}, u32[]{:S(2)}) collective-permute-start(bf16[16,1024]{1,0:T(8,128)(2,1)S(1)} %add_convert_fusion.refs_0_), channel_id=1, source_target_pairs={{0,4},{4,0},{8,12},{12,8},{1,5},{5,1},{9,13},{13,9},{2,6},{6,2},{1... | collective-permute-start | bytes 98312 | tf_op jit(solution)/shard_map/ppermute | solution.py:538
  27.1 7.4 %collective-permute-start.13 = (bf16[16,1024]{1,0:T(8,128)(2,1)S(1)}, bf16[16,1024]{1,0:T(8,128)(2,1)S(1)}, u32[]{:S(2)}, u32[]{:S(2)}) collective-permute-start(bf16[16,1024]{1,0:T(8,128)(2,1)S(1)} %add_convert_fusion.refs_0_), channel_id=1, source_target_pairs={{0,8},{4,12},{8,0},{12,4},{1,9},{5,13},{9,1},{13,5},{2,10},{6,14},... | collective-permute-start | bytes 98312 | tf_op jit(solution)/shard_map/ppermute | solution.py:538
  28.2 6.4 %collective-permute-start.14 = (bf16[16,1024]{1,0:T(8,128)(2,1)S(1)}, bf16[16,1024]{1,0:T(8,128)(2,1)S(1)}, u32[]{:S(2)}, u32[]{:S(2)}) collective-permute-start(bf16[16,1024]{1,0:T(8,128)(2,1)S(1)} %add_convert_fusion.refs_0_), channel_id=1, source_target_pairs={{0,12},{4,8},{8,4},{12,0},{1,13},{5,9},{9,5},{13,1},{2,14},{6,10},... | collective-permute-start | bytes 98312 | tf_op jit(solution)/shard_map/ppermute | solution.py:538
  37.7 9.9 %collective-permute-start.18 = (bf16[208,256]{1,0:T(8,128)(2,1)S(1)}, bf16[208,256]{1,0:T(8,128)(2,1)S(1)}, u32[]{:S(2)}, u32[]{:S(2)}) collective-permute-start(bf16[208,256]{1,0:T(8,128)(2,1)S(1)} %get-tuple-element.153.refs_4_.refs_0_), channel_id=1, source_target_pairs={{0,2},{2,0},{1,3},{3,1},{4,6},{6,4},{5,7},{7,5},{8,10},{10,8},{9,1... | collective-permute-start | bytes 319496 | tf_op jit(solution)/shard_map/ppermute | solution.py:654
  42.2 6.5 %collective-permute-start.17 = (bf16[208,256]{1,0:T(8,128)(2,1)S(1)}, bf16[208,256]{1,0:T(8,128)(2,1)S(1)}, u32[]{:S(2)}, u32[]{:S(2)}) collective-permute-start(bf16[208,256]{1,0:T(8,128)(2,1)S(1)} %gate_up_1.1.refs_4_.refs_0_), channel_id=1, source_target_pairs={{0,2},{2,0},{1,3},{3,1},{4,6},{6,4},{5,7},{7,5},{8,10},{10,8},{9,1... | collective-permute-start | bytes 319496 | tf_op jit(solution)/shard_map/ppermute | solution.py:654
  45.5 4.8 %collective-permute-start.16 = (bf16[208,256]{1,0:T(8,128)(2,1)S(1)}, bf16[208,256]{1,0:T(8,128)(2,1)S(1)}, u32[]{:S(2)}, u32[]{:S(2)}) collective-permute-start(bf16[208,256]{1,0:T(8,128)(2,1)S(1)} %gate_up_2.1.refs_0_), channel_id=1, source_target_pairs={{0,2},{2,0},{1,3},{3,1},{4,6},{6,4},{5,7},{7,5},{8,10},{10,8},{9,1... | collective-permute-start | bytes 319496 | tf_op jit(solution)/shard_map/ppermute | solution.py:654
  47.2 4.1 %collective-permute-start.15 = (bf16[4,1024]{1,0:T(4,128)(2,1)S(1)}, bf16[4,1024]{1,0:T(4,128)(2,1)S(1)}, u32[]{:S(2)}, u32[]{:S(2)}) collective-permute-start(bf16[4,1024]{1,0:T(4,128)(2,1)S(1)} %get-tuple-element.154), channel_id=1, source_target_pairs={{0,2},{2,0},{1,3},{3,1},{4,6},{6,4},{5,7},{7,5},{8,10},{10,8},{9,1... | collective-permute-start | bytes 24584 | tf_op jit(solution)/shard_map/ppermute | solution.py:619
  51.3 1.6 %collective-permute-start.19 = (f32[64,512]{1,0:T(8,128)S(1)}, f32[64,512]{1,0:T(8,128)S(1)}, u32[]{:S(2)}, u32[]{:S(2)}) collective-permute-start(f32[64,512]{1,0:T(8,128)S(1)} %get-tuple-element.165), channel_id=1, source_target_pairs={{0,1},{1,0},{2,3},{3,2},{4,5},{5,4},{6,7},{7,6},{8,9},{9,8},{10,11... | collective-permute-start | bytes 393224 | tf_op jit(solution)/shard_map/ppermute | solution.py:538
  53.0 5.1 %collective-permute-start.20 = (bf16[16,512]{1,0:T(8,128)(2,1)S(1)}, bf16[16,512]{1,0:T(8,128)(2,1)S(1)}, u32[]{:S(2)}, u32[]{:S(2)}) collective-permute-start(bf16[16,512]{1,0:T(8,128)(2,1)S(1)} %get-tuple-element.172), channel_id=1, source_target_pairs={{0,4},{4,0},{8,12},{12,8},{1,5},{5,1},{9,13},{13,9},{2,6},{6,2},{1... | collective-permute-start | bytes 49160 | tf_op jit(solution)/shard_map/ppermute | solution.py:538
  53.1 5.0 %collective-permute-start.21 = (bf16[16,512]{1,0:T(8,128)(2,1)S(1)}, bf16[16,512]{1,0:T(8,128)(2,1)S(1)}, u32[]{:S(2)}, u32[]{:S(2)}) collective-permute-start(bf16[16,512]{1,0:T(8,128)(2,1)S(1)} %get-tuple-element.173), channel_id=1, source_target_pairs={{0,8},{4,12},{8,0},{12,4},{1,9},{5,13},{9,1},{13,5},{2,10},{6,14},... | collective-permute-start | bytes 49160 | tf_op jit(solution)/shard_map/ppermute | solution.py:538
  55.3 5.5 %collective-permute-start.22 = (bf16[16,512]{1,0:T(8,128)(2,1)S(1)}, bf16[16,512]{1,0:T(8,128)(2,1)S(1)}, u32[]{:S(2)}, u32[]{:S(2)}) collective-permute-start(bf16[16,512]{1,0:T(8,128)(2,1)S(1)} %get-tuple-element.174), channel_id=1, source_target_pairs={{0,12},{4,8},{8,4},{12,0},{1,13},{5,9},{9,5},{13,1},{2,14},{6,10},... | collective-permute-start | bytes 49160 | tf_op jit(solution)/shard_map/ppermute | solution.py:538

commit v4 on v3

--- a/solution.py
+++ b/solution.py
@@ -39,6 +39,10 @@
 SMEM = pl.BlockSpec(memory_space=pltpu.SMEM)
 HBM = pl.BlockSpec(memory_space=pltpu.HBM)
 ANY = pl.BlockSpec(memory_space=pl.ANY)
+
+
+def in_vmem(value):
+    return pltpu.with_memory_space_constraint(value, pltpu.VMEM)
 
 
 def in_hbm(value):
@@ -365,7 +369,19 @@
     )
 
 
-def gate_up_kernel(*refs, sources, first):
+def add_kernel(kept, *refs):
+    total = kept[...]
+    for ref in refs[:-1]:
+        total = total + ref[:, : total.shape[1]].astype(F32)
+    refs[-1][...] = total.astype(BF16)
+
+
+def add(kept, others):
+    outs = [jax.ShapeDtypeStruct(kept.shape, BF16)]
+    return call(add_kernel, "add", [kept, *others], [VMEM] * (1 + len(others)), outs)[0][0]
+
+
+def gate_up_kernel(*refs, sources, first, index):
     where = position()
     inputs, refs = refs[:sources], refs[sources:]
     pick_ref, g_ref, u_ref, out_ref = refs[:4]
@@ -387,7 +403,8 @@
     experts, _, depth = g_ref.shape
     rows = columns_ref.shape[1]
     for base, w_ref in ((0, g_ref), (CHUNK, u_ref)):
-        value = dot_nn(w_ref[...].reshape(experts * CHUNK, depth), columns_ref[...]).astype(BF16)
+        units = slice(index * CHUNK, (index + 1) * CHUNK) if w_ref.shape[1] > CHUNK else slice(None)
+        value = dot_nn(w_ref[:, units, :].reshape(experts * CHUNK, depth), columns_ref[...]).astype(BF16)
         for e in range(experts):
             both[base : base + CHUNK, e * rows : (e + 1) * rows] = value[
                 e * CHUNK : (e + 1) * CHUNK
@@ -406,7 +423,7 @@
         outs += [jax.ShapeDtypeStruct((own_rows, depth), BF16)] * 2
         scratch.insert(0, pltpu.VMEM((rows, depth), F32))
     results, held = call(
-        functools.partial(gate_up_kernel, sources=len(xs), first=first),
+        functools.partial(gate_up_kernel, sources=len(xs), first=first, index=index),
         f"gate_up_{index}",
         [*xs, pick, w_gate, w_up],
         [VMEM] * (len(xs) + 3),
@@ -420,7 +437,7 @@
     return results[0], results[1:2] if first else xs, results[2:], held
 
 
-def down_kernel(own_ref, other_ref, weight_ref, spread_ref, d_ref, *refs, carried):
+def down_kernel(own_ref, other_ref, weight_ref, spread_ref, d_ref, *refs, carried, index):
     before, outs = refs[:carried], refs[carried:]
     experts, _, depth = d_ref.shape
     rows = spread_ref.shape[0] // experts
@@ -429,7 +446,8 @@
     hidden = (gate / (1.0 + jnp.exp(-gate)) * up * weight_ref[...]).astype(BF16)
     spread = dot_nn(spread_ref[...], hidden).astype(BF16)
     left = jnp.concatenate([spread[e * rows : (e + 1) * rows] for e in range(experts)], axis=1)
-    total = dot_nn(left, d_ref[...].reshape(experts * CHUNK, depth))
+    units = slice(index * CHUNK, (index + 1) * CHUNK)
+    total = dot_nn(left, d_ref[:, units, :].reshape(experts * CHUNK, depth))
     if carried:
         total = total + before[0][...]
     if len(outs) == 1:
@@ -448,7 +466,7 @@
     carried = [] if before is None else [before]
     parts = 2 if halved else 1
     return call(
-        functools.partial(down_kernel, carried=len(carried)),
+        functools.partial(down_kernel, carried=len(carried), index=index),
         f"down_{index}",
         [own, other, slot_weight, spread, w_down, *carried],
         [VMEM] * (5 + len(carried)),
@@ -570,32 +588,30 @@
 
     if direct:
         axes = ("tp", "sub")
-        (*pieces, facts), (out_held, gate_0, up_0) = attend(
+        (*pieces, facts), (out_held,) = attend(
             queries,
             keys_cache,
             values_cache,
             lengths,
             (routes.T, route_weight.T),
             shards,
-            [(out_weight, None), gates[0], ups[0]],
+            [(out_weight, None)],
             False,
         )
         inputs = [pieces[0]] + [xor_permute(pieces[k], axes, shards, k) for k in range(1, shards)]
         pairs = [(i, i ^ (shards * (i % shards))) for i in range(pools * shards) if i % shards]
         other_facts = lax.ppermute(facts, ("pool", "tp", "sub"), pairs)
-        gate_1, up_1 = load([gates[1], ups[1]], [pieces[0]], "load_a")
-        (kept, near, far, block), (gate_2,) = project(
-            inputs, [facts, other_facts], out_held, [gates[2]], [gate_1]
-        )
-        up_2, down_0 = load([ups[2], downs[0]], [near], "load_b")
-        x_sum, blocks = kept, [block]
+        (kept, near, far, block), _ = project(inputs, [facts, other_facts], out_held, [], [])
+        gate_1, up_1 = gate_2, up_2 = in_vmem(w_gate), in_vmem(w_up)
+        gate_0, up_0 = load([gates[0], ups[0]], [near], "load_b")
+        blocks = [block]
         for k in range(1, shards):
             blocks.append(xor_permute(near if k < subs else far, axes, shards, k))
-            x_sum = x_sum + blocks[k][:, :half_width].astype(F32)
-        x_half, up_2 = lax.optimization_barrier((x_sum.astype(BF16), up_2))
+        x_sum = add(kept, blocks[1:])
+        x_half, gate_0 = lax.optimization_barrier((x_sum, gate_0))
         xs = [x_half] + [xor_permute(x_half, "pool", pools, k) for k in range(1, pools)]
         blocks, _ = lax.optimization_barrier((blocks, x_half))
-        (slots, weights, largest), (pick, spread, slot_weight), (down_1, down_2) = route(
+        (slots, weights, largest), (pick, spread, slot_weight), _ = route(
             blocks,
             expert_table,
             experts,
@@ -603,11 +619,11 @@
             top,
             capacity,
             pools,
-            downs[1:3],
+            [],
             False,
         )
         held = [(gate_0, up_0), (gate_1, up_1), (gate_2, up_2)]
-        held_down, sent, given = [down_0, down_1, down_2], [], xs
+        sent, given = [], xs
         for c in range(chunks):
             value, given, rest, _ = gate_up(
                 given, pick, *held[c], c, own_rows, [], False, sent[-1:]
@@ -641,8 +657,8 @@
         attended = lax.all_to_all(x_pool, ("tp", "sub"), split_axis=0, concat_axis=1, tiled=True)
         x_part = lax.all_gather(x_pool, "pool", axis=0, tiled=True)
         xs = [lax.all_gather(x_part, "sub", axis=1, tiled=True)]
-        held = load(gates + ups + downs, [], "load")
-        held_down, sent, given = held[2 * chunks :], [], xs
+        held = load(gates + ups, [], "load")
+        sent, given = [], xs
         for c in range(chunks):
             value, given, *_ = gate_up(
                 given, pick, held[c], held[chunks + c], c, own_rows, [], True
@@ -694,7 +710,7 @@
     for c in range(chunks):
         last = direct and c == chunks - 1
         result = down(
-            *both[c], slot_weight, spread, held_down[c], result[0], c, last, not direct
+            *both[c], slot_weight, spread, in_vmem(w_down), result[0], c, last, not direct
         )
     if direct:
         theirs, largest, *result = lax.optimization_barrier((theirs, largest, *result))

time: 61.6 us -> 56.4 us (0.916)
  Pallas kernels: 31.7 us -> 21.5 us
  waiting for transfers between devices: 3.29 us -> 8.83 us
  starting transfers between devices: 23.5 us -> 22.8 us
    pallas_call x13, Pallas kernels: 31.7 us -> 21.5 us  [call(): pl.pallas_call(run, in_specs=list(specs) + [HBM] * count_load + [ANY] * l...]
    ppermute x13, waiting for transfers between devices: 2.76 us -> 8.36 us  [xor_permute(): return lax.ppermute(value, axes, [(i, i ^ k) for i in range(count)])]
    ppermute x13, starting transfers between devices: 18.6 us -> 17.5 us  [xor_permute(): return lax.ppermute(value, axes, [(i, i ^ k) for i in range(count)])]
    ppermute x3, starting transfers between devices: 3.86 us -> 4.6 us  [exchange(): return (value, lax.ppermute(value, 'tp', [(0, 1), (1, 0)]))]
  transfers between devices with their start and end apart: 18 -> 18, of which waited for: 2 -> 6; matrix products, arithmetic and copies ran while one was open for 0% -> 0% of each run, Pallas kernels for 33% -> 25%
where the time goes in v4:
time: 56.4 us; the launch traced here: 56.2 us
  starting transfers between devices  22.8 us (40%)
  Pallas kernels  21.5 us (38%)
  waiting for transfers between devices  8.83 us (16%)
  between operations  1.59 us (3%)
  loops' own time  0.84 us (1%)
  other arithmetic  0.62 us (1%)
    pallas_call x13, Pallas kernels, call(): pl.pallas_call(run, in_specs=list(specs) + [HBM] * count_load + [ANY] * l...  21.5 us
    ppermute x13, starting transfers between devices, xor_permute(): return lax.ppermute(value, axes, [(i, i ^ k) for i in range(count)])  17.5 us
    ppermute x13, waiting for transfers between devices, xor_permute(): return lax.ppermute(value, axes, [(i, i ^ k) for i in range(count)])  8.36 us
    ppermute x3, starting transfers between devices, exchange(): return (value, lax.ppermute(value, 'tp', [(0, 1), (1, 0)]))  4.6 us
  transfers between devices with their start and end apart: 18, of which 6 were waited for; matrix products, arithmetic and copies ran while one was open for 0% of the time, Pallas kernels for 25%

profile of v4, /device:TPU:0, one launch (start us, length us, event | category | flops | bytes accessed | tf_op | source)
XLA Modules:
  0.0 56.2 jit_solution(7566949900016946130)
XLA Ops:
  0.6 3.6 %attention.1 = (bf16[4,1024]{1,0:T(4,128)(2,1)S(1)}, bf16[4,1024]{1,0:T(4,128)(2,1)S(1)}, bf16[4,1024]{1,0:T(4,128)(2,1)S(1)}, bf16[4,1024]{1,0:T(4,128)(2,1)S(1...) custom-call(bf16[4,4096]{1,0:T(4,128)(2,1)} %refs_0_.2, s32[4]{0:T(128)} %refs_1_.2, s32[8,16]{1,0:T(8,128)} %bitcast.63, ...), custom_call_target="tpu_custom_call" | custom-call | bytes 12000000 | tf_op jit(solution)/shard_map/attention/pallas_call | solution.py:105
  4.3 0.5 collective-permute-start.5
  4.8 2.6 %collective-permute-start.6 = (bf16[4,1024]{1,0:T(4,128)(2,1)S(1)}, bf16[4,1024]{1,0:T(4,128)(2,1)S(1)}, u32[]{:S(2)}, u32[]{:S(2)}) collective-permute-start(bf16[4,1024]{1,0:T(4,128)(2,1)S(1)} %get-tuple-element.122), channel_id=1, source_target_pairs={{0,2},{1,3},{2,0},{3,1},{4,6},{5,7},{6,4},{7,5},{8,10},{9,11},{10,... | collective-permute-start | bytes 24584 | tf_op jit(solution)/shard_map/ppermute | solution.py:556
  7.3 0.1 collective-permute-start.7
  7.4 0.6 %collective-permute-start.8 = (bf16[16,128]{1,0:T(8,128)(2,1)S(1)}, bf16[16,128]{1,0:T(8,128)(2,1)S(1)}, u32[]{:S(2)}, u32[]{:S(2)}) collective-permute-start(bf16[16,128]{1,0:T(8,128)(2,1)S(1)} %get-tuple-element.124.refs_4_), channel_id=1, source_target_pairs={{1,5},{2,10},{3,15},{5,1},{6,14},{7,11},{9,13},{10,2},{11,7},{13,9... | collective-permute-start | bytes 12296 | tf_op jit(solution)/shard_map/ppermute | solution.py:603
  8.1 0.0 collective-permute-done.8.refs_5_
  8.1 0.0 collective-permute-done.5.refs_1_
  8.1 0.9 %collective-permute-done.6.refs_2_ = bf16[4,1024]{1,0:T(4,128)(2,1)S(1)} collective-permute-done((bf16[4,1024]{1,0:T(4,128)(2,1)S(1)}, bf16[4,1024]{1,0:T(4,128)(2,1)S(1)}, u32[]{:S(2)}, u32[]{:S(2)}) %collective-permute-start.6) | collective-permute-done | bytes 8224 | tf_op jit(solution)/shard_map/ppermute | solution.py:556
  9.0 1.4 %collective-permute-done.7.refs_3_ = bf16[4,1024]{1,0:T(4,128)(2,1)S(1)} collective-permute-done((bf16[4,1024]{1,0:T(4,128)(2,1)S(1)}, bf16[4,1024]{1,0:T(4,128)(2,1)S(1)}, u32[]{:S(2)}, u32[]{:S(2)}) %collective-permute-start.7) | collective-permute-done | bytes 8224 | tf_op jit(solution)/shard_map/ppermute | solution.py:556
  10.4 0.8 %project.1 = (f32[16,1024]{1,0:T(8,128)S(1)}, bf16[16,1152]{1,0:T(8,128)(2,1)S(1)}, bf16[16,1152]{1,0:T(8,128)(2,1)S(1)}, bf16[16,128]{1,0:T(8,128)(2,1)S(1)}) custom-call(bf16[4,1024]{1,0:T(4,128)(2,1)S(1)} %get-tuple-element.120.refs_0_, bf16[4,1024]{1,0:T(4,128)(2,1)S(1)} %collective-permute-done.5.refs_1_, ...), custom_call_target="tpu_custom_call" | custom-call | bytes 6000000 | tf_op jit(solution)/shard_map/project/pallas_call | solution.py:105
  11.2 5.2 %collective-permute-start.10 = (bf16[16,1152]{1,0:T(8,128)(2,1)S(1)}, bf16[16,1152]{1,0:T(8,128)(2,1)S(1)}, u32[]{:S(2)}, u32[]{:S(2)}) collective-permute-start(bf16[16,1152]{1,0:T(8,128)(2,1)S(1)} %get-tuple-element.128), channel_id=1, source_target_pairs={{0,2},{1,3},{2,0},{3,1},{4,6},{5,7},{6,4},{7,5},{8,10},{9,11},{10,... | collective-permute-start | bytes 110600 | tf_op jit(solution)/shard_map/ppermute | solution.py:556
  16.3 0.0 collective-permute-start.11
  16.3 0.0 slice-start.7
  16.4 0.0 slice-start.8
  16.4 0.2 collective-permute-start.9
  16.6 3.6 %load_b.1 = (bf16[16,128,1024]{2,1,0:T(8,128)(2,1)S(1)}, bf16[16,128,1024]{2,1,0:T(8,128)(2,1)S(1)}) custom-call(bf16[16,384,1024]{2,1,0:T(8,128)(2,1)} %refs_2_.3, bf16[16,384,1024]{2,1,0:T(8,128)(2,1)} %refs_3_.3, bf16[16,1152]{1,0:T(8,128)(2,1)S(1)} %get-tuple-element.127.refs_2_), custom_call_target="tpu_custom_call" | custom-call | bytes 12000000 | tf_op jit(solution)/shard_map/load_b/pallas_call | solution.py:105
  20.2 0.0 collective-permute-done.10.refs_2_.refs_3_
  20.2 0.0 collective-permute-done.11.refs_3_.refs_4_
  20.2 0.0 collective-permute-done.9.refs_1_.refs_2_
  20.3 1.6 %collective-permute-start.12 = (bf16[16,1024]{1,0:T(8,128)(2,1)S(1)}, bf16[16,1024]{1,0:T(8,128)(2,1)S(1)}, u32[]{:S(2)}, u32[]{:S(2)}) collective-permute-start(bf16[16,1024]{1,0:T(8,128)(2,1)S(1)} %add.65.refs_0_), channel_id=1, source_target_pairs={{0,4},{4,0},{8,12},{12,8},{1,5},{5,1},{9,13},{13,9},{2,6},{6,2},{1... | collective-permute-start | bytes 98312 | tf_op jit(solution)/shard_map/ppermute | solution.py:556
  21.9 2.6 %collective-permute-start.13 = (bf16[16,1024]{1,0:T(8,128)(2,1)S(1)}, bf16[16,1024]{1,0:T(8,128)(2,1)S(1)}, u32[]{:S(2)}, u32[]{:S(2)}) collective-permute-start(bf16[16,1024]{1,0:T(8,128)(2,1)S(1)} %add.65.refs_0_), channel_id=1, source_target_pairs={{0,8},{4,12},{8,0},{12,4},{1,9},{5,13},{9,1},{13,5},{2,10},{6,14},... | collective-permute-start | bytes 98312 | tf_op jit(solution)/shard_map/ppermute | solution.py:556
  24.5 0.2 collective-permute-start.14
  24.7 0.0 copy-done.1
  24.7 0.9 %route.1 = (s32[4,1,256]{2,1,0:T(1,128)S(1)}, f32[4,1,256]{2,1,0:T(1,128)S(1)}, s32[1,1]{1,0:T(1,128)}, bf16[208,1024]{1,0:T(8,128)(2,1)S(1)}, bf16[1024,208]{1,0:T(8,128)(2,1)S(1)}, /*index=5*/f32[208,1]{1,0:T(8,128)S(1)}) custom-call(s32[1,64]{1,0:T(1,128)S(1)} %bitcast.59, bf16[16,128]{1,0:T(8,128)(2,1)S(1)} %get-tuple-element.132.refs_1_, ...), custom_call_target="tpu_custom_call" | custom-call | bytes 18000000 | tf_op jit(solution)/shard_map/route/pallas_call | solution.py:105
  25.6 0.0 collective-permute-done.12.refs_1_
  25.6 1.7 %collective-permute-done.13.refs_2_ = bf16[16,1024]{1,0:T(8,128)(2,1)S(1)} collective-permute-done((bf16[16,1024]{1,0:T(8,128)(2,1)S(1)}, bf16[16,1024]{1,0:T(8,128)(2,1)S(1)}, u32[]{:S(2)}, u32[]{:S(2)}) %collective-permute-start.13) | collective-permute-done | bytes 32800 | tf_op jit(solution)/shard_map/ppermute | solution.py:556
  27.3 2.9 %collective-permute-done.14.refs_3_ = bf16[16,1024]{1,0:T(8,128)(2,1)S(1)} collective-permute-done((bf16[16,1024]{1,0:T(8,128)(2,1)S(1)}, bf16[16,1024]{1,0:T(8,128)(2,1)S(1)}, u32[]{:S(2)}, u32[]{:S(2)}) %collective-permute-start.14) | collective-permute-done | bytes 32800 | tf_op jit(solution)/shard_map/ppermute | solution.py:556
  30.2 3.1 %gate_up_0.1 = (bf16[208,256]{1,0:T(8,128)(2,1)S(1)}, bf16[1024,64]{1,0:T(8,128)(2,1)S(1)}, bf16[4,1024]{1,0:T(4,128)(2,1)S(1)}, bf16[4,1024]{1,0:T(4,128)(2,1)S(1)}) custom-call(bf16[16,1024]{1,0:T(8,128)(2,1)S(1)} %add.65.refs_0_, bf16[16,1024]{1,0:T(8,128)(2,1)S(1)} %collective-permute-done.12.refs_1_, ...), custom_call_target="tpu_custom_call" | custom-call | bytes 12000000 | tf_op jit(solution)/shard_map/gate_up_0/pallas_call | solution.py:105
  33.3 2.4 %collective-permute-start.18 = (bf16[208,256]{1,0:T(8,128)(2,1)S(1)}, bf16[208,256]{1,0:T(8,128)(2,1)S(1)}, u32[]{:S(2)}, u32[]{:S(2)}) collective-permute-start(bf16[208,256]{1,0:T(8,128)(2,1)S(1)} %get-tuple-element.142.refs_4_.refs_0_), channel_id=1, source_target_pairs={{0,2},{2,0},{1,3},{3,1},{4,6},{6,4},{5,7},{7,5},{8,10},{10,8},{9,1... | collective-permute-start | bytes 319496 | tf_op jit(solution)/shard_map/ppermute | solution.py:670
  35.7 0.0 slice-done.3
  35.7 0.0 slice-done.6
  35.7 0.0 slice-done.4
  35.7 0.0 slice-done.5
  35.7 0.0 slice-done.7
  35.7 0.0 slice-done.8
  35.8 0.0 slice-start
  35.8 0.0 slice-start.1
  35.8 2.8 %gate_up_1.1.refs_4_.refs_0_ = bf16[208,256]{1,0:T(8,128)(2,1)S(1)} custom-call(bf16[1024,64]{1,0:T(8,128)(2,1)S(1)} %get-tuple-element.141.refs_0_, bf16[208,1024]{1,0:T(8,128)(2,1)S(1)} %get-tuple-element.136.refs_4_.refs_1_, bf16[16,384,1024]{2,1,0:T(8,128)(2,1)S(1)} %bitcast.56, bf16[16,384,1024]{2,1,0:T(8,128)(2,1)S(1)} %bitcast.58, ...), custom_call_target="tpu_custom_call" | custom-call | bytes 12000000 | tf_op jit(solution)/shard_map/gate_up_1/pallas_call | solution.py:105
  38.6 0.0 slice-start.2
  38.6 0.1 collective-permute-start.17
  38.7 2.8 %gate_up_2.1.refs_0_ = bf16[208,256]{1,0:T(8,128)(2,1)S(1)} custom-call(bf16[1024,64]{1,0:T(8,128)(2,1)S(1)} %get-tuple-element.141.refs_0_, bf16[208,1024]{1,0:T(8,128)(2,1)S(1)} %get-tuple-element.136.refs_4_.refs_1_, bf16[16,384,1024]{2,1,0:T(8,128)(2,1)S(1)} %bitcast.56, bf16[16,384,1024]{2,1,0:T(8,128)(2,1)S(1)} %bitcast.58, ...), custom_call_target="tpu_custom_call" | custom-call | bytes 12000000 | tf_op jit(solution)/shard_map/gate_up_2/pallas_call | solution.py:105
  41.6 2.1 %collective-permute-start.16 = (bf16[208,256]{1,0:T(8,128)(2,1)S(1)}, bf16[208,256]{1,0:T(8,128)(2,1)S(1)}, u32[]{:S(2)}, u32[]{:S(2)}) collective-permute-start(bf16[208,256]{1,0:T(8,128)(2,1)S(1)} %gate_up_2.1.refs_0_), channel_id=1, source_target_pairs={{0,2},{2,0},{1,3},{3,1},{4,6},{6,4},{5,7},{7,5},{8,10},{10,8},{9,1... | collective-permute-start | bytes 319496 | tf_op jit(solution)/shard_map/ppermute | solution.py:670
  43.6 0.1 collective-permute-start.15
  43.7 0.0 collective-permute-done.18.refs_1_
  43.7 0.0 slice-done
  43.7 0.0 slice-done.1
  43.7 0.0 slice-done.2
  43.7 1.1 %down_0.1.refs_5_ = f32[64,1024]{1,0:T(8,128)S(1)} custom-call(bf16[208,256]{1,0:T(8,128)(2,1)S(1)} %get-tuple-element.142.refs_4_.refs_0_, bf16[208,256]{1,0:T(8,128)(2,1)S(1)} %collective-permute-done.18.refs_1_, f32[208,1]{1,0:T(8,128)S(1)} %get-tuple-element.145.refs_2_, bf16[1024,208]{1,0:T(8,128)(2,1)S(1)} %get-tuple-element.146.refs_3_, ...), custom_call_target="tpu_custom_call" | custom-call | bytes 9000000 | tf_op jit(solution)/shard_map/down_0/pallas_call | solution.py:105
  44.8 0.0 collective-permute-done.17.refs_1_
  44.8 1.1 %down_1.1.refs_5_ = f32[64,1024]{1,0:T(8,128)S(1)} custom-call(bf16[208,256]{1,0:T(8,128)(2,1)S(1)} %gate_up_1.1.refs_4_.refs_0_, bf16[208,256]{1,0:T(8,128)(2,1)S(1)} %collective-permute-done.17.refs_1_, f32[208,1]{1,0:T(8,128)S(1)} %get-tuple-element.145.refs_2_, bf16[1024,208]{1,0:T(8,128)(2,1)S(1)} %get-tuple-element.146.refs_3_, ...), custom_call_target="tpu_custom_call" | custom-call | bytes 9000000 | tf_op jit(solution)/shard_map/down_1/pallas_call | solution.py:105
  45.9 0.5 collective-permute-done.16.refs_1_
  46.3 1.1 %down_2.1 = (f32[64,512]{1,0:T(8,128)S(1)}, f32[64,512]{1,0:T(8,128)S(1)}) custom-call(bf16[208,256]{1,0:T(8,128)(2,1)S(1)} %gate_up_2.1.refs_0_, bf16[208,256]{1,0:T(8,128)(2,1)S(1)} %collective-permute-done.16.refs_1_, f32[208,1]{1,0:T(8,128)S(1)} %get-tuple-element.145.refs_2_, bf16[1024,208]{1,0:T(8,128)(2,1)S(1)} %get-tuple-element.146.refs_3_, ...), custom_call_target="tpu_custom_call" | custom-call | bytes 9000000 | tf_op jit(solution)/shard_map/down_2/pallas_call | solution.py:105
  47.4 0.0 collective-permute-done.15.refs_1_
  47.4 0.1 collective-permute-start.19
  48.2 0.8 %while.10 = (s32[]{:T(128)}, f32[16,512]{1,0:T(8,128)S(1)}, s32[1,1]{1,0:T(1,128)}, bf16[16,1024]{1,0:T(8,128)(2,1)S(1)}, bf16[16,1024]{1,0:T(8,128)(2,1)S(1)}, ...) while((s32[]{:T(128)}, f32[16,512]{1,0:T(8,128)S(1)}, ...), condition=%wide.region_1.2_spmd, body=%wide.region_0.1_spmd.sunk | while | flops 2912233472 | bytes 122560848 | solution.py:718
  49.0 0.0 collective-permute-done.19.refs_1_
  49.1 0.1 collective-permute-start.20
  49.1 0.9 %collective-permute-start.21 = (bf16[16,512]{1,0:T(8,128)(2,1)S(1)}, bf16[16,512]{1,0:T(8,128)(2,1)S(1)}, u32[]{:S(2)}, u32[]{:S(2)}) collective-permute-start(bf16[16,512]{1,0:T(8,128)(2,1)S(1)} %get-tuple-element.159), channel_id=1, source_target_pairs={{0,8},{4,12},{8,0},{12,4},{1,9},{5,13},{9,1},{13,5},{2,10},{6,14},... | collective-permute-start | bytes 49160 | tf_op jit(solution)/shard_map/ppermute | solution.py:556
  50.0 3.5 %collective-permute-start.22 = (bf16[16,512]{1,0:T(8,128)(2,1)S(1)}, bf16[16,512]{1,0:T(8,128)(2,1)S(1)}, u32[]{:S(2)}, u32[]{:S(2)}) collective-permute-start(bf16[16,512]{1,0:T(8,128)(2,1)S(1)} %get-tuple-element.160), channel_id=1, source_target_pairs={{0,12},{4,8},{8,4},{12,0},{1,13},{5,9},{9,5},{13,1},{2,14},{6,10},... | collective-permute-start | bytes 49160 | tf_op jit(solution)/shard_map/ppermute | solution.py:556
  53.5 0.6 %join.1 = bf16[4,2048]{1,0:T(4,128)(2,1)} custom-call(bf16[4,1024]{1,0:T(4,128)(2,1)S(1)} %get-tuple-element.139.refs_0_, bf16[4,1024]{1,0:T(4,128)(2,1)S(1)} %collective-permute-done.15.refs_1_), custom_call_target="tpu_custom_call" | custom-call | bytes 6000000 | tf_op jit(solution)/shard_map/join/pallas_call | solution.py:105
  54.1 0.0 collective-permute-done.20
  54.1 0.0 collective-permute-done.21
  54.2 1.4 %collective-permute-done.22 = bf16[16,512]{1,0:T(8,128)(2,1)S(1)} collective-permute-done((bf16[16,512]{1,0:T(8,128)(2,1)S(1)}, bf16[16,512]{1,0:T(8,128)(2,1)S(1)}, u32[]{:S(2)}, u32[]{:S(2)}) %collective-permute-start.22) | collective-permute-done | bytes 16416 | tf_op jit(solution)/shard_map/ppermute | solution.py:556
  55.6 0.6 %add_convert_fusion = bf16[16,512]{1,0:T(8,128)(2,1)} fusion(f32[16,512]{1,0:T(8,128)S(1)} %get-tuple-element.161, bf16[16,512]{1,0:T(8,128)(2,1)S(1)} %collective-permute-done.22, bf16[16,512]{1,0:T(8,128)(2,1)S(1)} %collective-permute-done.21, f32[16,512]{1,0:T(8,128)S(1)} %get-tuple-element.157, bf16[16,512]{1,0:T(8,128)(2,1)S(1)} %collective-permute-done.20), kind=kLoop, calls=%fused_computation.20 | loop fusion | flops 65536 | bytes 131072 | tf_op jit(solution)/shard_map/convert_element_type | solution.py:724
  (11 shorter events, 0.1 us)
Async XLA Ops:
  4.3 3.8 %collective-permute-start.5 = (bf16[4,1024]{1,0:T(4,128)(2,1)S(1)}, bf16[4,1024]{1,0:T(4,128)(2,1)S(1)}, u32[]{:S(2)}, u32[]{:S(2)}) collective-permute-start(bf16[4,1024]{1,0:T(4,128)(2,1)S(1)} %get-tuple-element.121), channel_id=1, source_target_pairs={{0,1},{1,0},{2,3},{3,2},{4,5},{5,4},{6,7},{7,6},{8,9},{9,8},{10,11... | collective-permute-start | bytes 24584 | tf_op jit(solution)/shard_map/ppermute | solution.py:556
  4.8 4.2 %collective-permute-start.6 = (bf16[4,1024]{1,0:T(4,128)(2,1)S(1)}, bf16[4,1024]{1,0:T(4,128)(2,1)S(1)}, u32[]{:S(2)}, u32[]{:S(2)}) collective-permute-start(bf16[4,1024]{1,0:T(4,128)(2,1)S(1)} %get-tuple-element.122), channel_id=1, source_target_pairs={{0,2},{1,3},{2,0},{3,1},{4,6},{5,7},{6,4},{7,5},{8,10},{9,11},{10,... | collective-permute-start | bytes 24584 | tf_op jit(solution)/shard_map/ppermute | solution.py:556
  7.3 3.1 %collective-permute-start.7 = (bf16[4,1024]{1,0:T(4,128)(2,1)S(1)}, bf16[4,1024]{1,0:T(4,128)(2,1)S(1)}, u32[]{:S(2)}, u32[]{:S(2)}) collective-permute-start(bf16[4,1024]{1,0:T(4,128)(2,1)S(1)} %get-tuple-element.123), channel_id=1, source_target_pairs={{0,3},{1,2},{2,1},{3,0},{4,7},{5,6},{6,5},{7,4},{8,11},{9,10},{10,... | collective-permute-start | bytes 24584 | tf_op jit(solution)/shard_map/ppermute | solution.py:556
  7.4 0.7 %collective-permute-start.8 = (bf16[16,128]{1,0:T(8,128)(2,1)S(1)}, bf16[16,128]{1,0:T(8,128)(2,1)S(1)}, u32[]{:S(2)}, u32[]{:S(2)}) collective-permute-start(bf16[16,128]{1,0:T(8,128)(2,1)S(1)} %get-tuple-element.124.refs_4_), channel_id=1, source_target_pairs={{1,5},{2,10},{3,15},{5,1},{6,14},{7,11},{9,13},{10,2},{11,7},{13,9... | collective-permute-start | bytes 12296 | tf_op jit(solution)/shard_map/ppermute | solution.py:603
  10.4 25.3 %slice-start.3 = ((s8[12582912]{0:T(1024)(128)(4,1)}), s8[4194304]{0:T(1024)(128)(4,1)S(1)}, s32[]{:S(2)}) async-start(s8[12582912]{0:T(1024)(128)(4,1)} %bitcast.55), calls=%async_computation.3 | async-start | bytes 8388608
  10.4 25.3 %slice-start.6 = ((s8[12582912]{0:T(1024)(128)(4,1)}), s8[4194304]{0:T(1024)(128)(4,1)S(1)}, s32[]{:S(2)}) async-start(s8[12582912]{0:T(1024)(128)(4,1)} %bitcast.57), calls=%async_computation.6 | async-start | bytes 8388608
  11.2 9.0 %collective-permute-start.10 = (bf16[16,1152]{1,0:T(8,128)(2,1)S(1)}, bf16[16,1152]{1,0:T(8,128)(2,1)S(1)}, u32[]{:S(2)}, u32[]{:S(2)}) collective-permute-start(bf16[16,1152]{1,0:T(8,128)(2,1)S(1)} %get-tuple-element.128), channel_id=1, source_target_pairs={{0,2},{1,3},{2,0},{3,1},{4,6},{5,7},{6,4},{7,5},{8,10},{9,11},{10,... | collective-permute-start | bytes 110600 | tf_op jit(solution)/shard_map/ppermute | solution.py:556
  16.3 3.9 %collective-permute-start.11 = (bf16[16,1152]{1,0:T(8,128)(2,1)S(1)}, bf16[16,1152]{1,0:T(8,128)(2,1)S(1)}, u32[]{:S(2)}, u32[]{:S(2)}) collective-permute-start(bf16[16,1152]{1,0:T(8,128)(2,1)S(1)} %get-tuple-element.128), channel_id=1, source_target_pairs={{0,3},{1,2},{2,1},{3,0},{4,7},{5,6},{6,5},{7,4},{8,11},{9,10},{10,... | collective-permute-start | bytes 110600 | tf_op jit(solution)/shard_map/ppermute | solution.py:556
  16.3 8.4 %copy-start.1 = (s32[64]{0:T(128)S(1)}, s32[64]{0:T(128)}, u32[]{:S(2)}) copy-start(s32[64]{0:T(128)} %param.20) | copy-start | bytes 772
  16.3 19.4 %slice-start.4 = ((s8[12582912]{0:T(1024)(128)(4,1)}), s8[4194304]{0:T(1024)(128)(4,1)S(1)}, s32[]{:S(2)}) async-start(s8[12582912]{0:T(1024)(128)(4,1)} %bitcast.55), calls=%async_computation.4 | async-start | bytes 8388608
  16.3 19.4 %slice-start.5 = ((s8[12582912]{0:T(1024)(128)(4,1)}), s8[4194304]{0:T(1024)(128)(4,1)S(1)}, s32[]{:S(2)}) async-start(s8[12582912]{0:T(1024)(128)(4,1)} %bitcast.55), calls=%async_computation.5 | async-start | bytes 8388608
  16.3 19.4 %slice-start.7 = ((s8[12582912]{0:T(1024)(128)(4,1)}), s8[4194304]{0:T(1024)(128)(4,1)S(1)}, s32[]{:S(2)}) async-start(s8[12582912]{0:T(1024)(128)(4,1)} %bitcast.57), calls=%async_computation.7 | async-start | bytes 8388608
  16.4 19.4 %slice-start.8 = ((s8[12582912]{0:T(1024)(128)(4,1)}), s8[4194304]{0:T(1024)(128)(4,1)S(1)}, s32[]{:S(2)}) async-start(s8[12582912]{0:T(1024)(128)(4,1)} %bitcast.57), calls=%async_computation.8 | async-start | bytes 8388608
  16.4 3.9 %collective-permute-start.9 = (bf16[16,1152]{1,0:T(8,128)(2,1)S(1)}, bf16[16,1152]{1,0:T(8,128)(2,1)S(1)}, u32[]{:S(2)}, u32[]{:S(2)}) collective-permute-start(bf16[16,1152]{1,0:T(8,128)(2,1)S(1)} %get-tuple-element.127.refs_2_), channel_id=1, source_target_pairs={{0,1},{1,0},{2,3},{3,2},{4,5},{5,4},{6,7},{7,6},{8,9},{9,8},{10,11... | collective-permute-start | bytes 110600 | tf_op jit(solution)/shard_map/ppermute | solution.py:556
  20.3 5.4 %collective-permute-start.12 = (bf16[16,1024]{1,0:T(8,128)(2,1)S(1)}, bf16[16,1024]{1,0:T(8,128)(2,1)S(1)}, u32[]{:S(2)}, u32[]{:S(2)}) collective-permute-start(bf16[16,1024]{1,0:T(8,128)(2,1)S(1)} %add.65.refs_0_), channel_id=1, source_target_pairs={{0,4},{4,0},{8,12},{12,8},{1,5},{5,1},{9,13},{13,9},{2,6},{6,2},{1... | collective-permute-start | bytes 98312 | tf_op jit(solution)/shard_map/ppermute | solution.py:556
  21.9 5.4 %collective-permute-start.13 = (bf16[16,1024]{1,0:T(8,128)(2,1)S(1)}, bf16[16,1024]{1,0:T(8,128)(2,1)S(1)}, u32[]{:S(2)}, u32[]{:S(2)}) collective-permute-start(bf16[16,1024]{1,0:T(8,128)(2,1)S(1)} %add.65.refs_0_), channel_id=1, source_target_pairs={{0,8},{4,12},{8,0},{12,4},{1,9},{5,13},{9,1},{13,5},{2,10},{6,14},... | collective-permute-start | bytes 98312 | tf_op jit(solution)/shard_map/ppermute | solution.py:556
  24.5 5.7 %collective-permute-start.14 = (bf16[16,1024]{1,0:T(8,128)(2,1)S(1)}, bf16[16,1024]{1,0:T(8,128)(2,1)S(1)}, u32[]{:S(2)}, u32[]{:S(2)}) collective-permute-start(bf16[16,1024]{1,0:T(8,128)(2,1)S(1)} %add.65.refs_0_), channel_id=1, source_target_pairs={{0,12},{4,8},{8,4},{12,0},{1,13},{5,9},{9,5},{13,1},{2,14},{6,10},... | collective-permute-start | bytes 98312 | tf_op jit(solution)/shard_map/ppermute | solution.py:556
  33.3 10.4 %collective-permute-start.18 = (bf16[208,256]{1,0:T(8,128)(2,1)S(1)}, bf16[208,256]{1,0:T(8,128)(2,1)S(1)}, u32[]{:S(2)}, u32[]{:S(2)}) collective-permute-start(bf16[208,256]{1,0:T(8,128)(2,1)S(1)} %get-tuple-element.142.refs_4_.refs_0_), channel_id=1, source_target_pairs={{0,2},{2,0},{1,3},{3,1},{4,6},{6,4},{5,7},{7,5},{8,10},{10,8},{9,1... | collective-permute-start | bytes 319496 | tf_op jit(solution)/shard_map/ppermute | solution.py:670
  35.8 7.9 %slice-start = ((s8[12582912]{0:T(1024)(128)(4,1)}), s8[4194304]{0:T(1024)(128)(4,1)S(1)}, s32[]{:S(2)}) async-start(s8[12582912]{0:T(1024)(128)(4,1)} %bitcast.53), calls=%async_computation | async-start | bytes 8388608
  35.8 7.9 %slice-start.1 = ((s8[12582912]{0:T(1024)(128)(4,1)}), s8[4194304]{0:T(1024)(128)(4,1)S(1)}, s32[]{:S(2)}) async-start(s8[12582912]{0:T(1024)(128)(4,1)} %bitcast.53), calls=%async_computation.1 | async-start | bytes 8388608
  38.6 5.1 %slice-start.2 = ((s8[12582912]{0:T(1024)(128)(4,1)}), s8[4194304]{0:T(1024)(128)(4,1)S(1)}, s32[]{:S(2)}) async-start(s8[12582912]{0:T(1024)(128)(4,1)} %bitcast.53), calls=%async_computation.2 | async-start | bytes 8388608
  38.6 6.2 %collective-permute-start.17 = (bf16[208,256]{1,0:T(8,128)(2,1)S(1)}, bf16[208,256]{1,0:T(8,128)(2,1)S(1)}, u32[]{:S(2)}, u32[]{:S(2)}) collective-permute-start(bf16[208,256]{1,0:T(8,128)(2,1)S(1)} %gate_up_1.1.refs_4_.refs_0_), channel_id=1, source_target_pairs={{0,2},{2,0},{1,3},{3,1},{4,6},{6,4},{5,7},{7,5},{8,10},{10,8},{9,1... | collective-permute-start | bytes 319496 | tf_op jit(solution)/shard_map/ppermute | solution.py:670
  41.6 4.8 %collective-permute-start.16 = (bf16[208,256]{1,0:T(8,128)(2,1)S(1)}, bf16[208,256]{1,0:T(8,128)(2,1)S(1)}, u32[]{:S(2)}, u32[]{:S(2)}) collective-permute-start(bf16[208,256]{1,0:T(8,128)(2,1)S(1)} %gate_up_2.1.refs_0_), channel_id=1, source_target_pairs={{0,2},{2,0},{1,3},{3,1},{4,6},{6,4},{5,7},{7,5},{8,10},{10,8},{9,1... | collective-permute-start | bytes 319496 | tf_op jit(solution)/shard_map/ppermute | solution.py:670
  43.6 3.8 %collective-permute-start.15 = (bf16[4,1024]{1,0:T(4,128)(2,1)S(1)}, bf16[4,1024]{1,0:T(4,128)(2,1)S(1)}, u32[]{:S(2)}, u32[]{:S(2)}) collective-permute-start(bf16[4,1024]{1,0:T(4,128)(2,1)S(1)} %get-tuple-element.143), channel_id=1, source_target_pairs={{0,2},{2,0},{1,3},{3,1},{4,6},{6,4},{5,7},{7,5},{8,10},{10,8},{9,1... | collective-permute-start | bytes 24584 | tf_op jit(solution)/shard_map/ppermute | solution.py:635
  47.4 1.6 %collective-permute-start.19 = (f32[64,512]{1,0:T(8,128)S(1)}, f32[64,512]{1,0:T(8,128)S(1)}, u32[]{:S(2)}, u32[]{:S(2)}) collective-permute-start(f32[64,512]{1,0:T(8,128)S(1)} %get-tuple-element.151), channel_id=1, source_target_pairs={{0,1},{1,0},{2,3},{3,2},{4,5},{5,4},{6,7},{7,6},{8,9},{9,8},{10,11... | collective-permute-start | bytes 393224 | tf_op jit(solution)/shard_map/ppermute | solution.py:556
  49.1 5.1 %collective-permute-start.20 = (bf16[16,512]{1,0:T(8,128)(2,1)S(1)}, bf16[16,512]{1,0:T(8,128)(2,1)S(1)}, u32[]{:S(2)}, u32[]{:S(2)}) collective-permute-start(bf16[16,512]{1,0:T(8,128)(2,1)S(1)} %get-tuple-element.158), channel_id=1, source_target_pairs={{0,4},{4,0},{8,12},{12,8},{1,5},{5,1},{9,13},{13,9},{2,6},{6,2},{1... | collective-permute-start | bytes 49160 | tf_op jit(solution)/shard_map/ppermute | solution.py:556
  49.1 5.0 %collective-permute-start.21 = (bf16[16,512]{1,0:T(8,128)(2,1)S(1)}, bf16[16,512]{1,0:T(8,128)(2,1)S(1)}, u32[]{:S(2)}, u32[]{:S(2)}) collective-permute-start(bf16[16,512]{1,0:T(8,128)(2,1)S(1)} %get-tuple-element.159), channel_id=1, source_target_pairs={{0,8},{4,12},{8,0},{12,4},{1,9},{5,13},{9,1},{13,5},{2,10},{6,14},... | collective-permute-start | bytes 49160 | tf_op jit(solution)/shard_map/ppermute | solution.py:556
  50.0 5.5 %collective-permute-start.22 = (bf16[16,512]{1,0:T(8,128)(2,1)S(1)}, bf16[16,512]{1,0:T(8,128)(2,1)S(1)}, u32[]{:S(2)}, u32[]{:S(2)}) collective-permute-start(bf16[16,512]{1,0:T(8,128)(2,1)S(1)} %get-tuple-element.160), channel_id=1, source_target_pairs={{0,12},{4,8},{8,4},{12,0},{1,13},{5,9},{9,5},{13,1},{2,14},{6,10},... | collective-permute-start | bytes 49160 | tf_op jit(solution)/shard_map/ppermute | solution.py:556

commit v5 on v4

--- a/solution.py
+++ b/solution.py
@@ -158,20 +158,24 @@
     for h in range(heads):
         spread[:, h, :] = queries[:, h * HEAD_DIM : (h + 1) * HEAD_DIM]
     column = lax.broadcasted_iota(jnp.int32, (group, positions), 1)
-    for row in range(rows):
+    for pair in copies:
+        pair[0].wait()
+        pair[1].wait()
+    cases = [(row, j) for row in range(rows) for j in range(KV_HEADS)]
+    lanes = [slice(j * HEAD_DIM, (j + 1) * HEAD_DIM) for j in range(KV_HEADS)]
+    scores, terms, totals = [], [], []
+    for row, j in cases:
+        own = spread[row, j * group : (j + 1) * group, :].astype(BF16)
+        scores.append(dot_nt(own, k_ref[row, :, lanes[j]]))
+    for (row, j), score in zip(cases, scores):
         valid = column < lengths[row]
-        copies[row][0].wait()
-        copies[row][1].wait()
-        for j in range(KV_HEADS):
-            lanes = slice(j * HEAD_DIM, (j + 1) * HEAD_DIM)
-            own = spread[row, j * group : (j + 1) * group, :].astype(BF16)
-            scores = dot_nt(own, k_ref[row, :, lanes])
-            scores = jnp.where(valid, scores * (1.0 / math.sqrt(HEAD_DIM)), -1e30)
-            top = jnp.max(scores, axis=1, keepdims=True)
-            terms = jnp.where(valid, jnp.exp(scores - top), 0.0)
-            total = jnp.sum(terms, axis=1, keepdims=True)
-            value = dot_nn(terms.astype(BF16), v_ref[row, :, lanes]) / total
-            gathered[row, j * group : (j + 1) * group, :] = value
+        score = jnp.where(valid, score * (1.0 / math.sqrt(HEAD_DIM)), -1e30)
+        top = jnp.max(score, axis=1, keepdims=True)
+        terms.append(jnp.where(valid, jnp.exp(score - top), 0.0))
+        totals.append(jnp.sum(terms[-1], axis=1, keepdims=True))
+    for (row, j), term, total in zip(cases, terms, totals):
+        value = dot_nn(term.astype(BF16), v_ref[row, :, lanes[j]]) / total
+        gathered[row, j * group : (j + 1) * group, :] = value
     for h in range(heads):
         flat[:, h * HEAD_DIM : (h + 1) * HEAD_DIM] = gathered[:, h, :]
     width = heads * HEAD_DIM // pieces
@@ -218,7 +222,7 @@
     else:
         for k in range(sources):
             width = given[k].shape[1]
-            held[where[3] ^ where[0] ^ k] = given[k][:, width - lanes :].astype(F32)
+            held[where[3] ^ k] = given[k][:, width - lanes :].astype(F32)
     rows = pools * pool_rows
     total = table_ref.shape[1]
     groups, _, lanes = slot_ref.shape
@@ -327,14 +331,10 @@
 
 def project_kernel(*refs, sources):
     where = position()
-    inputs, (own_ref, sent_ref, w_ref) = refs[:sources], refs[sources : sources + 3]
-    kept, near, far, held = refs[sources + 3 :]
+    inputs, (w_ref, kept, near, far) = refs[:sources], refs[sources:]
     own_rows = inputs[0].shape[0]
     count = sources * own_rows
     half = kept.shape[1]
-    facts = jnp.where(where[0] == 0, own_ref[...].astype(F32), sent_ref[...].astype(F32))
-    facts = facts.astype(BF16)
-    held[...] = facts
     stacked = jnp.concatenate([ref[...].astype(F32) for ref in inputs], axis=0).astype(BF16)
     target = lax.broadcasted_iota(jnp.int32, (count, count), 0)
     origin = lax.broadcasted_iota(jnp.int32, (count, count), 1)
@@ -343,42 +343,35 @@
     for k, out in ((1, far), (0, near)):
         start = pl.multiple_of((where[1] ^ k) * half, half)
         value = dot_nn(x, w_ref[:, pl.ds(start, half)])
-        out[:, :half] = value.astype(BF16)
-        out[:, half:] = facts
+        out[...] = value.astype(BF16)
         if k == 0:
             kept[...] = value
 
 
-def project(inputs, facts, out_weight, loads, anchors):
+def project(inputs, out_weight):
     sources = len(inputs)
-    count, half = sources * inputs[0].shape[0], out_weight.shape[1] // 2
-    sent = jax.ShapeDtypeStruct((count, half + FACT_LANES), BF16)
+    shape = (sources * inputs[0].shape[0], out_weight.shape[1] // 2)
     return call(
         functools.partial(project_kernel, sources=sources),
         "project",
-        [*inputs, *facts, out_weight],
-        [VMEM] * (sources + 3),
-        [
-            jax.ShapeDtypeStruct((count, half), F32),
-            sent,
-            sent,
-            jax.ShapeDtypeStruct((count, FACT_LANES), BF16),
-        ],
-        loads=loads,
-        anchors=anchors,
-    )
-
-
-def add_kernel(kept, *refs):
+        [*inputs, out_weight],
+        [VMEM] * (sources + 1),
+        [jax.ShapeDtypeStruct(shape, kind) for kind in (F32, BF16, BF16)],
+    )[0]
+
+
+def add_kernel(kept, facts, *refs):
+    half = kept.shape[1]
     total = kept[...]
     for ref in refs[:-1]:
-        total = total + ref[:, : total.shape[1]].astype(F32)
-    refs[-1][...] = total.astype(BF16)
-
-
-def add(kept, others):
-    outs = [jax.ShapeDtypeStruct(kept.shape, BF16)]
-    return call(add_kernel, "add", [kept, *others], [VMEM] * (1 + len(others)), outs)[0][0]
+        total = total + ref[...].astype(F32)
+    refs[-1][:, :half] = total.astype(BF16)
+    refs[-1][:, half:] = facts[...]
+
+
+def add(kept, facts, others):
+    outs = [jax.ShapeDtypeStruct((kept.shape[0], kept.shape[1] + facts.shape[1]), BF16)]
+    return call(add_kernel, "add", [kept, facts, *others], [VMEM] * (2 + len(others)), outs)[0][0]
 
 
 def gate_up_kernel(*refs, sources, first, index):
@@ -393,10 +386,10 @@
         place = lax.broadcasted_iota(jnp.int32, (own_rows, count), 1)
         for out, shard in ((mine_ref, where[0]), (theirs_ref, where[0] ^ where[4])):
             chosen = jnp.where(place == row + shard * own_rows, 1.0, 0.0).astype(BF16)
-            out[...] = dot_nn(chosen, inputs[0][...]).astype(BF16)
+            out[...] = dot_nn(chosen, inputs[0][:, : x.shape[1]]).astype(BF16)
         for k in range(sources):
             start = pl.multiple_of((where[3] ^ k) * count, count) if sources > 1 else 0
-            x[pl.ds(start, count), :] = inputs[k][...].astype(F32)
+            x[pl.ds(start, count), :] = inputs[k][:, : x.shape[1]].astype(F32)
         columns_ref[...] = x[...].T.astype(BF16)
     else:
         (columns_ref,), (both,) = inputs, refs[4:]
@@ -487,11 +480,11 @@
     count = inputs[0].shape[0]
     for k, ref in enumerate(inputs):
         start = pl.multiple_of((lax.axis_index("pool") ^ k) * count, count)
-        out_ref[pl.ds(start, count), :] = ref[...]
-
-
-def arrange(blocks):
-    shape = (len(blocks) * blocks[0].shape[0], blocks[0].shape[1])
+        out_ref[pl.ds(start, count), :] = ref[:, : out_ref.shape[1]]
+
+
+def arrange(blocks, width):
+    shape = (len(blocks) * blocks[0].shape[0], width)
     outs = [jax.ShapeDtypeStruct(shape, BF16)]
     return call(arrange_kernel, "arrange", blocks, [VMEM] * len(blocks), outs, roomy=True)[0][0]
 
@@ -588,31 +581,28 @@
 
     if direct:
         axes = ("tp", "sub")
-        (*pieces, facts), (out_held,) = attend(
+        (*pieces, facts), _ = attend(
             queries,
             keys_cache,
             values_cache,
             lengths,
             (routes.T, route_weight.T),
             shards,
-            [(out_weight, None)],
+            [],
             False,
         )
         inputs = [pieces[0]] + [xor_permute(pieces[k], axes, shards, k) for k in range(1, shards)]
-        pairs = [(i, i ^ (shards * (i % shards))) for i in range(pools * shards) if i % shards]
-        other_facts = lax.ppermute(facts, ("pool", "tp", "sub"), pairs)
-        (kept, near, far, block), _ = project(inputs, [facts, other_facts], out_held, [], [])
+        (out_held,) = load([(out_weight, None)], [pieces[0]], "load_a")
+        kept, near, far = project(inputs, out_held)
         gate_1, up_1 = gate_2, up_2 = in_vmem(w_gate), in_vmem(w_up)
         gate_0, up_0 = load([gates[0], ups[0]], [near], "load_b")
-        blocks = [block]
-        for k in range(1, shards):
-            blocks.append(xor_permute(near if k < subs else far, axes, shards, k))
-        x_sum = add(kept, blocks[1:])
-        x_half, gate_0 = lax.optimization_barrier((x_sum, gate_0))
+        others = [
+            xor_permute(near if k < subs else far, axes, shards, k) for k in range(1, shards)
+        ]
+        x_half, gate_0 = lax.optimization_barrier((add(kept, facts, others), gate_0))
         xs = [x_half] + [xor_permute(x_half, "pool", pools, k) for k in range(1, pools)]
-        blocks, _ = lax.optimization_barrier((blocks, x_half))
         (slots, weights, largest), (pick, spread, slot_weight), _ = route(
-            blocks,
+            xs,
             expert_table,
             experts,
             rows,
@@ -687,7 +677,7 @@
     def more(state):
         k, total = state
         k, *held_x = lax.optimization_barrier((k, *xs))
-        x = arrange(held_x) if direct else held_x[0]
+        x = arrange(held_x, half_width) if direct else held_x[0]
         pick, spread, slot_weight = pick_slots(k * capacity, slots, weights, capacity)
         gate = jnp.einsum("rd,efd->erf", x, w_gate, preferred_element_type=F32)
         up = jnp.einsum("rd,efd->erf", x, w_up, preferred_element_type=F32)

time: 56.4 us -> 53.2 us (0.943)
  starting transfers between devices: 22.8 us -> 18.6 us
  Pallas kernels: 21.5 us -> 22.9 us
    ppermute x13, starting transfers between devices: 17.5 us -> 14.3 us  [xor_permute(): return lax.ppermute(value, axes, [(i, i ^ k) for i in range(count)])]
    pallas_call x13 -> x14, Pallas kernels: 21.5 us -> 22.9 us  [call(): pl.pallas_call(run, in_specs=list(specs) + [HBM] * count_load + [ANY] * l...]
    ppermute x3, starting transfers between devices: 4.6 us -> 3.2 us  [exchange(): return (value, lax.ppermute(value, 'tp', [(0, 1), (1, 0)]))]
    ppermute x1, starting transfers between devices: 0.08 us -> 1.04 us  [body(): theirs = lax.ppermute(theirs, 'tp', [(0, 1), (1, 0)])]
    ppermute x1 -> x0, starting transfers between devices: 0.65 us -> none  [body(): other_facts = lax.ppermute(facts, ('pool', 'tp', 'sub'), pairs)]
  transfers between devices with their start and end apart: 18 -> 17, of which waited for: 6 -> 5; matrix products, arithmetic and copies ran while one was open for 0% -> 0% of each run, Pallas kernels for 25% -> 30%
where the time goes in v5:
time: 53.2 us; the launch traced here: 53 us
  Pallas kernels  22.9 us (43%)
  starting transfers between devices  18.6 us (35%)
  waiting for transfers between devices  8.41 us (16%)
  between operations  1.59 us (3%)
  loops' own time  0.84 us (2%)
  other arithmetic  0.62 us (1%)
    pallas_call x14, Pallas kernels, call(): pl.pallas_call(run, in_specs=list(specs) + [HBM] * count_load + [ANY] * l...  22.9 us
    ppermute x13, starting transfers between devices, xor_permute(): return lax.ppermute(value, axes, [(i, i ^ k) for i in range(count)])  14.3 us
    ppermute x13, waiting for transfers between devices, xor_permute(): return lax.ppermute(value, axes, [(i, i ^ k) for i in range(count)])  7.9 us
    ppermute x3, starting transfers between devices, exchange(): return (value, lax.ppermute(value, 'tp', [(0, 1), (1, 0)]))  3.2 us
  transfers between devices with their start and end apart: 17, of which 5 were waited for; matrix products, arithmetic and copies ran while one was open for 0% of the time, Pallas kernels for 30%

profile of v5, /device:TPU:0, one launch (start us, length us, event | category | flops | bytes accessed | tf_op | source)
XLA Modules:
  0.0 53.0 jit_solution(13003719531359063167)
XLA Ops:
  0.6 2.3 %attention.1 = (bf16[4,1024]{1,0:T(4,128)(2,1)S(1)}, bf16[4,1024]{1,0:T(4,128)(2,1)S(1)}, bf16[4,1024]{1,0:T(4,128)(2,1)S(1)}, bf16[4,1024]{1,0:T(4,128)(2,1)S(1)}, bf16[16,128]{1,0:T(8,128)(2,1)S(1)}) custom-call(bf16[4,4096]{1,0:T(4,128)(2,1)} %refs_0_.3, s32[4]{0:T(128)} %refs_1_.2, s32[8,16]{1,0:T(8,128)} %bitcast.63, f32[8,16]{1,0:T(8,128)} %bitcast.64, ...), custom_call_target="tpu_custom_call" | custom-call | bytes 12000000 | tf_op jit(solution)/shard_map/attention/pallas_call | solution.py:105
  2.9 0.5 collective-permute-start.5
  3.4 2.6 %collective-permute-start.6 = (bf16[4,1024]{1,0:T(4,128)(2,1)S(1)}, bf16[4,1024]{1,0:T(4,128)(2,1)S(1)}, u32[]{:S(2)}, u32[]{:S(2)}) collective-permute-start(bf16[4,1024]{1,0:T(4,128)(2,1)S(1)} %get-tuple-element.116), channel_id=1, source_target_pairs={{0,2},{1,3},{2,0},{3,1},{4,6},{5,7},{6,4},{7,5},{8,10},{9,11},{10,... | collective-permute-start | bytes 24584 | tf_op jit(solution)/shard_map/ppermute | solution.py:549
  6.0 0.1 collective-permute-start.7
  6.1 2.2 %load_a.1.refs_4_ = bf16[1024,2048]{1,0:T(8,128)(2,1)S(1)} custom-call(bf16[1024,2048]{1,0:T(8,128)(2,1)} %refs_0_.4, bf16[4,1024]{1,0:T(4,128)(2,1)S(1)} %get-tuple-element.114.refs_1_.refs_0_), custom_call_target="tpu_custom_call" | custom-call | bytes 6000000 | tf_op jit(solution)/shard_map/load_a/pallas_call | solution.py:105
  8.3 0.0 collective-permute-done.5.refs_1_
  8.3 0.0 collective-permute-done.6.refs_2_
  8.3 0.8 %collective-permute-done.7.refs_3_ = bf16[4,1024]{1,0:T(4,128)(2,1)S(1)} collective-permute-done((bf16[4,1024]{1,0:T(4,128)(2,1)S(1)}, bf16[4,1024]{1,0:T(4,128)(2,1)S(1)}, u32[]{:S(2)}, u32[]{:S(2)}) %collective-permute-start.7) | collective-permute-done | bytes 8224 | tf_op jit(solution)/shard_map/ppermute | solution.py:549
  9.1 0.0 slice-start.3
  9.1 0.0 slice-start.6
  9.1 0.7 %project.1 = (f32[16,1024]{1,0:T(8,128)S(1)}, bf16[16,1024]{1,0:T(8,128)(2,1)S(1)}, bf16[16,1024]{1,0:T(8,128)(2,1)S(1)}) custom-call(bf16[4,1024]{1,0:T(4,128)(2,1)S(1)} %get-tuple-element.114.refs_1_.refs_0_, bf16[4,1024]{1,0:T(4,128)(2,1)S(1)} %collective-permute-done.5.refs_1_, bf16[4,1024]{1,0:T(4,128)(2,1)S(1)} %collective-permute-done.6.refs_2_, ...), custom_call_target="tpu_custom_call" | custom-call | bytes 6000000 | tf_op jit(solution)/shard_map/project/pallas_call | solution.py:105
  9.8 0.9 %collective-permute-start.10 = (bf16[16,1024]{1,0:T(8,128)(2,1)S(1)}, bf16[16,1024]{1,0:T(8,128)(2,1)S(1)}, u32[]{:S(2)}, u32[]{:S(2)}) collective-permute-start(bf16[16,1024]{1,0:T(8,128)(2,1)S(1)} %get-tuple-element.121), channel_id=1, source_target_pairs={{0,3},{1,2},{2,1},{3,0},{4,7},{5,6},{6,5},{7,4},{8,11},{9,10},{10,... | collective-permute-start | bytes 98312 | tf_op jit(solution)/shard_map/ppermute | solution.py:549
  10.8 0.0 slice-start.8
  10.8 0.2 collective-permute-start.8
  11.0 1.0 %collective-permute-start.9 = (bf16[16,1024]{1,0:T(8,128)(2,1)S(1)}, bf16[16,1024]{1,0:T(8,128)(2,1)S(1)}, u32[]{:S(2)}, u32[]{:S(2)}) collective-permute-start(bf16[16,1024]{1,0:T(8,128)(2,1)S(1)} %get-tuple-element.121), channel_id=1, source_target_pairs={{0,2},{1,3},{2,0},{3,1},{4,6},{5,7},{6,4},{7,5},{8,10},{9,11},{10,... | collective-permute-start | bytes 98312 | tf_op jit(solution)/shard_map/ppermute | solution.py:549
  12.1 4.2 %load_b.1 = (bf16[16,128,1024]{2,1,0:T(8,128)(2,1)S(1)}, bf16[16,128,1024]{2,1,0:T(8,128)(2,1)S(1)}) custom-call(bf16[16,384,1024]{2,1,0:T(8,128)(2,1)} %refs_2_.3, bf16[16,384,1024]{2,1,0:T(8,128)(2,1)} %refs_3_.3, bf16[16,1024]{1,0:T(8,128)(2,1)S(1)} %get-tuple-element.120.refs_2_), custom_call_target="tpu_custom_call" | custom-call | bytes 12000000 | tf_op jit(solution)/shard_map/load_b/pallas_call | solution.py:105
  16.3 0.0 collective-permute-done.10.refs_4_
  16.3 0.0 collective-permute-done.8.refs_2_
  16.3 0.0 collective-permute-done.9.refs_3_
  16.4 1.6 %collective-permute-start.11 = (bf16[16,1152]{1,0:T(8,128)(2,1)S(1)}, bf16[16,1152]{1,0:T(8,128)(2,1)S(1)}, u32[]{:S(2)}, u32[]{:S(2)}) collective-permute-start(bf16[16,1152]{1,0:T(8,128)(2,1)S(1)} %add.65.refs_1_.refs_0_), channel_id=1, source_target_pairs={{0,4},{4,0},{8,12},{12,8},{1,5},{5,1},{9,13},{13,9},{2,6},{6,2},{1... | collective-permute-start | bytes 110600 | tf_op jit(solution)/shard_map/ppermute | solution.py:549
  18.0 2.6 %collective-permute-start.12 = (bf16[16,1152]{1,0:T(8,128)(2,1)S(1)}, bf16[16,1152]{1,0:T(8,128)(2,1)S(1)}, u32[]{:S(2)}, u32[]{:S(2)}) collective-permute-start(bf16[16,1152]{1,0:T(8,128)(2,1)S(1)} %add.65.refs_1_.refs_0_), channel_id=1, source_target_pairs={{0,8},{4,12},{8,0},{12,4},{1,9},{5,13},{9,1},{13,5},{2,10},{6,14},... | collective-permute-start | bytes 110600 | tf_op jit(solution)/shard_map/ppermute | solution.py:549
  20.6 0.2 collective-permute-start.13
  20.8 0.0 collective-permute-done.11.refs_2_.refs_1_
  20.8 2.8 %collective-permute-done.12.refs_3_.refs_2_ = bf16[16,1152]{1,0:T(8,128)(2,1)S(1)} collective-permute-done((bf16[16,1152]{1,0:T(8,128)(2,1)S(1)}, bf16[16,1152]{1,0:T(8,128)(2,1)S(1)}, u32[]{:S(2)}, u32[]{:S(2)}) %collective-permute-start.12) | collective-permute-done | bytes 36896 | tf_op jit(solution)/shard_map/ppermute | solution.py:549
  23.6 2.8 %collective-permute-done.13.refs_4_.refs_3_ = bf16[16,1152]{1,0:T(8,128)(2,1)S(1)} collective-permute-done((bf16[16,1152]{1,0:T(8,128)(2,1)S(1)}, bf16[16,1152]{1,0:T(8,128)(2,1)S(1)}, u32[]{:S(2)}, u32[]{:S(2)}) %collective-permute-start.13) | collective-permute-done | bytes 36896 | tf_op jit(solution)/shard_map/ppermute | solution.py:549
  26.4 0.0 copy-done.1
  26.4 0.9 %route.1 = (s32[4,1,256]{2,1,0:T(1,128)S(1)}, f32[4,1,256]{2,1,0:T(1,128)S(1)}, s32[1,1]{1,0:T(1,128)}, bf16[208,1024]{1,0:T(8,128)(2,1)S(1)}, bf16[1024,208]{1,0:T(8,128)(2,1)S(1)}, /*index=5*/f32[208,1]{1,0:T(8,128)S(1)}) custom-call(s32[1,64]{1,0:T(1,128)S(1)} %bitcast.59, bf16[16,1152]{1,0:T(8,128)(2,1)S(1)} %add.65.refs_1_.refs_0_, ...), custom_call_target="tpu_custom_call" | custom-call | bytes 18000000 | tf_op jit(solution)/shard_map/route/pallas_call | solution.py:105
  27.3 3.1 %gate_up_0.1 = (bf16[208,256]{1,0:T(8,128)(2,1)S(1)}, bf16[1024,64]{1,0:T(8,128)(2,1)S(1)}, bf16[4,1024]{1,0:T(4,128)(2,1)S(1)}, bf16[4,1024]{1,0:T(4,128)(2,1)S(1)}) custom-call(bf16[16,1152]{1,0:T(8,128)(2,1)S(1)} %add.65.refs_1_.refs_0_, bf16[16,1152]{1,0:T(8,128)(2,1)S(1)} %collective-permute-done.11.refs_2_.refs_1_, ...), custom_call_target="tpu_custom_call" | custom-call | bytes 12000000 | tf_op jit(solution)/shard_map/gate_up_0/pallas_call | solution.py:105
  30.3 1.0 %collective-permute-start.17 = (bf16[208,256]{1,0:T(8,128)(2,1)S(1)}, bf16[208,256]{1,0:T(8,128)(2,1)S(1)}, u32[]{:S(2)}, u32[]{:S(2)}) collective-permute-start(bf16[208,256]{1,0:T(8,128)(2,1)S(1)} %get-tuple-element.130.refs_4_.refs_0_), channel_id=1, source_target_pairs={{0,2},{2,0},{1,3},{3,1},{4,6},{6,4},{5,7},{7,5},{8,10},{10,8},{9,1... | collective-permute-start | bytes 319496 | tf_op jit(solution)/shard_map/ppermute | solution.py:660
  31.4 0.0 slice-done.3
  31.4 0.0 slice-done.6
  31.4 0.0 slice-done.4
  31.4 0.0 slice-done.5
  31.4 0.0 slice-done.7
  31.4 0.0 slice-done.8
  31.4 0.0 slice-start
  31.5 0.0 slice-start.1
  31.5 2.8 %gate_up_1.1.refs_4_.refs_0_ = bf16[208,256]{1,0:T(8,128)(2,1)S(1)} custom-call(bf16[1024,64]{1,0:T(8,128)(2,1)S(1)} %get-tuple-element.129.refs_0_, bf16[208,1024]{1,0:T(8,128)(2,1)S(1)} %get-tuple-element.124.refs_4_.refs_1_, bf16[16,384,1024]{2,1,0:T(8,128)(2,1)S(1)} %bitcast.56, bf16[16,384,1024]{2,1,0:T(8,128)(2,1)S(1)} %bitcast.58, ...), custom_call_target="tpu_custom_call" | custom-call | bytes 12000000 | tf_op jit(solution)/shard_map/gate_up_1/pallas_call | solution.py:105
  34.3 0.0 slice-start.2
  34.3 1.1 %collective-permute-start.16 = (bf16[208,256]{1,0:T(8,128)(2,1)S(1)}, bf16[208,256]{1,0:T(8,128)(2,1)S(1)}, u32[]{:S(2)}, u32[]{:S(2)}) collective-permute-start(bf16[208,256]{1,0:T(8,128)(2,1)S(1)} %gate_up_1.1.refs_4_.refs_0_), channel_id=1, source_target_pairs={{0,2},{2,0},{1,3},{3,1},{4,6},{6,4},{5,7},{7,5},{8,10},{10,8},{9,1... | collective-permute-start | bytes 319496 | tf_op jit(solution)/shard_map/ppermute | solution.py:660
  35.4 2.8 %gate_up_2.1.refs_0_ = bf16[208,256]{1,0:T(8,128)(2,1)S(1)} custom-call(bf16[1024,64]{1,0:T(8,128)(2,1)S(1)} %get-tuple-element.129.refs_0_, bf16[208,1024]{1,0:T(8,128)(2,1)S(1)} %get-tuple-element.124.refs_4_.refs_1_, bf16[16,384,1024]{2,1,0:T(8,128)(2,1)S(1)} %bitcast.56, bf16[16,384,1024]{2,1,0:T(8,128)(2,1)S(1)} %bitcast.58, ...), custom_call_target="tpu_custom_call" | custom-call | bytes 12000000 | tf_op jit(solution)/shard_map/gate_up_2/pallas_call | solution.py:105
  38.2 1.0 %collective-permute-start.15 = (bf16[208,256]{1,0:T(8,128)(2,1)S(1)}, bf16[208,256]{1,0:T(8,128)(2,1)S(1)}, u32[]{:S(2)}, u32[]{:S(2)}) collective-permute-start(bf16[208,256]{1,0:T(8,128)(2,1)S(1)} %gate_up_2.1.refs_0_), channel_id=1, source_target_pairs={{0,2},{2,0},{1,3},{3,1},{4,6},{6,4},{5,7},{7,5},{8,10},{10,8},{9,1... | collective-permute-start | bytes 319496 | tf_op jit(solution)/shard_map/ppermute | solution.py:660
  39.3 1.0 %collective-permute-start.14 = (bf16[4,1024]{1,0:T(4,128)(2,1)S(1)}, bf16[4,1024]{1,0:T(4,128)(2,1)S(1)}, u32[]{:S(2)}, u32[]{:S(2)}) collective-permute-start(bf16[4,1024]{1,0:T(4,128)(2,1)S(1)} %get-tuple-element.131), channel_id=1, source_target_pairs={{0,2},{2,0},{1,3},{3,1},{4,6},{6,4},{5,7},{7,5},{8,10},{10,8},{9,1... | collective-permute-start | bytes 24584 | tf_op jit(solution)/shard_map/ppermute | solution.py:625
  40.3 0.0 collective-permute-done.17.refs_1_
  40.3 0.0 slice-done
  40.3 0.0 slice-done.1
  40.3 0.0 slice-done.2
  40.4 1.1 %down_0.1.refs_5_ = f32[64,1024]{1,0:T(8,128)S(1)} custom-call(bf16[208,256]{1,0:T(8,128)(2,1)S(1)} %get-tuple-element.130.refs_4_.refs_0_, bf16[208,256]{1,0:T(8,128)(2,1)S(1)} %collective-permute-done.17.refs_1_, f32[208,1]{1,0:T(8,128)S(1)} %get-tuple-element.133.refs_2_, bf16[1024,208]{1,0:T(8,128)(2,1)S(1)} %get-tuple-element.134.refs_3_, ...), custom_call_target="tpu_custom_call" | custom-call | bytes 9000000 | tf_op jit(solution)/shard_map/down_0/pallas_call | solution.py:105
  41.4 0.0 collective-permute-done.16.refs_1_
  41.4 1.1 %down_1.1.refs_5_ = f32[64,1024]{1,0:T(8,128)S(1)} custom-call(bf16[208,256]{1,0:T(8,128)(2,1)S(1)} %gate_up_1.1.refs_4_.refs_0_, bf16[208,256]{1,0:T(8,128)(2,1)S(1)} %collective-permute-done.16.refs_1_, f32[208,1]{1,0:T(8,128)S(1)} %get-tuple-element.133.refs_2_, bf16[1024,208]{1,0:T(8,128)(2,1)S(1)} %get-tuple-element.134.refs_3_, ...), custom_call_target="tpu_custom_call" | custom-call | bytes 9000000 | tf_op jit(solution)/shard_map/down_1/pallas_call | solution.py:105
  42.5 0.5 collective-permute-done.15.refs_1_
  43.0 1.1 %down_2.1 = (f32[64,512]{1,0:T(8,128)S(1)}, f32[64,512]{1,0:T(8,128)S(1)}) custom-call(bf16[208,256]{1,0:T(8,128)(2,1)S(1)} %gate_up_2.1.refs_0_, bf16[208,256]{1,0:T(8,128)(2,1)S(1)} %collective-permute-done.15.refs_1_, f32[208,1]{1,0:T(8,128)S(1)} %get-tuple-element.133.refs_2_, bf16[1024,208]{1,0:T(8,128)(2,1)S(1)} %get-tuple-element.134.refs_3_, ...), custom_call_target="tpu_custom_call" | custom-call | bytes 9000000 | tf_op jit(solution)/shard_map/down_2/pallas_call | solution.py:105
  44.1 0.0 collective-permute-done.14.refs_1_
  44.1 0.1 collective-permute-start.18
  44.8 0.8 %while.10 = (s32[]{:T(128)}, f32[16,512]{1,0:T(8,128)S(1)}, s32[1,1]{1,0:T(1,128)}, bf16[16,1152]{1,0:T(8,128)(2,1)S(1)}, bf16[16,1152]{1,0:T(8,128)(2,1)S(1)}, ...) while((s32[]{:T(128)}, f32[16,512]{1,0:T(8,128)S(1)}, ...), condition=%wide.region_1.2_spmd, body=%wide.region_0.1_spmd.sunk | while | flops 2912233472 | bytes 122560848 | solution.py:708
  45.7 0.0 collective-permute-done.18.refs_1_
  45.7 0.1 collective-permute-start.19
  45.8 1.1 %collective-permute-start.20 = (bf16[16,512]{1,0:T(8,128)(2,1)S(1)}, bf16[16,512]{1,0:T(8,128)(2,1)S(1)}, u32[]{:S(2)}, u32[]{:S(2)}) collective-permute-start(bf16[16,512]{1,0:T(8,128)(2,1)S(1)} %get-tuple-element.147), channel_id=1, source_target_pairs={{0,8},{4,12},{8,0},{12,4},{1,9},{5,13},{9,1},{13,5},{2,10},{6,14},... | collective-permute-start | bytes 49160 | tf_op jit(solution)/shard_map/ppermute | solution.py:549
  46.9 3.3 %collective-permute-start.21 = (bf16[16,512]{1,0:T(8,128)(2,1)S(1)}, bf16[16,512]{1,0:T(8,128)(2,1)S(1)}, u32[]{:S(2)}, u32[]{:S(2)}) collective-permute-start(bf16[16,512]{1,0:T(8,128)(2,1)S(1)} %get-tuple-element.148), channel_id=1, source_target_pairs={{0,12},{4,8},{8,4},{12,0},{1,13},{5,9},{9,5},{13,1},{2,14},{6,10},... | collective-permute-start | bytes 49160 | tf_op jit(solution)/shard_map/ppermute | solution.py:549
  50.2 0.6 %join.1 = bf16[4,2048]{1,0:T(4,128)(2,1)} custom-call(bf16[4,1024]{1,0:T(4,128)(2,1)S(1)} %get-tuple-element.127.refs_0_, bf16[4,1024]{1,0:T(4,128)(2,1)S(1)} %collective-permute-done.14.refs_1_), custom_call_target="tpu_custom_call" | custom-call | bytes 6000000 | tf_op jit(solution)/shard_map/join/pallas_call | solution.py:105
  50.8 0.0 collective-permute-done.19
  50.8 0.0 collective-permute-done.20
  50.8 1.6 %collective-permute-done.21 = bf16[16,512]{1,0:T(8,128)(2,1)S(1)} collective-permute-done((bf16[16,512]{1,0:T(8,128)(2,1)S(1)}, bf16[16,512]{1,0:T(8,128)(2,1)S(1)}, u32[]{:S(2)}, u32[]{:S(2)}) %collective-permute-start.21) | collective-permute-done | bytes 16416 | tf_op jit(solution)/shard_map/ppermute | solution.py:549
  52.4 0.6 %add_convert_fusion = bf16[16,512]{1,0:T(8,128)(2,1)} fusion(f32[16,512]{1,0:T(8,128)S(1)} %get-tuple-element.149, bf16[16,512]{1,0:T(8,128)(2,1)S(1)} %collective-permute-done.21, bf16[16,512]{1,0:T(8,128)(2,1)S(1)} %collective-permute-done.20, f32[16,512]{1,0:T(8,128)S(1)} %get-tuple-element.145, bf16[16,512]{1,0:T(8,128)(2,1)S(1)} %collective-permute-done.19), kind=kLoop, calls=%fused_computation.20 | loop fusion | flops 65536 | bytes 131072 | tf_op jit(solution)/shard_map/convert_element_type | solution.py:714
  (10 shorter events, 0.1 us)
Async XLA Ops:
  2.9 5.4 %collective-permute-start.5 = (bf16[4,1024]{1,0:T(4,128)(2,1)S(1)}, bf16[4,1024]{1,0:T(4,128)(2,1)S(1)}, u32[]{:S(2)}, u32[]{:S(2)}) collective-permute-start(bf16[4,1024]{1,0:T(4,128)(2,1)S(1)} %get-tuple-element.115), channel_id=1, source_target_pairs={{0,1},{1,0},{2,3},{3,2},{4,5},{5,4},{6,7},{7,6},{8,9},{9,8},{10,11... | collective-permute-start | bytes 24584 | tf_op jit(solution)/shard_map/ppermute | solution.py:549
  3.4 4.9 %collective-permute-start.6 = (bf16[4,1024]{1,0:T(4,128)(2,1)S(1)}, bf16[4,1024]{1,0:T(4,128)(2,1)S(1)}, u32[]{:S(2)}, u32[]{:S(2)}) collective-permute-start(bf16[4,1024]{1,0:T(4,128)(2,1)S(1)} %get-tuple-element.116), channel_id=1, source_target_pairs={{0,2},{1,3},{2,0},{3,1},{4,6},{5,7},{6,4},{7,5},{8,10},{9,11},{10,... | collective-permute-start | bytes 24584 | tf_op jit(solution)/shard_map/ppermute | solution.py:549
  6.0 3.1 %collective-permute-start.7 = (bf16[4,1024]{1,0:T(4,128)(2,1)S(1)}, bf16[4,1024]{1,0:T(4,128)(2,1)S(1)}, u32[]{:S(2)}, u32[]{:S(2)}) collective-permute-start(bf16[4,1024]{1,0:T(4,128)(2,1)S(1)} %get-tuple-element.117), channel_id=1, source_target_pairs={{0,3},{1,2},{2,1},{3,0},{4,7},{5,6},{6,5},{7,4},{8,11},{9,10},{10,... | collective-permute-start | bytes 24584 | tf_op jit(solution)/shard_map/ppermute | solution.py:549
  9.1 22.3 %slice-start.3 = ((s8[12582912]{0:T(1024)(128)(4,1)}), s8[4194304]{0:T(1024)(128)(4,1)S(1)}, s32[]{:S(2)}) async-start(s8[12582912]{0:T(1024)(128)(4,1)} %bitcast.55), calls=%async_computation.3 | async-start | bytes 8388608
  9.1 22.3 %slice-start.6 = ((s8[12582912]{0:T(1024)(128)(4,1)}), s8[4194304]{0:T(1024)(128)(4,1)S(1)}, s32[]{:S(2)}) async-start(s8[12582912]{0:T(1024)(128)(4,1)} %bitcast.57), calls=%async_computation.6 | async-start | bytes 8388608
  9.8 6.5 %collective-permute-start.10 = (bf16[16,1024]{1,0:T(8,128)(2,1)S(1)}, bf16[16,1024]{1,0:T(8,128)(2,1)S(1)}, u32[]{:S(2)}, u32[]{:S(2)}) collective-permute-start(bf16[16,1024]{1,0:T(8,128)(2,1)S(1)} %get-tuple-element.121), channel_id=1, source_target_pairs={{0,3},{1,2},{2,1},{3,0},{4,7},{5,6},{6,5},{7,4},{8,11},{9,10},{10,... | collective-permute-start | bytes 98312 | tf_op jit(solution)/shard_map/ppermute | solution.py:549
  10.8 15.6 %copy-start.1 = (s32[64]{0:T(128)S(1)}, s32[64]{0:T(128)}, u32[]{:S(2)}) copy-start(s32[64]{0:T(128)} %param.20) | copy-start | bytes 772
  10.8 20.6 %slice-start.4 = ((s8[12582912]{0:T(1024)(128)(4,1)}), s8[4194304]{0:T(1024)(128)(4,1)S(1)}, s32[]{:S(2)}) async-start(s8[12582912]{0:T(1024)(128)(4,1)} %bitcast.55), calls=%async_computation.4 | async-start | bytes 8388608
  10.8 20.6 %slice-start.5 = ((s8[12582912]{0:T(1024)(128)(4,1)}), s8[4194304]{0:T(1024)(128)(4,1)S(1)}, s32[]{:S(2)}) async-start(s8[12582912]{0:T(1024)(128)(4,1)} %bitcast.55), calls=%async_computation.5 | async-start | bytes 8388608
  10.8 20.6 %slice-start.7 = ((s8[12582912]{0:T(1024)(128)(4,1)}), s8[4194304]{0:T(1024)(128)(4,1)S(1)}, s32[]{:S(2)}) async-start(s8[12582912]{0:T(1024)(128)(4,1)} %bitcast.57), calls=%async_computation.7 | async-start | bytes 8388608
  10.8 20.6 %slice-start.8 = ((s8[12582912]{0:T(1024)(128)(4,1)}), s8[4194304]{0:T(1024)(128)(4,1)S(1)}, s32[]{:S(2)}) async-start(s8[12582912]{0:T(1024)(128)(4,1)} %bitcast.57), calls=%async_computation.8 | async-start | bytes 8388608
  10.8 5.5 %collective-permute-start.8 = (bf16[16,1024]{1,0:T(8,128)(2,1)S(1)}, bf16[16,1024]{1,0:T(8,128)(2,1)S(1)}, u32[]{:S(2)}, u32[]{:S(2)}) collective-permute-start(bf16[16,1024]{1,0:T(8,128)(2,1)S(1)} %get-tuple-element.120.refs_2_), channel_id=1, source_target_pairs={{0,1},{1,0},{2,3},{3,2},{4,5},{5,4},{6,7},{7,6},{8,9},{9,8},{10,11... | collective-permute-start | bytes 98312 | tf_op jit(solution)/shard_map/ppermute | solution.py:549
  11.0 5.3 %collective-permute-start.9 = (bf16[16,1024]{1,0:T(8,128)(2,1)S(1)}, bf16[16,1024]{1,0:T(8,128)(2,1)S(1)}, u32[]{:S(2)}, u32[]{:S(2)}) collective-permute-start(bf16[16,1024]{1,0:T(8,128)(2,1)S(1)} %get-tuple-element.121), channel_id=1, source_target_pairs={{0,2},{1,3},{2,0},{3,1},{4,6},{5,7},{6,4},{7,5},{8,10},{9,11},{10,... | collective-permute-start | bytes 98312 | tf_op jit(solution)/shard_map/ppermute | solution.py:549
  16.4 4.5 %collective-permute-start.11 = (bf16[16,1152]{1,0:T(8,128)(2,1)S(1)}, bf16[16,1152]{1,0:T(8,128)(2,1)S(1)}, u32[]{:S(2)}, u32[]{:S(2)}) collective-permute-start(bf16[16,1152]{1,0:T(8,128)(2,1)S(1)} %add.65.refs_1_.refs_0_), channel_id=1, source_target_pairs={{0,4},{4,0},{8,12},{12,8},{1,5},{5,1},{9,13},{13,9},{2,6},{6,2},{1... | collective-permute-start | bytes 110600 | tf_op jit(solution)/shard_map/ppermute | solution.py:549
  18.0 5.6 %collective-permute-start.12 = (bf16[16,1152]{1,0:T(8,128)(2,1)S(1)}, bf16[16,1152]{1,0:T(8,128)(2,1)S(1)}, u32[]{:S(2)}, u32[]{:S(2)}) collective-permute-start(bf16[16,1152]{1,0:T(8,128)(2,1)S(1)} %add.65.refs_1_.refs_0_), channel_id=1, source_target_pairs={{0,8},{4,12},{8,0},{12,4},{1,9},{5,13},{9,1},{13,5},{2,10},{6,14},... | collective-permute-start | bytes 110600 | tf_op jit(solution)/shard_map/ppermute | solution.py:549
  20.6 5.8 %collective-permute-start.13 = (bf16[16,1152]{1,0:T(8,128)(2,1)S(1)}, bf16[16,1152]{1,0:T(8,128)(2,1)S(1)}, u32[]{:S(2)}, u32[]{:S(2)}) collective-permute-start(bf16[16,1152]{1,0:T(8,128)(2,1)S(1)} %add.65.refs_1_.refs_0_), channel_id=1, source_target_pairs={{0,12},{4,8},{8,4},{12,0},{1,13},{5,9},{9,5},{13,1},{2,14},{6,10},... | collective-permute-start | bytes 110600 | tf_op jit(solution)/shard_map/ppermute | solution.py:549
  30.3 10.0 %collective-permute-start.17 = (bf16[208,256]{1,0:T(8,128)(2,1)S(1)}, bf16[208,256]{1,0:T(8,128)(2,1)S(1)}, u32[]{:S(2)}, u32[]{:S(2)}) collective-permute-start(bf16[208,256]{1,0:T(8,128)(2,1)S(1)} %get-tuple-element.130.refs_4_.refs_0_), channel_id=1, source_target_pairs={{0,2},{2,0},{1,3},{3,1},{4,6},{6,4},{5,7},{7,5},{8,10},{10,8},{9,1... | collective-permute-start | bytes 319496 | tf_op jit(solution)/shard_map/ppermute | solution.py:660
  31.4 8.9 %slice-start = ((s8[12582912]{0:T(1024)(128)(4,1)}), s8[4194304]{0:T(1024)(128)(4,1)S(1)}, s32[]{:S(2)}) async-start(s8[12582912]{0:T(1024)(128)(4,1)} %bitcast.53), calls=%async_computation | async-start | bytes 8388608
  31.5 8.9 %slice-start.1 = ((s8[12582912]{0:T(1024)(128)(4,1)}), s8[4194304]{0:T(1024)(128)(4,1)S(1)}, s32[]{:S(2)}) async-start(s8[12582912]{0:T(1024)(128)(4,1)} %bitcast.53), calls=%async_computation.1 | async-start | bytes 8388608
  34.3 6.1 %slice-start.2 = ((s8[12582912]{0:T(1024)(128)(4,1)}), s8[4194304]{0:T(1024)(128)(4,1)S(1)}, s32[]{:S(2)}) async-start(s8[12582912]{0:T(1024)(128)(4,1)} %bitcast.53), calls=%async_computation.2 | async-start | bytes 8388608
  34.3 7.1 %collective-permute-start.16 = (bf16[208,256]{1,0:T(8,128)(2,1)S(1)}, bf16[208,256]{1,0:T(8,128)(2,1)S(1)}, u32[]{:S(2)}, u32[]{:S(2)}) collective-permute-start(bf16[208,256]{1,0:T(8,128)(2,1)S(1)} %gate_up_1.1.refs_4_.refs_0_), channel_id=1, source_target_pairs={{0,2},{2,0},{1,3},{3,1},{4,6},{6,4},{5,7},{7,5},{8,10},{10,8},{9,1... | collective-permute-start | bytes 319496 | tf_op jit(solution)/shard_map/ppermute | solution.py:660
  38.2 4.8 %collective-permute-start.15 = (bf16[208,256]{1,0:T(8,128)(2,1)S(1)}, bf16[208,256]{1,0:T(8,128)(2,1)S(1)}, u32[]{:S(2)}, u32[]{:S(2)}) collective-permute-start(bf16[208,256]{1,0:T(8,128)(2,1)S(1)} %gate_up_2.1.refs_0_), channel_id=1, source_target_pairs={{0,2},{2,0},{1,3},{3,1},{4,6},{6,4},{5,7},{7,5},{8,10},{10,8},{9,1... | collective-permute-start | bytes 319496 | tf_op jit(solution)/shard_map/ppermute | solution.py:660
  39.3 4.8 %collective-permute-start.14 = (bf16[4,1024]{1,0:T(4,128)(2,1)S(1)}, bf16[4,1024]{1,0:T(4,128)(2,1)S(1)}, u32[]{:S(2)}, u32[]{:S(2)}) collective-permute-start(bf16[4,1024]{1,0:T(4,128)(2,1)S(1)} %get-tuple-element.131), channel_id=1, source_target_pairs={{0,2},{2,0},{1,3},{3,1},{4,6},{6,4},{5,7},{7,5},{8,10},{10,8},{9,1... | collective-permute-start | bytes 24584 | tf_op jit(solution)/shard_map/ppermute | solution.py:625
  44.1 1.6 %collective-permute-start.18 = (f32[64,512]{1,0:T(8,128)S(1)}, f32[64,512]{1,0:T(8,128)S(1)}, u32[]{:S(2)}, u32[]{:S(2)}) collective-permute-start(f32[64,512]{1,0:T(8,128)S(1)} %get-tuple-element.139), channel_id=1, source_target_pairs={{0,1},{1,0},{2,3},{3,2},{4,5},{5,4},{6,7},{7,6},{8,9},{9,8},{10,11... | collective-permute-start | bytes 393224 | tf_op jit(solution)/shard_map/ppermute | solution.py:549
  45.7 5.1 %collective-permute-start.19 = (bf16[16,512]{1,0:T(8,128)(2,1)S(1)}, bf16[16,512]{1,0:T(8,128)(2,1)S(1)}, u32[]{:S(2)}, u32[]{:S(2)}) collective-permute-start(bf16[16,512]{1,0:T(8,128)(2,1)S(1)} %get-tuple-element.146), channel_id=1, source_target_pairs={{0,4},{4,0},{8,12},{12,8},{1,5},{5,1},{9,13},{13,9},{2,6},{6,2},{1... | collective-permute-start | bytes 49160 | tf_op jit(solution)/shard_map/ppermute | solution.py:549
  45.8 5.0 %collective-permute-start.20 = (bf16[16,512]{1,0:T(8,128)(2,1)S(1)}, bf16[16,512]{1,0:T(8,128)(2,1)S(1)}, u32[]{:S(2)}, u32[]{:S(2)}) collective-permute-start(bf16[16,512]{1,0:T(8,128)(2,1)S(1)} %get-tuple-element.147), channel_id=1, source_target_pairs={{0,8},{4,12},{8,0},{12,4},{1,9},{5,13},{9,1},{13,5},{2,10},{6,14},... | collective-permute-start | bytes 49160 | tf_op jit(solution)/shard_map/ppermute | solution.py:549
  46.9 5.5 %collective-permute-start.21 = (bf16[16,512]{1,0:T(8,128)(2,1)S(1)}, bf16[16,512]{1,0:T(8,128)(2,1)S(1)}, u32[]{:S(2)}, u32[]{:S(2)}) collective-permute-start(bf16[16,512]{1,0:T(8,128)(2,1)S(1)} %get-tuple-element.148), channel_id=1, source_target_pairs={{0,12},{4,8},{8,4},{12,0},{1,13},{5,9},{9,5},{13,1},{2,14},{6,10},... | collective-permute-start | bytes 49160 | tf_op jit(solution)/shard_map/ppermute | solution.py:549

commit v6 on v5

--- a/solution.py
+++ b/solution.py
@@ -53,6 +53,10 @@
     tp, sub = lax.axis_index("tp"), lax.axis_index("sub")
     subs = lax.axis_size("sub")
     return tp * subs + sub, tp, sub, lax.axis_index("pool"), subs
+
+
+def far_first(k, count):
+    return (count - k) % count
 
 
 def call(kernel, name, inputs, specs, outs, out_specs=None, scratch=(), loads=(), anchors=(), us=2, roomy=False, begins=False):
@@ -215,14 +219,14 @@
 
 def route_kernel(table_ref, *refs, sources, experts, top):
     where = position()
-    given, (slot_ref, weight_ref, largest_ref, *picks, held) = refs[:sources], refs[sources:]
+    given, (slot_ref, weight_ref, largest_ref, extra_ref, *picks, held) = refs[:sources], refs[sources:]
     pools, pool_rows, lanes = held.shape
     if sources == 1:
         held[...] = given[0][...].astype(F32)
     else:
         for k in range(sources):
             width = given[k].shape[1]
-            held[where[3] ^ k] = given[k][:, width - lanes :].astype(F32)
+            held[where[3] ^ far_first(k, sources)] = given[k][:, width - lanes :].astype(F32)
     rows = pools * pool_rows
     total = table_ref.shape[1]
     groups, _, lanes = slot_ref.shape
@@ -239,6 +243,7 @@
     inside = jnp.where((entry >= first) & (entry < first + experts), 1.0, 0.0)
     loads = jnp.sum(inside, axis=1, keepdims=True)
     largest_ref[...] = jnp.max(loads, axis=0, keepdims=True).astype(jnp.int32)
+    extra_ref[...] = largest_ref[...] - picks[0].shape[0]
 
     lane = lax.broadcasted_iota(jnp.int32, (groups, lanes), 1)
     block = lax.broadcasted_iota(jnp.int32, (groups, lanes), 0)
@@ -302,6 +307,7 @@
             jax.ShapeDtypeStruct(shape, jnp.int32),
             jax.ShapeDtypeStruct(shape, F32),
             jax.ShapeDtypeStruct((1, 1), jnp.int32),
+            jax.ShapeDtypeStruct((1, 1), jnp.int32),
             *pick_shapes(capacity, experts * rows),
         ],
         scratch=[pltpu.VMEM((pools, rows // pools, FACT_LANES), F32)],
@@ -309,7 +315,7 @@
         us=6,
         roomy=roomy,
     )
-    return results[:3], results[3:], held
+    return results[:4], results[4:], held
 
 
 def pick_slots(shift, slots, weights, capacity):
@@ -388,7 +394,9 @@
             chosen = jnp.where(place == row + shard * own_rows, 1.0, 0.0).astype(BF16)
             out[...] = dot_nn(chosen, inputs[0][:, : x.shape[1]]).astype(BF16)
         for k in range(sources):
-            start = pl.multiple_of((where[3] ^ k) * count, count) if sources > 1 else 0
+            start = 0
+            if sources > 1:
+                start = pl.multiple_of((where[3] ^ far_first(k, sources)) * count, count)
             x[pl.ds(start, count), :] = inputs[k][:, : x.shape[1]].astype(F32)
         columns_ref[...] = x[...].T.astype(BF16)
     else:
@@ -479,7 +487,7 @@
     inputs, out_ref = refs[:-1], refs[-1]
     count = inputs[0].shape[0]
     for k, ref in enumerate(inputs):
-        start = pl.multiple_of((lax.axis_index("pool") ^ k) * count, count)
+        start = pl.multiple_of((lax.axis_index("pool") ^ far_first(k, len(inputs))) * count, count)
         out_ref[pl.ds(start, count), :] = ref[:, : out_ref.shape[1]]
 
 
@@ -600,8 +608,10 @@
             xor_permute(near if k < subs else far, axes, shards, k) for k in range(1, shards)
         ]
         x_half, gate_0 = lax.optimization_barrier((add(kept, facts, others), gate_0))
-        xs = [x_half] + [xor_permute(x_half, "pool", pools, k) for k in range(1, pools)]
-        (slots, weights, largest), (pick, spread, slot_weight), _ = route(
+        xs = [x_half]
+        for k in range(1, pools):
+            xs.append(xor_permute(x_half, "pool", pools, far_first(k, pools)))
+        (slots, weights, largest, extra_pairs), (pick, spread, slot_weight), _ = route(
             xs,
             expert_table,
             experts,
@@ -635,7 +645,7 @@
             True,
         )
         blocks = lax.all_gather(facts, "pool", axis=0)
-        (slots, weights, largest), (pick, spread, slot_weight), _ = route(
+        (slots, weights, largest, extra_pairs), (pick, spread, slot_weight), _ = route(
             [blocks], expert_table, experts, rows, top, capacity, pools, [], True
         )
         head_rows = lax.all_to_all(
@@ -671,14 +681,15 @@
         pieces = split(own, received, pools)
         total = pieces[0]
         for k in range(1, pools):
-            total = total + xor_permute(pieces[k], "pool", pools, k).astype(F32)
+            far = far_first(k, pools)
+            total = total + xor_permute(pieces[far], "pool", pools, far).astype(F32)
         return total if extra is None else total + extra
 
     def more(state):
-        k, total = state
-        k, *held_x = lax.optimization_barrier((k, *xs))
+        left, total = state
+        left, *held_x = lax.optimization_barrier((left, *xs))
         x = arrange(held_x, half_width) if direct else held_x[0]
-        pick, spread, slot_weight = pick_slots(k * capacity, slots, weights, capacity)
+        pick, spread, slot_weight = pick_slots(largest[0, 0] - left, slots, weights, capacity)
         gate = jnp.einsum("rd,efd->erf", x, w_gate, preferred_element_type=F32)
         up = jnp.einsum("rd,efd->erf", x, w_up, preferred_element_type=F32)
         both = jnp.concatenate([gate, up], axis=2).astype(BF16)
@@ -693,7 +704,7 @@
         spread = spread.reshape(experts, rows, hidden_units)
         value = jnp.einsum("erf,efd->rd", spread, w_down, preferred_element_type=F32)
         value = halves(value) if direct else [value]
-        return k + 1, total + combine(value)
+        return left - capacity, total + combine(value)
 
     both = [exchange(value) for value in sent]
     result = [None]
@@ -703,12 +714,14 @@
             *both[c], slot_weight, spread, in_vmem(w_down), result[0], c, last, not direct
         )
     if direct:
-        theirs, largest, *result = lax.optimization_barrier((theirs, largest, *result))
+        theirs, extra_pairs, *result = lax.optimization_barrier(
+            (theirs, extra_pairs, *result)
+        )
         attended = join(mine, theirs)
     _, extra = lax.while_loop(
-        lambda state: state[0] * capacity < largest[0, 0],
+        lambda state: state[0] > 0,
         more,
-        (jnp.minimum(largest[0, 0], 1), jnp.zeros((pool_rows, half_width // subs), F32)),
+        (extra_pairs[0, 0], jnp.zeros((pool_rows, half_width // subs), F32)),
     )
     if direct:
         return attended, combine(result, extra).astype(BF16)

time: 53.2 us -> 51.2 us (0.962)
  waiting for transfers between devices: 8.41 us -> 7.11 us
  between operations: 1.59 us -> 0.91 us
    ppermute x13, waiting for transfers between devices: 7.9 us -> 6.6 us  [xor_permute(): return lax.ppermute(value, axes, [(i, i ^ k) for i in range(count)])]
  transfers between devices with their start and end apart: 17 -> 17, of which waited for: 5 -> 8; matrix products, arithmetic and copies ran while one was open for 0% -> 0% of each run, Pallas kernels for 30% -> 31%
where the time goes in v6:
time: 51.2 us; the launch traced here: 51 us
  Pallas kernels  22.9 us (45%)
  starting transfers between devices  18.6 us (36%)
  waiting for transfers between devices  7.11 us (14%)
  between operations  0.91 us (2%)
  loops' own time  0.83 us (2%)
  other arithmetic  0.62 us (1%)
    pallas_call x14, Pallas kernels, call(): pl.pallas_call(run, in_specs=list(specs) + [HBM] * count_load + [ANY] * l...  22.9 us
    ppermute x13, starting transfers between devices, xor_permute(): return lax.ppermute(value, axes, [(i, i ^ k) for i in range(count)])  14.3 us
    ppermute x13, waiting for transfers between devices, xor_permute(): return lax.ppermute(value, axes, [(i, i ^ k) for i in range(count)])  6.6 us
    ppermute x3, starting transfers between devices, exchange(): return (value, lax.ppermute(value, 'tp', [(0, 1), (1, 0)]))  3.21 us
    ppermute x1, starting transfers between devices, body(): theirs = lax.ppermute(theirs, 'tp', [(0, 1), (1, 0)])  1.04 us
  transfers between devices with their start and end apart: 17, of which 8 were waited for; matrix products, arithmetic and copies ran while one was open for 0% of the time, Pallas kernels for 31%

profile of v6, /device:TPU:0, one launch (start us, length us, event | category | flops | bytes accessed | tf_op | source)
XLA Modules:
  0.0 51.0 jit_solution(3882296861779819326)
XLA Ops:
  0.6 2.3 %attention.1 = (bf16[4,1024]{1,0:T(4,128)(2,1)S(1)}, bf16[4,1024]{1,0:T(4,128)(2,1)S(1)}, bf16[4,1024]{1,0:T(4,128)(2,1)S(1)}, bf16[4,1024]{1,0:T(4,128)(2,1)S(1)}, bf16[16,128]{1,0:T(8,128)(2,1)S(1)}) custom-call(bf16[4,4096]{1,0:T(4,128)(2,1)} %refs_0_.3, s32[4]{0:T(128)} %refs_1_.2, s32[8,16]{1,0:T(8,128)} %bitcast.64, f32[8,16]{1,0:T(8,128)} %bitcast.65, ...), custom_call_target="tpu_custom_call" | custom-call | bytes 12000000 | tf_op jit(solution)/shard_map/attention/pallas_call | solution.py:109
  2.9 0.5 %collective-permute-start.5 = (bf16[4,1024]{1,0:T(4,128)(2,1)S(1)}, bf16[4,1024]{1,0:T(4,128)(2,1)S(1)}, u32[]{:S(2)}, u32[]{:S(2)}) collective-permute-start(bf16[4,1024]{1,0:T(4,128)(2,1)S(1)} %get-tuple-element.200), channel_id=1, source_target_pairs={{0,1},{1,0},{2,3},{3,2},{4,5},{5,4},{6,7},{7,6},{8,9},{9,8},{10,11... | collective-permute-start | bytes 24584 | tf_op jit(solution)/shard_map/ppermute | solution.py:557
  3.4 2.6 %collective-permute-start.6 = (bf16[4,1024]{1,0:T(4,128)(2,1)S(1)}, bf16[4,1024]{1,0:T(4,128)(2,1)S(1)}, u32[]{:S(2)}, u32[]{:S(2)}) collective-permute-start(bf16[4,1024]{1,0:T(4,128)(2,1)S(1)} %get-tuple-element.201), channel_id=1, source_target_pairs={{0,2},{1,3},{2,0},{3,1},{4,6},{5,7},{6,4},{7,5},{8,10},{9,11},{10,... | collective-permute-start | bytes 24584 | tf_op jit(solution)/shard_map/ppermute | solution.py:557
  6.0 0.1 collective-permute-start.7
  6.1 2.2 %load_a.1.refs_4_ = bf16[1024,2048]{1,0:T(8,128)(2,1)S(1)} custom-call(bf16[1024,2048]{1,0:T(8,128)(2,1)} %refs_0_.4, bf16[4,1024]{1,0:T(4,128)(2,1)S(1)} %get-tuple-element.199.refs_1_.refs_0_), custom_call_target="tpu_custom_call" | custom-call | bytes 6000000 | tf_op jit(solution)/shard_map/load_a/pallas_call | solution.py:109
  8.3 0.0 collective-permute-done.5.refs_1_
  8.3 0.0 collective-permute-done.6.refs_2_
  8.3 0.8 %collective-permute-done.7.refs_3_ = bf16[4,1024]{1,0:T(4,128)(2,1)S(1)} collective-permute-done((bf16[4,1024]{1,0:T(4,128)(2,1)S(1)}, bf16[4,1024]{1,0:T(4,128)(2,1)S(1)}, u32[]{:S(2)}, u32[]{:S(2)}) %collective-permute-start.7) | collective-permute-done | bytes 8224 | tf_op jit(solution)/shard_map/ppermute | solution.py:557
  9.1 0.0 slice-start.3
  9.1 0.0 slice-start.6
  9.1 0.7 %project.1 = (f32[16,1024]{1,0:T(8,128)S(1)}, bf16[16,1024]{1,0:T(8,128)(2,1)S(1)}, bf16[16,1024]{1,0:T(8,128)(2,1)S(1)}) custom-call(bf16[4,1024]{1,0:T(4,128)(2,1)S(1)} %get-tuple-element.199.refs_1_.refs_0_, bf16[4,1024]{1,0:T(4,128)(2,1)S(1)} %collective-permute-done.5.refs_1_, bf16[4,1024]{1,0:T(4,128)(2,1)S(1)} %collective-permute-done.6.refs_2_, ...), custom_call_target="tpu_custom_call" | custom-call | bytes 6000000 | tf_op jit(solution)/shard_map/project/pallas_call | solution.py:109
  9.8 0.9 %collective-permute-start.10 = (bf16[16,1024]{1,0:T(8,128)(2,1)S(1)}, bf16[16,1024]{1,0:T(8,128)(2,1)S(1)}, u32[]{:S(2)}, u32[]{:S(2)}) collective-permute-start(bf16[16,1024]{1,0:T(8,128)(2,1)S(1)} %get-tuple-element.206), channel_id=1, source_target_pairs={{0,3},{1,2},{2,1},{3,0},{4,7},{5,6},{6,5},{7,4},{8,11},{9,10},{10,... | collective-permute-start | bytes 98312 | tf_op jit(solution)/shard_map/ppermute | solution.py:557
  10.8 0.0 slice-start.8
  10.8 0.2 collective-permute-start.8
  11.0 1.0 %collective-permute-start.9 = (bf16[16,1024]{1,0:T(8,128)(2,1)S(1)}, bf16[16,1024]{1,0:T(8,128)(2,1)S(1)}, u32[]{:S(2)}, u32[]{:S(2)}) collective-permute-start(bf16[16,1024]{1,0:T(8,128)(2,1)S(1)} %get-tuple-element.206), channel_id=1, source_target_pairs={{0,2},{1,3},{2,0},{3,1},{4,6},{5,7},{6,4},{7,5},{8,10},{9,11},{10,... | collective-permute-start | bytes 98312 | tf_op jit(solution)/shard_map/ppermute | solution.py:557
  12.1 4.2 %load_b.1 = (bf16[16,128,1024]{2,1,0:T(8,128)(2,1)S(1)}, bf16[16,128,1024]{2,1,0:T(8,128)(2,1)S(1)}) custom-call(bf16[16,384,1024]{2,1,0:T(8,128)(2,1)} %refs_2_.3, bf16[16,384,1024]{2,1,0:T(8,128)(2,1)} %refs_3_.3, bf16[16,1024]{1,0:T(8,128)(2,1)S(1)} %get-tuple-element.205.refs_2_), custom_call_target="tpu_custom_call" | custom-call | bytes 12000000 | tf_op jit(solution)/shard_map/load_b/pallas_call | solution.py:109
  16.3 0.0 collective-permute-done.10.refs_4_
  16.3 0.0 collective-permute-done.8.refs_2_
  16.3 0.0 collective-permute-done.9.refs_3_
  16.4 3.7 %collective-permute-start.11 = (bf16[16,1152]{1,0:T(8,128)(2,1)S(1)}, bf16[16,1152]{1,0:T(8,128)(2,1)S(1)}, u32[]{:S(2)}, u32[]{:S(2)}) collective-permute-start(bf16[16,1152]{1,0:T(8,128)(2,1)S(1)} %add.82.refs_1_.refs_0_), channel_id=1, source_target_pairs={{0,12},{4,8},{8,4},{12,0},{1,13},{5,9},{9,5},{13,1},{2,14},{6,10},... | collective-permute-start | bytes 110600 | tf_op jit(solution)/shard_map/ppermute | solution.py:557
  20.1 0.0 collective-permute-start.12
  20.1 0.8 %collective-permute-start.13 = (bf16[16,1152]{1,0:T(8,128)(2,1)S(1)}, bf16[16,1152]{1,0:T(8,128)(2,1)S(1)}, u32[]{:S(2)}, u32[]{:S(2)}) collective-permute-start(bf16[16,1152]{1,0:T(8,128)(2,1)S(1)} %add.82.refs_1_.refs_0_), channel_id=1, source_target_pairs={{0,4},{4,0},{8,12},{12,8},{1,5},{5,1},{9,13},{13,9},{2,6},{6,2},{1... | collective-permute-start | bytes 110600 | tf_op jit(solution)/shard_map/ppermute | solution.py:557
  20.8 1.4 %collective-permute-done.11.refs_2_.refs_1_ = bf16[16,1152]{1,0:T(8,128)(2,1)S(1)} collective-permute-done((bf16[16,1152]{1,0:T(8,128)(2,1)S(1)}, bf16[16,1152]{1,0:T(8,128)(2,1)S(1)}, u32[]{:S(2)}, u32[]{:S(2)}) %collective-permute-start.11) | collective-permute-done | bytes 36896 | tf_op jit(solution)/shard_map/ppermute | solution.py:557
  22.3 2.6 %collective-permute-done.12.refs_3_.refs_2_ = bf16[16,1152]{1,0:T(8,128)(2,1)S(1)} collective-permute-done((bf16[16,1152]{1,0:T(8,128)(2,1)S(1)}, bf16[16,1152]{1,0:T(8,128)(2,1)S(1)}, u32[]{:S(2)}, u32[]{:S(2)}) %collective-permute-start.12) | collective-permute-done | bytes 36896 | tf_op jit(solution)/shard_map/ppermute | solution.py:557
  24.9 0.0 collective-permute-done.13.refs_4_.refs_3_
  24.9 0.0 copy-done.1
  24.9 0.9 %route.1 = (s32[4,1,256]{2,1,0:T(1,128)S(1)}, f32[4,1,256]{2,1,0:T(1,128)S(1)}, s32[1,1]{1,0:T(1,128)}, s32[1,1]{1,0:T(1,128)}, bf16[208,1024]{1,0:T(8,128)(2,1)...) custom-call(s32[1,64]{1,0:T(1,128)S(1)} %bitcast.60, bf16[16,1152]{1,0:T(8,128)(2,1)S(1)} %add.82.refs_1_.refs_0_, ...), custom_call_target="tpu_custom_call" | custom-call | bytes 18000000 | tf_op jit(solution)/shard_map/route/pallas_call | solution.py:109
  25.8 3.1 %gate_up_0.1 = (bf16[208,256]{1,0:T(8,128)(2,1)S(1)}, bf16[1024,64]{1,0:T(8,128)(2,1)S(1)}, bf16[4,1024]{1,0:T(4,128)(2,1)S(1)}, bf16[4,1024]{1,0:T(4,128)(2,1)S(1)}) custom-call(bf16[16,1152]{1,0:T(8,128)(2,1)S(1)} %add.82.refs_1_.refs_0_, bf16[16,1152]{1,0:T(8,128)(2,1)S(1)} %collective-permute-done.11.refs_2_.refs_1_, ...), custom_call_target="tpu_custom_call" | custom-call | bytes 12000000 | tf_op jit(solution)/shard_map/gate_up_0/pallas_call | solution.py:109
  28.9 1.0 %collective-permute-start.17 = (bf16[208,256]{1,0:T(8,128)(2,1)S(1)}, bf16[208,256]{1,0:T(8,128)(2,1)S(1)}, u32[]{:S(2)}, u32[]{:S(2)}) collective-permute-start(bf16[208,256]{1,0:T(8,128)(2,1)S(1)} %get-tuple-element.215.refs_4_.refs_0_), channel_id=1, source_target_pairs={{0,2},{2,0},{1,3},{3,1},{4,6},{6,4},{5,7},{7,5},{8,10},{10,8},{9,1... | collective-permute-start | bytes 319496 | tf_op jit(solution)/shard_map/ppermute | solution.py:670
  30.0 0.0 slice-done.3
  30.0 0.0 slice-done.6
  30.0 0.0 slice-done.4
  30.0 0.0 slice-done.5
  30.0 0.0 slice-done.7
  30.0 0.0 slice-done.8
  30.0 0.0 slice-start
  30.0 0.0 slice-start.1
  30.0 2.8 %gate_up_1.1.refs_4_.refs_0_ = bf16[208,256]{1,0:T(8,128)(2,1)S(1)} custom-call(bf16[1024,64]{1,0:T(8,128)(2,1)S(1)} %get-tuple-element.214.refs_0_, bf16[208,1024]{1,0:T(8,128)(2,1)S(1)} %get-tuple-element.209.refs_4_.refs_1_, bf16[16,384,1024]{2,1,0:T(8,128)(2,1)S(1)} %bitcast.57, bf16[16,384,1024]{2,1,0:T(8,128)(2,1)S(1)} %bitcast.59, ...), custom_call_target="tpu_custom_call" | custom-call | bytes 12000000 | tf_op jit(solution)/shard_map/gate_up_1/pallas_call | solution.py:109
  32.9 0.0 slice-start.2
  32.9 1.1 %collective-permute-start.16 = (bf16[208,256]{1,0:T(8,128)(2,1)S(1)}, bf16[208,256]{1,0:T(8,128)(2,1)S(1)}, u32[]{:S(2)}, u32[]{:S(2)}) collective-permute-start(bf16[208,256]{1,0:T(8,128)(2,1)S(1)} %gate_up_1.1.refs_4_.refs_0_), channel_id=1, source_target_pairs={{0,2},{2,0},{1,3},{3,1},{4,6},{6,4},{5,7},{7,5},{8,10},{10,8},{9,1... | collective-permute-start | bytes 319496 | tf_op jit(solution)/shard_map/ppermute | solution.py:670
  34.0 2.8 %gate_up_2.1.refs_0_ = bf16[208,256]{1,0:T(8,128)(2,1)S(1)} custom-call(bf16[1024,64]{1,0:T(8,128)(2,1)S(1)} %get-tuple-element.214.refs_0_, bf16[208,1024]{1,0:T(8,128)(2,1)S(1)} %get-tuple-element.209.refs_4_.refs_1_, bf16[16,384,1024]{2,1,0:T(8,128)(2,1)S(1)} %bitcast.57, bf16[16,384,1024]{2,1,0:T(8,128)(2,1)S(1)} %bitcast.59, ...), custom_call_target="tpu_custom_call" | custom-call | bytes 12000000 | tf_op jit(solution)/shard_map/gate_up_2/pallas_call | solution.py:109
  36.8 1.1 %collective-permute-start.15 = (bf16[208,256]{1,0:T(8,128)(2,1)S(1)}, bf16[208,256]{1,0:T(8,128)(2,1)S(1)}, u32[]{:S(2)}, u32[]{:S(2)}) collective-permute-start(bf16[208,256]{1,0:T(8,128)(2,1)S(1)} %gate_up_2.1.refs_0_), channel_id=1, source_target_pairs={{0,2},{2,0},{1,3},{3,1},{4,6},{6,4},{5,7},{7,5},{8,10},{10,8},{9,1... | collective-permute-start | bytes 319496 | tf_op jit(solution)/shard_map/ppermute | solution.py:670
  37.9 1.0 %collective-permute-start.14 = (bf16[4,1024]{1,0:T(4,128)(2,1)S(1)}, bf16[4,1024]{1,0:T(4,128)(2,1)S(1)}, u32[]{:S(2)}, u32[]{:S(2)}) collective-permute-start(bf16[4,1024]{1,0:T(4,128)(2,1)S(1)} %get-tuple-element.216), channel_id=1, source_target_pairs={{0,2},{2,0},{1,3},{3,1},{4,6},{6,4},{5,7},{7,5},{8,10},{10,8},{9,1... | collective-permute-start | bytes 24584 | tf_op jit(solution)/shard_map/ppermute | solution.py:635
  38.9 0.0 collective-permute-done.17.refs_1_
  38.9 0.0 slice-done
  38.9 0.0 slice-done.1
  38.9 0.0 slice-done.2
  38.9 1.1 %down_0.1.refs_5_ = f32[64,1024]{1,0:T(8,128)S(1)} custom-call(bf16[208,256]{1,0:T(8,128)(2,1)S(1)} %get-tuple-element.215.refs_4_.refs_0_, bf16[208,256]{1,0:T(8,128)(2,1)S(1)} %collective-permute-done.17.refs_1_, f32[208,1]{1,0:T(8,128)S(1)} %get-tuple-element.218.refs_2_, bf16[1024,208]{1,0:T(8,128)(2,1)S(1)} %get-tuple-element.219.refs_3_, ...), custom_call_target="tpu_custom_call" | custom-call | bytes 9000000 | tf_op jit(solution)/shard_map/down_0/pallas_call | solution.py:109
  40.0 0.0 collective-permute-done.16.refs_1_
  40.0 1.1 %down_1.1.refs_5_ = f32[64,1024]{1,0:T(8,128)S(1)} custom-call(bf16[208,256]{1,0:T(8,128)(2,1)S(1)} %gate_up_1.1.refs_4_.refs_0_, bf16[208,256]{1,0:T(8,128)(2,1)S(1)} %collective-permute-done.16.refs_1_, f32[208,1]{1,0:T(8,128)S(1)} %get-tuple-element.218.refs_2_, bf16[1024,208]{1,0:T(8,128)(2,1)S(1)} %get-tuple-element.219.refs_3_, ...), custom_call_target="tpu_custom_call" | custom-call | bytes 9000000 | tf_op jit(solution)/shard_map/down_1/pallas_call | solution.py:109
  41.1 0.5 collective-permute-done.15.refs_1_
  41.6 1.1 %down_2.1 = (f32[64,512]{1,0:T(8,128)S(1)}, f32[64,512]{1,0:T(8,128)S(1)}) custom-call(bf16[208,256]{1,0:T(8,128)(2,1)S(1)} %gate_up_2.1.refs_0_, bf16[208,256]{1,0:T(8,128)(2,1)S(1)} %collective-permute-done.15.refs_1_, f32[208,1]{1,0:T(8,128)S(1)} %get-tuple-element.218.refs_2_, bf16[1024,208]{1,0:T(8,128)(2,1)S(1)} %get-tuple-element.219.refs_3_, ...), custom_call_target="tpu_custom_call" | custom-call | bytes 9000000 | tf_op jit(solution)/shard_map/down_2/pallas_call | solution.py:109
  42.6 0.0 collective-permute-done.14.refs_1_
  42.7 0.1 collective-permute-start.18
  42.7 0.8 %while.12 = (s32[]{:T(128)}, f32[16,512]{1,0:T(8,128)S(1)}, bf16[16,1152]{1,0:T(8,128)(2,1)S(1)}, bf16[16,1152]{1,0:T(8,128)(2,1)S(1)}, bf16[16,1152]{1,0:T(8,12...) while((s32[]{:T(128)}, f32[16,512]{1,0:T(8,128)S(1)}, ...), condition=%wide.region_1.2_spmd, body=%wide.region_0.1_spmd.sunk | while | flops 2912233472 | bytes 122560824 | solution.py:721
  43.6 0.5 collective-permute-done.18.refs_1_
  44.1 1.5 %collective-permute-start.19 = (bf16[16,512]{1,0:T(8,128)(2,1)S(1)}, bf16[16,512]{1,0:T(8,128)(2,1)S(1)}, u32[]{:S(2)}, u32[]{:S(2)}) collective-permute-start(bf16[16,512]{1,0:T(8,128)(2,1)S(1)} %get-tuple-element.232), channel_id=1, source_target_pairs={{0,12},{4,8},{8,4},{12,0},{1,13},{5,9},{9,5},{13,1},{2,14},{6,10},... | collective-permute-start | bytes 49160 | tf_op jit(solution)/shard_map/ppermute | solution.py:557
  45.6 0.6 %collective-permute-start.20 = (bf16[16,512]{1,0:T(8,128)(2,1)S(1)}, bf16[16,512]{1,0:T(8,128)(2,1)S(1)}, u32[]{:S(2)}, u32[]{:S(2)}) collective-permute-start(bf16[16,512]{1,0:T(8,128)(2,1)S(1)} %get-tuple-element.233), channel_id=1, source_target_pairs={{0,8},{4,12},{8,0},{12,4},{1,9},{5,13},{9,1},{13,5},{2,10},{6,14},... | collective-permute-start | bytes 49160 | tf_op jit(solution)/shard_map/ppermute | solution.py:557
  46.2 2.3 %collective-permute-start.21 = (bf16[16,512]{1,0:T(8,128)(2,1)S(1)}, bf16[16,512]{1,0:T(8,128)(2,1)S(1)}, u32[]{:S(2)}, u32[]{:S(2)}) collective-permute-start(bf16[16,512]{1,0:T(8,128)(2,1)S(1)} %get-tuple-element.234), channel_id=1, source_target_pairs={{0,4},{4,0},{8,12},{12,8},{1,5},{5,1},{9,13},{13,9},{2,6},{6,2},{1... | collective-permute-start | bytes 49160 | tf_op jit(solution)/shard_map/ppermute | solution.py:557
  48.5 0.6 %join.1 = bf16[4,2048]{1,0:T(4,128)(2,1)} custom-call(bf16[4,1024]{1,0:T(4,128)(2,1)S(1)} %get-tuple-element.212.refs_0_, bf16[4,1024]{1,0:T(4,128)(2,1)S(1)} %collective-permute-done.14.refs_1_), custom_call_target="tpu_custom_call" | custom-call | bytes 6000000 | tf_op jit(solution)/shard_map/join/pallas_call | solution.py:109
  49.2 0.7 %collective-permute-done.19 = bf16[16,512]{1,0:T(8,128)(2,1)S(1)} collective-permute-done((bf16[16,512]{1,0:T(8,128)(2,1)S(1)}, bf16[16,512]{1,0:T(8,128)(2,1)S(1)}, u32[]{:S(2)}, u32[]{:S(2)}) %collective-permute-start.19) | collective-permute-done | bytes 16416 | tf_op jit(solution)/shard_map/ppermute | solution.py:557
  49.8 0.4 collective-permute-done.20
  50.3 0.2 collective-permute-done.21
  50.4 0.6 %add_convert_fusion = bf16[16,512]{1,0:T(8,128)(2,1)} fusion(f32[16,512]{1,0:T(8,128)S(1)} %get-tuple-element.235, bf16[16,512]{1,0:T(8,128)(2,1)S(1)} %collective-permute-done.21, bf16[16,512]{1,0:T(8,128)(2,1)S(1)} %collective-permute-done.20, f32[16,512]{1,0:T(8,128)S(1)} %get-tuple-element.231, bf16[16,512]{1,0:T(8,128)(2,1)S(1)} %collective-permute-done.19), kind=kLoop, calls=%fused_computation.20 | loop fusion | flops 65536 | bytes 131072 | tf_op jit(solution)/shard_map/convert_element_type | solution.py:727
  (10 shorter events, 0.0 us)
Async XLA Ops:
  2.9 5.4 %collective-permute-start.5 = (bf16[4,1024]{1,0:T(4,128)(2,1)S(1)}, bf16[4,1024]{1,0:T(4,128)(2,1)S(1)}, u32[]{:S(2)}, u32[]{:S(2)}) collective-permute-start(bf16[4,1024]{1,0:T(4,128)(2,1)S(1)} %get-tuple-element.200), channel_id=1, source_target_pairs={{0,1},{1,0},{2,3},{3,2},{4,5},{5,4},{6,7},{7,6},{8,9},{9,8},{10,11... | collective-permute-start | bytes 24584 | tf_op jit(solution)/shard_map/ppermute | solution.py:557
  3.4 4.9 %collective-permute-start.6 = (bf16[4,1024]{1,0:T(4,128)(2,1)S(1)}, bf16[4,1024]{1,0:T(4,128)(2,1)S(1)}, u32[]{:S(2)}, u32[]{:S(2)}) collective-permute-start(bf16[4,1024]{1,0:T(4,128)(2,1)S(1)} %get-tuple-element.201), channel_id=1, source_target_pairs={{0,2},{1,3},{2,0},{3,1},{4,6},{5,7},{6,4},{7,5},{8,10},{9,11},{10,... | collective-permute-start | bytes 24584 | tf_op jit(solution)/shard_map/ppermute | solution.py:557
  6.0 3.1 %collective-permute-start.7 = (bf16[4,1024]{1,0:T(4,128)(2,1)S(1)}, bf16[4,1024]{1,0:T(4,128)(2,1)S(1)}, u32[]{:S(2)}, u32[]{:S(2)}) collective-permute-start(bf16[4,1024]{1,0:T(4,128)(2,1)S(1)} %get-tuple-element.202), channel_id=1, source_target_pairs={{0,3},{1,2},{2,1},{3,0},{4,7},{5,6},{6,5},{7,4},{8,11},{9,10},{10,... | collective-permute-start | bytes 24584 | tf_op jit(solution)/shard_map/ppermute | solution.py:557
  9.1 20.9 %slice-start.3 = ((s8[12582912]{0:T(1024)(128)(4,1)}), s8[4194304]{0:T(1024)(128)(4,1)S(1)}, s32[]{:S(2)}) async-start(s8[12582912]{0:T(1024)(128)(4,1)} %bitcast.56), calls=%async_computation.3 | async-start | bytes 8388608
  9.1 20.9 %slice-start.6 = ((s8[12582912]{0:T(1024)(128)(4,1)}), s8[4194304]{0:T(1024)(128)(4,1)S(1)}, s32[]{:S(2)}) async-start(s8[12582912]{0:T(1024)(128)(4,1)} %bitcast.58), calls=%async_computation.6 | async-start | bytes 8388608
  9.8 6.5 %collective-permute-start.10 = (bf16[16,1024]{1,0:T(8,128)(2,1)S(1)}, bf16[16,1024]{1,0:T(8,128)(2,1)S(1)}, u32[]{:S(2)}, u32[]{:S(2)}) collective-permute-start(bf16[16,1024]{1,0:T(8,128)(2,1)S(1)} %get-tuple-element.206), channel_id=1, source_target_pairs={{0,3},{1,2},{2,1},{3,0},{4,7},{5,6},{6,5},{7,4},{8,11},{9,10},{10,... | collective-permute-start | bytes 98312 | tf_op jit(solution)/shard_map/ppermute | solution.py:557
  10.8 14.1 %copy-start.1 = (s32[64]{0:T(128)S(1)}, s32[64]{0:T(128)}, u32[]{:S(2)}) copy-start(s32[64]{0:T(128)} %param.20) | copy-start | bytes 772
  10.8 19.2 %slice-start.4 = ((s8[12582912]{0:T(1024)(128)(4,1)}), s8[4194304]{0:T(1024)(128)(4,1)S(1)}, s32[]{:S(2)}) async-start(s8[12582912]{0:T(1024)(128)(4,1)} %bitcast.56), calls=%async_computation.4 | async-start | bytes 8388608
  10.8 19.2 %slice-start.5 = ((s8[12582912]{0:T(1024)(128)(4,1)}), s8[4194304]{0:T(1024)(128)(4,1)S(1)}, s32[]{:S(2)}) async-start(s8[12582912]{0:T(1024)(128)(4,1)} %bitcast.56), calls=%async_computation.5 | async-start | bytes 8388608
  10.8 19.2 %slice-start.7 = ((s8[12582912]{0:T(1024)(128)(4,1)}), s8[4194304]{0:T(1024)(128)(4,1)S(1)}, s32[]{:S(2)}) async-start(s8[12582912]{0:T(1024)(128)(4,1)} %bitcast.58), calls=%async_computation.7 | async-start | bytes 8388608
  10.8 19.2 %slice-start.8 = ((s8[12582912]{0:T(1024)(128)(4,1)}), s8[4194304]{0:T(1024)(128)(4,1)S(1)}, s32[]{:S(2)}) async-start(s8[12582912]{0:T(1024)(128)(4,1)} %bitcast.58), calls=%async_computation.8 | async-start | bytes 8388608
  10.8 5.5 %collective-permute-start.8 = (bf16[16,1024]{1,0:T(8,128)(2,1)S(1)}, bf16[16,1024]{1,0:T(8,128)(2,1)S(1)}, u32[]{:S(2)}, u32[]{:S(2)}) collective-permute-start(bf16[16,1024]{1,0:T(8,128)(2,1)S(1)} %get-tuple-element.205.refs_2_), channel_id=1, source_target_pairs={{0,1},{1,0},{2,3},{3,2},{4,5},{5,4},{6,7},{7,6},{8,9},{9,8},{10,11... | collective-permute-start | bytes 98312 | tf_op jit(solution)/shard_map/ppermute | solution.py:557
  11.0 5.3 %collective-permute-start.9 = (bf16[16,1024]{1,0:T(8,128)(2,1)S(1)}, bf16[16,1024]{1,0:T(8,128)(2,1)S(1)}, u32[]{:S(2)}, u32[]{:S(2)}) collective-permute-start(bf16[16,1024]{1,0:T(8,128)(2,1)S(1)} %get-tuple-element.206), channel_id=1, source_target_pairs={{0,2},{1,3},{2,0},{3,1},{4,6},{5,7},{6,4},{7,5},{8,10},{9,11},{10,... | collective-permute-start | bytes 98312 | tf_op jit(solution)/shard_map/ppermute | solution.py:557
  16.4 5.9 %collective-permute-start.11 = (bf16[16,1152]{1,0:T(8,128)(2,1)S(1)}, bf16[16,1152]{1,0:T(8,128)(2,1)S(1)}, u32[]{:S(2)}, u32[]{:S(2)}) collective-permute-start(bf16[16,1152]{1,0:T(8,128)(2,1)S(1)} %add.82.refs_1_.refs_0_), channel_id=1, source_target_pairs={{0,12},{4,8},{8,4},{12,0},{1,13},{5,9},{9,5},{13,1},{2,14},{6,10},... | collective-permute-start | bytes 110600 | tf_op jit(solution)/shard_map/ppermute | solution.py:557
  20.1 4.9 %collective-permute-start.12 = (bf16[16,1152]{1,0:T(8,128)(2,1)S(1)}, bf16[16,1152]{1,0:T(8,128)(2,1)S(1)}, u32[]{:S(2)}, u32[]{:S(2)}) collective-permute-start(bf16[16,1152]{1,0:T(8,128)(2,1)S(1)} %add.82.refs_1_.refs_0_), channel_id=1, source_target_pairs={{0,8},{4,12},{8,0},{12,4},{1,9},{5,13},{9,1},{13,5},{2,10},{6,14},... | collective-permute-start | bytes 110600 | tf_op jit(solution)/shard_map/ppermute | solution.py:557
  20.1 4.9 %collective-permute-start.13 = (bf16[16,1152]{1,0:T(8,128)(2,1)S(1)}, bf16[16,1152]{1,0:T(8,128)(2,1)S(1)}, u32[]{:S(2)}, u32[]{:S(2)}) collective-permute-start(bf16[16,1152]{1,0:T(8,128)(2,1)S(1)} %add.82.refs_1_.refs_0_), channel_id=1, source_target_pairs={{0,4},{4,0},{8,12},{12,8},{1,5},{5,1},{9,13},{13,9},{2,6},{6,2},{1... | collective-permute-start | bytes 110600 | tf_op jit(solution)/shard_map/ppermute | solution.py:557
  28.9 10.0 %collective-permute-start.17 = (bf16[208,256]{1,0:T(8,128)(2,1)S(1)}, bf16[208,256]{1,0:T(8,128)(2,1)S(1)}, u32[]{:S(2)}, u32[]{:S(2)}) collective-permute-start(bf16[208,256]{1,0:T(8,128)(2,1)S(1)} %get-tuple-element.215.refs_4_.refs_0_), channel_id=1, source_target_pairs={{0,2},{2,0},{1,3},{3,1},{4,6},{6,4},{5,7},{7,5},{8,10},{10,8},{9,1... | collective-permute-start | bytes 319496 | tf_op jit(solution)/shard_map/ppermute | solution.py:670
  30.0 8.9 %slice-start = ((s8[12582912]{0:T(1024)(128)(4,1)}), s8[4194304]{0:T(1024)(128)(4,1)S(1)}, s32[]{:S(2)}) async-start(s8[12582912]{0:T(1024)(128)(4,1)} %bitcast.54), calls=%async_computation | async-start | bytes 8388608
  30.0 8.9 %slice-start.1 = ((s8[12582912]{0:T(1024)(128)(4,1)}), s8[4194304]{0:T(1024)(128)(4,1)S(1)}, s32[]{:S(2)}) async-start(s8[12582912]{0:T(1024)(128)(4,1)} %bitcast.54), calls=%async_computation.1 | async-start | bytes 8388608
  32.9 6.1 %slice-start.2 = ((s8[12582912]{0:T(1024)(128)(4,1)}), s8[4194304]{0:T(1024)(128)(4,1)S(1)}, s32[]{:S(2)}) async-start(s8[12582912]{0:T(1024)(128)(4,1)} %bitcast.54), calls=%async_computation.2 | async-start | bytes 8388608
  32.9 7.1 %collective-permute-start.16 = (bf16[208,256]{1,0:T(8,128)(2,1)S(1)}, bf16[208,256]{1,0:T(8,128)(2,1)S(1)}, u32[]{:S(2)}, u32[]{:S(2)}) collective-permute-start(bf16[208,256]{1,0:T(8,128)(2,1)S(1)} %gate_up_1.1.refs_4_.refs_0_), channel_id=1, source_target_pairs={{0,2},{2,0},{1,3},{3,1},{4,6},{6,4},{5,7},{7,5},{8,10},{10,8},{9,1... | collective-permute-start | bytes 319496 | tf_op jit(solution)/shard_map/ppermute | solution.py:670
  36.8 4.8 %collective-permute-start.15 = (bf16[208,256]{1,0:T(8,128)(2,1)S(1)}, bf16[208,256]{1,0:T(8,128)(2,1)S(1)}, u32[]{:S(2)}, u32[]{:S(2)}) collective-permute-start(bf16[208,256]{1,0:T(8,128)(2,1)S(1)} %gate_up_2.1.refs_0_), channel_id=1, source_target_pairs={{0,2},{2,0},{1,3},{3,1},{4,6},{6,4},{5,7},{7,5},{8,10},{10,8},{9,1... | collective-permute-start | bytes 319496 | tf_op jit(solution)/shard_map/ppermute | solution.py:670
  37.9 4.8 %collective-permute-start.14 = (bf16[4,1024]{1,0:T(4,128)(2,1)S(1)}, bf16[4,1024]{1,0:T(4,128)(2,1)S(1)}, u32[]{:S(2)}, u32[]{:S(2)}) collective-permute-start(bf16[4,1024]{1,0:T(4,128)(2,1)S(1)} %get-tuple-element.216), channel_id=1, source_target_pairs={{0,2},{2,0},{1,3},{3,1},{4,6},{6,4},{5,7},{7,5},{8,10},{10,8},{9,1... | collective-permute-start | bytes 24584 | tf_op jit(solution)/shard_map/ppermute | solution.py:635
  42.7 1.4 %collective-permute-start.18 = (f32[64,512]{1,0:T(8,128)S(1)}, f32[64,512]{1,0:T(8,128)S(1)}, u32[]{:S(2)}, u32[]{:S(2)}) collective-permute-start(f32[64,512]{1,0:T(8,128)S(1)} %get-tuple-element.224), channel_id=1, source_target_pairs={{0,1},{1,0},{2,3},{3,2},{4,5},{5,4},{6,7},{7,6},{8,9},{9,8},{10,11... | collective-permute-start | bytes 393224 | tf_op jit(solution)/shard_map/ppermute | solution.py:557
  44.1 5.8 %collective-permute-start.19 = (bf16[16,512]{1,0:T(8,128)(2,1)S(1)}, bf16[16,512]{1,0:T(8,128)(2,1)S(1)}, u32[]{:S(2)}, u32[]{:S(2)}) collective-permute-start(bf16[16,512]{1,0:T(8,128)(2,1)S(1)} %get-tuple-element.232), channel_id=1, source_target_pairs={{0,12},{4,8},{8,4},{12,0},{1,13},{5,9},{9,5},{13,1},{2,14},{6,10},... | collective-permute-start | bytes 49160 | tf_op jit(solution)/shard_map/ppermute | solution.py:557
  45.6 4.7 %collective-permute-start.20 = (bf16[16,512]{1,0:T(8,128)(2,1)S(1)}, bf16[16,512]{1,0:T(8,128)(2,1)S(1)}, u32[]{:S(2)}, u32[]{:S(2)}) collective-permute-start(bf16[16,512]{1,0:T(8,128)(2,1)S(1)} %get-tuple-element.233), channel_id=1, source_target_pairs={{0,8},{4,12},{8,0},{12,4},{1,9},{5,13},{9,1},{13,5},{2,10},{6,14},... | collective-permute-start | bytes 49160 | tf_op jit(solution)/shard_map/ppermute | solution.py:557
  46.2 4.2 %collective-permute-start.21 = (bf16[16,512]{1,0:T(8,128)(2,1)S(1)}, bf16[16,512]{1,0:T(8,128)(2,1)S(1)}, u32[]{:S(2)}, u32[]{:S(2)}) collective-permute-start(bf16[16,512]{1,0:T(8,128)(2,1)S(1)} %get-tuple-element.234), channel_id=1, source_target_pairs={{0,4},{4,0},{8,12},{12,8},{1,5},{5,1},{9,13},{13,9},{2,6},{6,2},{1... | collective-permute-start | bytes 49160 | tf_op jit(solution)/shard_map/ppermute | solution.py:557

commit v7 on v6

--- a/solution.py
+++ b/solution.py
@@ -603,11 +603,12 @@
         (out_held,) = load([(out_weight, None)], [pieces[0]], "load_a")
         kept, near, far = project(inputs, out_held)
         gate_1, up_1 = gate_2, up_2 = in_vmem(w_gate), in_vmem(w_up)
-        gate_0, up_0 = load([gates[0], ups[0]], [near], "load_b")
+        (gate_0,) = load([gates[0]], [near], "load_b")
         others = [
             xor_permute(near if k < subs else far, axes, shards, k) for k in range(1, shards)
         ]
         x_half, gate_0 = lax.optimization_barrier((add(kept, facts, others), gate_0))
+        (up_0,) = load([ups[0]], [x_half], "load_c")
         xs = [x_half]
         for k in range(1, pools):
             xs.append(xor_permute(x_half, "pool", pools, far_first(k, pools)))

time: 51.2 us -> 50.1 us (0.979)
  waiting for transfers between devices: 7.11 us -> 5.59 us
    ppermute x13, waiting for transfers between devices: 6.6 us -> 5.08 us  [xor_permute(): return lax.ppermute(value, axes, [(i, i ^ k) for i in range(count)])]
    pallas_call x14 -> x15, Pallas kernels: 22.9 us -> 23.3 us  [call(): pl.pallas_call(run, in_specs=list(specs) + [HBM] * count_load + [ANY] * l...]
  transfers between devices with their start and end apart: 17 -> 17, of which waited for: 8 -> 7; matrix products, arithmetic and copies ran while one was open for 0% -> 0% of each run, Pallas kernels for 31% -> 33%
where the time goes in v7:
time: 50.1 us; the launch traced here: 49.9 us
  Pallas kernels  23.3 us (47%)
  starting transfers between devices  18.5 us (37%)
  waiting for transfers between devices  5.59 us (11%)
  between operations  0.92 us (2%)
  loops' own time  0.83 us (2%)
  other arithmetic  0.62 us (1%)
    pallas_call x15, Pallas kernels, call(): pl.pallas_call(run, in_specs=list(specs) + [HBM] * count_load + [ANY] * l...  23.3 us
    ppermute x13, starting transfers between devices, xor_permute(): return lax.ppermute(value, axes, [(i, i ^ k) for i in range(count)])  14.3 us
    ppermute x13, waiting for transfers between devices, xor_permute(): return lax.ppermute(value, axes, [(i, i ^ k) for i in range(count)])  5.08 us
    ppermute x3, starting transfers between devices, exchange(): return (value, lax.ppermute(value, 'tp', [(0, 1), (1, 0)]))  3.29 us
  transfers between devices with their start and end apart: 17, of which 7 were waited for; matrix products, arithmetic and copies ran while one was open for 0% of the time, Pallas kernels for 33%

profile of v7, /device:TPU:0, one launch (start us, length us, event | category | flops | bytes accessed | tf_op | source)
XLA Modules:
  0.0 49.9 jit_solution(16589622508477938755)
XLA Ops:
  0.6 2.3 %attention.1 = (bf16[4,1024]{1,0:T(4,128)(2,1)S(1)}, bf16[4,1024]{1,0:T(4,128)(2,1)S(1)}, bf16[4,1024]{1,0:T(4,128)(2,1)S(1)}, bf16[4,1024]{1,0:T(4,128)(2,1)S(1)}, bf16[16,128]{1,0:T(8,128)(2,1)S(1)}) custom-call(bf16[4,4096]{1,0:T(4,128)(2,1)} %refs_0_.4, s32[4]{0:T(128)} %refs_1_.1, s32[8,16]{1,0:T(8,128)} %bitcast.64, f32[8,16]{1,0:T(8,128)} %bitcast.65, ...), custom_call_target="tpu_custom_call" | custom-call | bytes 12000000 | tf_op jit(solution)/shard_map/attention/pallas_call | solution.py:109
  2.9 0.5 %collective-permute-start.5 = (bf16[4,1024]{1,0:T(4,128)(2,1)S(1)}, bf16[4,1024]{1,0:T(4,128)(2,1)S(1)}, u32[]{:S(2)}, u32[]{:S(2)}) collective-permute-start(bf16[4,1024]{1,0:T(4,128)(2,1)S(1)} %get-tuple-element.198), channel_id=1, source_target_pairs={{0,1},{1,0},{2,3},{3,2},{4,5},{5,4},{6,7},{7,6},{8,9},{9,8},{10,11... | collective-permute-start | bytes 24584 | tf_op jit(solution)/shard_map/ppermute | solution.py:557
  3.4 2.6 %collective-permute-start.6 = (bf16[4,1024]{1,0:T(4,128)(2,1)S(1)}, bf16[4,1024]{1,0:T(4,128)(2,1)S(1)}, u32[]{:S(2)}, u32[]{:S(2)}) collective-permute-start(bf16[4,1024]{1,0:T(4,128)(2,1)S(1)} %get-tuple-element.199), channel_id=1, source_target_pairs={{0,2},{1,3},{2,0},{3,1},{4,6},{5,7},{6,4},{7,5},{8,10},{9,11},{10,... | collective-permute-start | bytes 24584 | tf_op jit(solution)/shard_map/ppermute | solution.py:557
  6.0 0.1 collective-permute-start.7
  6.1 2.2 %load_a.1.refs_4_ = bf16[1024,2048]{1,0:T(8,128)(2,1)S(1)} custom-call(bf16[1024,2048]{1,0:T(8,128)(2,1)} %refs_0_.5, bf16[4,1024]{1,0:T(4,128)(2,1)S(1)} %get-tuple-element.197.refs_1_.refs_0_), custom_call_target="tpu_custom_call" | custom-call | bytes 6000000 | tf_op jit(solution)/shard_map/load_a/pallas_call | solution.py:109
  8.3 0.0 collective-permute-done.5.refs_1_
  8.3 0.0 collective-permute-done.6.refs_2_
  8.3 0.8 %collective-permute-done.7.refs_3_ = bf16[4,1024]{1,0:T(4,128)(2,1)S(1)} collective-permute-done((bf16[4,1024]{1,0:T(4,128)(2,1)S(1)}, bf16[4,1024]{1,0:T(4,128)(2,1)S(1)}, u32[]{:S(2)}, u32[]{:S(2)}) %collective-permute-start.7) | collective-permute-done | bytes 8224 | tf_op jit(solution)/shard_map/ppermute | solution.py:557
  9.1 0.7 %project.1 = (f32[16,1024]{1,0:T(8,128)S(1)}, bf16[16,1024]{1,0:T(8,128)(2,1)S(1)}, bf16[16,1024]{1,0:T(8,128)(2,1)S(1)}) custom-call(bf16[4,1024]{1,0:T(4,128)(2,1)S(1)} %get-tuple-element.197.refs_1_.refs_0_, bf16[4,1024]{1,0:T(4,128)(2,1)S(1)} %collective-permute-done.5.refs_1_, bf16[4,1024]{1,0:T(4,128)(2,1)S(1)} %collective-permute-done.6.refs_2_, ...), custom_call_target="tpu_custom_call" | custom-call | bytes 6000000 | tf_op jit(solution)/shard_map/project/pallas_call | solution.py:109
  9.8 0.9 %collective-permute-start.10 = (bf16[16,1024]{1,0:T(8,128)(2,1)S(1)}, bf16[16,1024]{1,0:T(8,128)(2,1)S(1)}, u32[]{:S(2)}, u32[]{:S(2)}) collective-permute-start(bf16[16,1024]{1,0:T(8,128)(2,1)S(1)} %get-tuple-element.204), channel_id=1, source_target_pairs={{0,3},{1,2},{2,1},{3,0},{4,7},{5,6},{6,5},{7,4},{8,11},{9,10},{10,... | collective-permute-start | bytes 98312 | tf_op jit(solution)/shard_map/ppermute | solution.py:557
  10.7 0.2 collective-permute-start.8
  10.9 1.1 %collective-permute-start.9 = (bf16[16,1024]{1,0:T(8,128)(2,1)S(1)}, bf16[16,1024]{1,0:T(8,128)(2,1)S(1)}, u32[]{:S(2)}, u32[]{:S(2)}) collective-permute-start(bf16[16,1024]{1,0:T(8,128)(2,1)S(1)} %get-tuple-element.204), channel_id=1, source_target_pairs={{0,2},{1,3},{2,0},{3,1},{4,6},{5,7},{6,4},{7,5},{8,10},{9,11},{10,... | collective-permute-start | bytes 98312 | tf_op jit(solution)/shard_map/ppermute | solution.py:557
  12.0 2.3 %load_b.1.refs_5_ = bf16[16,128,1024]{2,1,0:T(8,128)(2,1)S(1)} custom-call(bf16[16,384,1024]{2,1,0:T(8,128)(2,1)} %refs_2_.3, bf16[16,1024]{1,0:T(8,128)(2,1)S(1)} %get-tuple-element.203.refs_1_), custom_call_target="tpu_custom_call" | custom-call | bytes 6000000 | tf_op jit(solution)/shard_map/load_b/pallas_call | solution.py:109
  14.3 0.0 collective-permute-done.10.refs_4_
  14.3 0.0 collective-permute-done.8.refs_2_
  14.4 0.5 collective-permute-done.9.refs_3_
  14.9 0.0 copy-start.1
  14.9 0.0 slice-start.8
  14.9 3.7 %collective-permute-start.11 = (bf16[16,1152]{1,0:T(8,128)(2,1)S(1)}, bf16[16,1152]{1,0:T(8,128)(2,1)S(1)}, u32[]{:S(2)}, u32[]{:S(2)}) collective-permute-start(bf16[16,1152]{1,0:T(8,128)(2,1)S(1)} %add.82.refs_1_.refs_0_), channel_id=1, source_target_pairs={{0,12},{4,8},{8,4},{12,0},{1,13},{5,9},{9,5},{13,1},{2,14},{6,10},... | collective-permute-start | bytes 110600 | tf_op jit(solution)/shard_map/ppermute | solution.py:557
  18.5 0.0 collective-permute-start.12
  18.5 0.8 %collective-permute-start.13 = (bf16[16,1152]{1,0:T(8,128)(2,1)S(1)}, bf16[16,1152]{1,0:T(8,128)(2,1)S(1)}, u32[]{:S(2)}, u32[]{:S(2)}) collective-permute-start(bf16[16,1152]{1,0:T(8,128)(2,1)S(1)} %add.82.refs_1_.refs_0_), channel_id=1, source_target_pairs={{0,4},{4,0},{8,12},{12,8},{1,5},{5,1},{9,13},{13,9},{2,6},{6,2},{1... | collective-permute-start | bytes 110600 | tf_op jit(solution)/shard_map/ppermute | solution.py:557
  19.3 2.3 %load_c.1.refs_6_ = bf16[16,128,1024]{2,1,0:T(8,128)(2,1)S(1)} custom-call(bf16[16,384,1024]{2,1,0:T(8,128)(2,1)} %refs_3_.3, bf16[16,1152]{1,0:T(8,128)(2,1)S(1)} %add.82.refs_1_.refs_0_), custom_call_target="tpu_custom_call" | custom-call | bytes 6000000 | tf_op jit(solution)/shard_map/load_c/pallas_call | solution.py:109
  21.7 0.0 collective-permute-done.11.refs_2_.refs_1_
  21.7 1.7 %collective-permute-done.12.refs_3_.refs_2_ = bf16[16,1152]{1,0:T(8,128)(2,1)S(1)} collective-permute-done((bf16[16,1152]{1,0:T(8,128)(2,1)S(1)}, bf16[16,1152]{1,0:T(8,128)(2,1)S(1)}, u32[]{:S(2)}, u32[]{:S(2)}) %collective-permute-start.12) | collective-permute-done | bytes 36896 | tf_op jit(solution)/shard_map/ppermute | solution.py:557
  23.4 0.0 collective-permute-done.13.refs_4_.refs_3_
  23.4 0.0 copy-done.1
  23.4 0.9 %route.1 = (s32[4,1,256]{2,1,0:T(1,128)S(1)}, f32[4,1,256]{2,1,0:T(1,128)S(1)}, s32[1,1]{1,0:T(1,128)}, s32[1,1]{1,0:T(1,128)}, bf16[208,1024]{1,0:T(8,128)(2,1)...) custom-call(s32[1,64]{1,0:T(1,128)S(1)} %bitcast.60, bf16[16,1152]{1,0:T(8,128)(2,1)S(1)} %add.82.refs_1_.refs_0_, ...), custom_call_target="tpu_custom_call" | custom-call | bytes 18000000 | tf_op jit(solution)/shard_map/route/pallas_call | solution.py:109
  24.3 3.0 %gate_up_0.1 = (bf16[208,256]{1,0:T(8,128)(2,1)S(1)}, bf16[1024,64]{1,0:T(8,128)(2,1)S(1)}, bf16[4,1024]{1,0:T(4,128)(2,1)S(1)}, bf16[4,1024]{1,0:T(4,128)(2,1)S(1)}) custom-call(bf16[16,1152]{1,0:T(8,128)(2,1)S(1)} %add.82.refs_1_.refs_0_, bf16[16,1152]{1,0:T(8,128)(2,1)S(1)} %collective-permute-done.11.refs_2_.refs_1_, ...), custom_call_target="tpu_custom_call" | custom-call | bytes 12000000 | tf_op jit(solution)/shard_map/gate_up_0/pallas_call | solution.py:109
  27.3 1.1 %collective-permute-start.17 = (bf16[208,256]{1,0:T(8,128)(2,1)S(1)}, bf16[208,256]{1,0:T(8,128)(2,1)S(1)}, u32[]{:S(2)}, u32[]{:S(2)}) collective-permute-start(bf16[208,256]{1,0:T(8,128)(2,1)S(1)} %get-tuple-element.211.refs_4_.refs_0_), channel_id=1, source_target_pairs={{0,2},{2,0},{1,3},{3,1},{4,6},{6,4},{5,7},{7,5},{8,10},{10,8},{9,1... | collective-permute-start | bytes 319496 | tf_op jit(solution)/shard_map/ppermute | solution.py:671
  28.5 0.0 slice-done.6
  28.5 0.0 slice-done.7
  28.5 0.0 slice-done.8
  28.5 0.0 slice-done.3
  28.5 0.0 slice-done.4
  28.5 0.0 slice-done.5
  28.5 0.0 slice-start
  28.5 0.0 slice-start.1
  28.5 2.8 %gate_up_1.1.refs_4_.refs_0_ = bf16[208,256]{1,0:T(8,128)(2,1)S(1)} custom-call(bf16[1024,64]{1,0:T(8,128)(2,1)S(1)} %get-tuple-element.210.refs_0_, bf16[208,1024]{1,0:T(8,128)(2,1)S(1)} %get-tuple-element.206.refs_4_.refs_1_, bf16[16,384,1024]{2,1,0:T(8,128)(2,1)S(1)} %bitcast.57, bf16[16,384,1024]{2,1,0:T(8,128)(2,1)S(1)} %bitcast.59, ...), custom_call_target="tpu_custom_call" | custom-call | bytes 12000000 | tf_op jit(solution)/shard_map/gate_up_1/pallas_call | solution.py:109
  31.4 0.0 slice-start.2
  31.4 1.0 %collective-permute-start.16 = (bf16[208,256]{1,0:T(8,128)(2,1)S(1)}, bf16[208,256]{1,0:T(8,128)(2,1)S(1)}, u32[]{:S(2)}, u32[]{:S(2)}) collective-permute-start(bf16[208,256]{1,0:T(8,128)(2,1)S(1)} %gate_up_1.1.refs_4_.refs_0_), channel_id=1, source_target_pairs={{0,2},{2,0},{1,3},{3,1},{4,6},{6,4},{5,7},{7,5},{8,10},{10,8},{9,1... | collective-permute-start | bytes 319496 | tf_op jit(solution)/shard_map/ppermute | solution.py:671
  32.4 2.8 %gate_up_2.1.refs_0_ = bf16[208,256]{1,0:T(8,128)(2,1)S(1)} custom-call(bf16[1024,64]{1,0:T(8,128)(2,1)S(1)} %get-tuple-element.210.refs_0_, bf16[208,1024]{1,0:T(8,128)(2,1)S(1)} %get-tuple-element.206.refs_4_.refs_1_, bf16[16,384,1024]{2,1,0:T(8,128)(2,1)S(1)} %bitcast.57, bf16[16,384,1024]{2,1,0:T(8,128)(2,1)S(1)} %bitcast.59, ...), custom_call_target="tpu_custom_call" | custom-call | bytes 12000000 | tf_op jit(solution)/shard_map/gate_up_2/pallas_call | solution.py:109
  35.2 1.1 %collective-permute-start.15 = (bf16[208,256]{1,0:T(8,128)(2,1)S(1)}, bf16[208,256]{1,0:T(8,128)(2,1)S(1)}, u32[]{:S(2)}, u32[]{:S(2)}) collective-permute-start(bf16[208,256]{1,0:T(8,128)(2,1)S(1)} %gate_up_2.1.refs_0_), channel_id=1, source_target_pairs={{0,2},{2,0},{1,3},{3,1},{4,6},{6,4},{5,7},{7,5},{8,10},{10,8},{9,1... | collective-permute-start | bytes 319496 | tf_op jit(solution)/shard_map/ppermute | solution.py:671
  36.4 1.0 %collective-permute-start.14 = (bf16[4,1024]{1,0:T(4,128)(2,1)S(1)}, bf16[4,1024]{1,0:T(4,128)(2,1)S(1)}, u32[]{:S(2)}, u32[]{:S(2)}) collective-permute-start(bf16[4,1024]{1,0:T(4,128)(2,1)S(1)} %get-tuple-element.212), channel_id=1, source_target_pairs={{0,2},{2,0},{1,3},{3,1},{4,6},{6,4},{5,7},{7,5},{8,10},{10,8},{9,1... | collective-permute-start | bytes 24584 | tf_op jit(solution)/shard_map/ppermute | solution.py:636
  37.3 0.0 collective-permute-done.17.refs_1_
  37.3 0.0 slice-done
  37.3 0.0 slice-done.1
  37.3 0.0 slice-done.2
  37.4 1.1 %down_0.1.refs_5_ = f32[64,1024]{1,0:T(8,128)S(1)} custom-call(bf16[208,256]{1,0:T(8,128)(2,1)S(1)} %get-tuple-element.211.refs_4_.refs_0_, bf16[208,256]{1,0:T(8,128)(2,1)S(1)} %collective-permute-done.17.refs_1_, f32[208,1]{1,0:T(8,128)S(1)} %get-tuple-element.214.refs_2_, bf16[1024,208]{1,0:T(8,128)(2,1)S(1)} %get-tuple-element.215.refs_3_, ...), custom_call_target="tpu_custom_call" | custom-call | bytes 9000000 | tf_op jit(solution)/shard_map/down_0/pallas_call | solution.py:109
  38.4 0.0 collective-permute-done.16.refs_1_
  38.4 1.1 %down_1.1.refs_5_ = f32[64,1024]{1,0:T(8,128)S(1)} custom-call(bf16[208,256]{1,0:T(8,128)(2,1)S(1)} %gate_up_1.1.refs_4_.refs_0_, bf16[208,256]{1,0:T(8,128)(2,1)S(1)} %collective-permute-done.16.refs_1_, f32[208,1]{1,0:T(8,128)S(1)} %get-tuple-element.214.refs_2_, bf16[1024,208]{1,0:T(8,128)(2,1)S(1)} %get-tuple-element.215.refs_3_, ...), custom_call_target="tpu_custom_call" | custom-call | bytes 9000000 | tf_op jit(solution)/shard_map/down_1/pallas_call | solution.py:109
  39.5 0.5 %collective-permute-done.15.refs_1_ = bf16[208,256]{1,0:T(8,128)(2,1)S(1)} collective-permute-done((bf16[208,256]{1,0:T(8,128)(2,1)S(1)}, bf16[208,256]{1,0:T(8,128)(2,1)S(1)}, u32[]{:S(2)}, u32[]{:S(2)}) %collective-permute-start.15) | collective-permute-done | bytes 106528 | tf_op jit(solution)/shard_map/ppermute | solution.py:671
  40.0 1.1 %down_2.1 = (f32[64,512]{1,0:T(8,128)S(1)}, f32[64,512]{1,0:T(8,128)S(1)}) custom-call(bf16[208,256]{1,0:T(8,128)(2,1)S(1)} %gate_up_2.1.refs_0_, bf16[208,256]{1,0:T(8,128)(2,1)S(1)} %collective-permute-done.15.refs_1_, f32[208,1]{1,0:T(8,128)S(1)} %get-tuple-element.214.refs_2_, bf16[1024,208]{1,0:T(8,128)(2,1)S(1)} %get-tuple-element.215.refs_3_, ...), custom_call_target="tpu_custom_call" | custom-call | bytes 9000000 | tf_op jit(solution)/shard_map/down_2/pallas_call | solution.py:109
  41.1 0.0 collective-permute-done.14.refs_1_
  41.1 0.1 collective-permute-start.18
  41.2 0.8 %while.12 = (s32[]{:T(128)}, f32[16,512]{1,0:T(8,128)S(1)}, bf16[16,1152]{1,0:T(8,128)(2,1)S(1)}, bf16[16,1152]{1,0:T(8,128)(2,1)S(1)}, bf16[16,1152]{1,0:T(8,12...) while((s32[]{:T(128)}, f32[16,512]{1,0:T(8,128)S(1)}, ...), condition=%wide.region_1.2_spmd, body=%wide.region_0.1_spmd.sunk | while | flops 2912233472 | bytes 122560824 | solution.py:722
  42.0 0.5 collective-permute-done.18.refs_1_
  42.5 2.0 %collective-permute-start.19 = (bf16[16,512]{1,0:T(8,128)(2,1)S(1)}, bf16[16,512]{1,0:T(8,128)(2,1)S(1)}, u32[]{:S(2)}, u32[]{:S(2)}) collective-permute-start(bf16[16,512]{1,0:T(8,128)(2,1)S(1)} %get-tuple-element.228), channel_id=1, source_target_pairs={{0,12},{4,8},{8,4},{12,0},{1,13},{5,9},{9,5},{13,1},{2,14},{6,10},... | collective-permute-start | bytes 49160 | tf_op jit(solution)/shard_map/ppermute | solution.py:557
  44.5 0.2 collective-permute-start.20
  44.7 2.3 %collective-permute-start.21 = (bf16[16,512]{1,0:T(8,128)(2,1)S(1)}, bf16[16,512]{1,0:T(8,128)(2,1)S(1)}, u32[]{:S(2)}, u32[]{:S(2)}) collective-permute-start(bf16[16,512]{1,0:T(8,128)(2,1)S(1)} %get-tuple-element.230), channel_id=1, source_target_pairs={{0,4},{4,0},{8,12},{12,8},{1,5},{5,1},{9,13},{13,9},{2,6},{6,2},{1... | collective-permute-start | bytes 49160 | tf_op jit(solution)/shard_map/ppermute | solution.py:557
  47.0 0.6 %join.1 = bf16[4,2048]{1,0:T(4,128)(2,1)} custom-call(bf16[4,1024]{1,0:T(4,128)(2,1)S(1)} %get-tuple-element.208.refs_0_, bf16[4,1024]{1,0:T(4,128)(2,1)S(1)} %collective-permute-done.14.refs_1_), custom_call_target="tpu_custom_call" | custom-call | bytes 6000000 | tf_op jit(solution)/shard_map/join/pallas_call | solution.py:109
  47.6 0.8 %collective-permute-done.19 = bf16[16,512]{1,0:T(8,128)(2,1)S(1)} collective-permute-done((bf16[16,512]{1,0:T(8,128)(2,1)S(1)}, bf16[16,512]{1,0:T(8,128)(2,1)S(1)}, u32[]{:S(2)}, u32[]{:S(2)}) %collective-permute-start.19) | collective-permute-done | bytes 16416 | tf_op jit(solution)/shard_map/ppermute | solution.py:557
  48.4 0.9 %collective-permute-done.20 = bf16[16,512]{1,0:T(8,128)(2,1)S(1)} collective-permute-done((bf16[16,512]{1,0:T(8,128)(2,1)S(1)}, bf16[16,512]{1,0:T(8,128)(2,1)S(1)}, u32[]{:S(2)}, u32[]{:S(2)}) %collective-permute-start.20) | collective-permute-done | bytes 16416 | tf_op jit(solution)/shard_map/ppermute | solution.py:557
  49.2 0.0 collective-permute-done.21
  49.2 0.6 %add_convert_fusion = bf16[16,512]{1,0:T(8,128)(2,1)} fusion(f32[16,512]{1,0:T(8,128)S(1)} %get-tuple-element.231, bf16[16,512]{1,0:T(8,128)(2,1)S(1)} %collective-permute-done.21, bf16[16,512]{1,0:T(8,128)(2,1)S(1)} %collective-permute-done.20, f32[16,512]{1,0:T(8,128)S(1)} %get-tuple-element.227, bf16[16,512]{1,0:T(8,128)(2,1)S(1)} %collective-permute-done.19), kind=kLoop, calls=%fused_computation.20 | loop fusion | flops 65536 | bytes 131072 | tf_op jit(solution)/shard_map/convert_element_type | solution.py:728
  (11 shorter events, 0.0 us)
Async XLA Ops:
  2.9 5.4 %collective-permute-start.5 = (bf16[4,1024]{1,0:T(4,128)(2,1)S(1)}, bf16[4,1024]{1,0:T(4,128)(2,1)S(1)}, u32[]{:S(2)}, u32[]{:S(2)}) collective-permute-start(bf16[4,1024]{1,0:T(4,128)(2,1)S(1)} %get-tuple-element.198), channel_id=1, source_target_pairs={{0,1},{1,0},{2,3},{3,2},{4,5},{5,4},{6,7},{7,6},{8,9},{9,8},{10,11... | collective-permute-start | bytes 24584 | tf_op jit(solution)/shard_map/ppermute | solution.py:557
  3.4 4.9 %collective-permute-start.6 = (bf16[4,1024]{1,0:T(4,128)(2,1)S(1)}, bf16[4,1024]{1,0:T(4,128)(2,1)S(1)}, u32[]{:S(2)}, u32[]{:S(2)}) collective-permute-start(bf16[4,1024]{1,0:T(4,128)(2,1)S(1)} %get-tuple-element.199), channel_id=1, source_target_pairs={{0,2},{1,3},{2,0},{3,1},{4,6},{5,7},{6,4},{7,5},{8,10},{9,11},{10,... | collective-permute-start | bytes 24584 | tf_op jit(solution)/shard_map/ppermute | solution.py:557
  6.0 3.1 %collective-permute-start.7 = (bf16[4,1024]{1,0:T(4,128)(2,1)S(1)}, bf16[4,1024]{1,0:T(4,128)(2,1)S(1)}, u32[]{:S(2)}, u32[]{:S(2)}) collective-permute-start(bf16[4,1024]{1,0:T(4,128)(2,1)S(1)} %get-tuple-element.200), channel_id=1, source_target_pairs={{0,3},{1,2},{2,1},{3,0},{4,7},{5,6},{6,5},{7,4},{8,11},{9,10},{10,... | collective-permute-start | bytes 24584 | tf_op jit(solution)/shard_map/ppermute | solution.py:557
  9.8 4.5 %collective-permute-start.10 = (bf16[16,1024]{1,0:T(8,128)(2,1)S(1)}, bf16[16,1024]{1,0:T(8,128)(2,1)S(1)}, u32[]{:S(2)}, u32[]{:S(2)}) collective-permute-start(bf16[16,1024]{1,0:T(8,128)(2,1)S(1)} %get-tuple-element.204), channel_id=1, source_target_pairs={{0,3},{1,2},{2,1},{3,0},{4,7},{5,6},{6,5},{7,4},{8,11},{9,10},{10,... | collective-permute-start | bytes 98312 | tf_op jit(solution)/shard_map/ppermute | solution.py:557
  10.7 3.6 %collective-permute-start.8 = (bf16[16,1024]{1,0:T(8,128)(2,1)S(1)}, bf16[16,1024]{1,0:T(8,128)(2,1)S(1)}, u32[]{:S(2)}, u32[]{:S(2)}) collective-permute-start(bf16[16,1024]{1,0:T(8,128)(2,1)S(1)} %get-tuple-element.203.refs_1_), channel_id=1, source_target_pairs={{0,1},{1,0},{2,3},{3,2},{4,5},{5,4},{6,7},{7,6},{8,9},{9,8},{10,11... | collective-permute-start | bytes 98312 | tf_op jit(solution)/shard_map/ppermute | solution.py:557
  10.9 3.9 %collective-permute-start.9 = (bf16[16,1024]{1,0:T(8,128)(2,1)S(1)}, bf16[16,1024]{1,0:T(8,128)(2,1)S(1)}, u32[]{:S(2)}, u32[]{:S(2)}) collective-permute-start(bf16[16,1024]{1,0:T(8,128)(2,1)S(1)} %get-tuple-element.204), channel_id=1, source_target_pairs={{0,2},{1,3},{2,0},{3,1},{4,6},{5,7},{6,4},{7,5},{8,10},{9,11},{10,... | collective-permute-start | bytes 98312 | tf_op jit(solution)/shard_map/ppermute | solution.py:557
  12.0 16.5 %slice-start.6 = ((s8[12582912]{0:T(1024)(128)(4,1)}), s8[4194304]{0:T(1024)(128)(4,1)S(1)}, s32[]{:S(2)}) async-start(s8[12582912]{0:T(1024)(128)(4,1)} %bitcast.58), calls=%async_computation.6 | async-start | bytes 8388608
  12.0 16.5 %slice-start.7 = ((s8[12582912]{0:T(1024)(128)(4,1)}), s8[4194304]{0:T(1024)(128)(4,1)S(1)}, s32[]{:S(2)}) async-start(s8[12582912]{0:T(1024)(128)(4,1)} %bitcast.58), calls=%async_computation.7 | async-start | bytes 8388608
  14.9 8.6 %copy-start.1 = (s32[64]{0:T(128)S(1)}, s32[64]{0:T(128)}, u32[]{:S(2)}) copy-start(s32[64]{0:T(128)} %param.20) | copy-start | bytes 772
  14.9 13.6 %slice-start.8 = ((s8[12582912]{0:T(1024)(128)(4,1)}), s8[4194304]{0:T(1024)(128)(4,1)S(1)}, s32[]{:S(2)}) async-start(s8[12582912]{0:T(1024)(128)(4,1)} %bitcast.58), calls=%async_computation.8 | async-start | bytes 8388608
  14.9 6.8 %collective-permute-start.11 = (bf16[16,1152]{1,0:T(8,128)(2,1)S(1)}, bf16[16,1152]{1,0:T(8,128)(2,1)S(1)}, u32[]{:S(2)}, u32[]{:S(2)}) collective-permute-start(bf16[16,1152]{1,0:T(8,128)(2,1)S(1)} %add.82.refs_1_.refs_0_), channel_id=1, source_target_pairs={{0,12},{4,8},{8,4},{12,0},{1,13},{5,9},{9,5},{13,1},{2,14},{6,10},... | collective-permute-start | bytes 110600 | tf_op jit(solution)/shard_map/ppermute | solution.py:557
  18.5 4.9 %collective-permute-start.12 = (bf16[16,1152]{1,0:T(8,128)(2,1)S(1)}, bf16[16,1152]{1,0:T(8,128)(2,1)S(1)}, u32[]{:S(2)}, u32[]{:S(2)}) collective-permute-start(bf16[16,1152]{1,0:T(8,128)(2,1)S(1)} %add.82.refs_1_.refs_0_), channel_id=1, source_target_pairs={{0,8},{4,12},{8,0},{12,4},{1,9},{5,13},{9,1},{13,5},{2,10},{6,14},... | collective-permute-start | bytes 110600 | tf_op jit(solution)/shard_map/ppermute | solution.py:557
  18.5 4.9 %collective-permute-start.13 = (bf16[16,1152]{1,0:T(8,128)(2,1)S(1)}, bf16[16,1152]{1,0:T(8,128)(2,1)S(1)}, u32[]{:S(2)}, u32[]{:S(2)}) collective-permute-start(bf16[16,1152]{1,0:T(8,128)(2,1)S(1)} %add.82.refs_1_.refs_0_), channel_id=1, source_target_pairs={{0,4},{4,0},{8,12},{12,8},{1,5},{5,1},{9,13},{13,9},{2,6},{6,2},{1... | collective-permute-start | bytes 110600 | tf_op jit(solution)/shard_map/ppermute | solution.py:557
  19.3 9.1 %slice-start.3 = ((s8[12582912]{0:T(1024)(128)(4,1)}), s8[4194304]{0:T(1024)(128)(4,1)S(1)}, s32[]{:S(2)}) async-start(s8[12582912]{0:T(1024)(128)(4,1)} %bitcast.56), calls=%async_computation.3 | async-start | bytes 8388608
  19.3 9.1 %slice-start.4 = ((s8[12582912]{0:T(1024)(128)(4,1)}), s8[4194304]{0:T(1024)(128)(4,1)S(1)}, s32[]{:S(2)}) async-start(s8[12582912]{0:T(1024)(128)(4,1)} %bitcast.56), calls=%async_computation.4 | async-start | bytes 8388608
  24.3 4.2 %slice-start.5 = ((s8[12582912]{0:T(1024)(128)(4,1)}), s8[4194304]{0:T(1024)(128)(4,1)S(1)}, s32[]{:S(2)}) async-start(s8[12582912]{0:T(1024)(128)(4,1)} %bitcast.56), calls=%async_computation.5 | async-start | bytes 8388608
  27.3 10.0 %collective-permute-start.17 = (bf16[208,256]{1,0:T(8,128)(2,1)S(1)}, bf16[208,256]{1,0:T(8,128)(2,1)S(1)}, u32[]{:S(2)}, u32[]{:S(2)}) collective-permute-start(bf16[208,256]{1,0:T(8,128)(2,1)S(1)} %get-tuple-element.211.refs_4_.refs_0_), channel_id=1, source_target_pairs={{0,2},{2,0},{1,3},{3,1},{4,6},{6,4},{5,7},{7,5},{8,10},{10,8},{9,1... | collective-permute-start | bytes 319496 | tf_op jit(solution)/shard_map/ppermute | solution.py:671
  28.5 8.8 %slice-start = ((s8[12582912]{0:T(1024)(128)(4,1)}), s8[4194304]{0:T(1024)(128)(4,1)S(1)}, s32[]{:S(2)}) async-start(s8[12582912]{0:T(1024)(128)(4,1)} %bitcast.54), calls=%async_computation | async-start | bytes 8388608
  28.5 8.8 %slice-start.1 = ((s8[12582912]{0:T(1024)(128)(4,1)}), s8[4194304]{0:T(1024)(128)(4,1)S(1)}, s32[]{:S(2)}) async-start(s8[12582912]{0:T(1024)(128)(4,1)} %bitcast.54), calls=%async_computation.1 | async-start | bytes 8388608
  31.4 6.0 %slice-start.2 = ((s8[12582912]{0:T(1024)(128)(4,1)}), s8[4194304]{0:T(1024)(128)(4,1)S(1)}, s32[]{:S(2)}) async-start(s8[12582912]{0:T(1024)(128)(4,1)} %bitcast.54), calls=%async_computation.2 | async-start | bytes 8388608
  31.4 7.0 %collective-permute-start.16 = (bf16[208,256]{1,0:T(8,128)(2,1)S(1)}, bf16[208,256]{1,0:T(8,128)(2,1)S(1)}, u32[]{:S(2)}, u32[]{:S(2)}) collective-permute-start(bf16[208,256]{1,0:T(8,128)(2,1)S(1)} %gate_up_1.1.refs_4_.refs_0_), channel_id=1, source_target_pairs={{0,2},{2,0},{1,3},{3,1},{4,6},{6,4},{5,7},{7,5},{8,10},{10,8},{9,1... | collective-permute-start | bytes 319496 | tf_op jit(solution)/shard_map/ppermute | solution.py:671
  35.2 4.8 %collective-permute-start.15 = (bf16[208,256]{1,0:T(8,128)(2,1)S(1)}, bf16[208,256]{1,0:T(8,128)(2,1)S(1)}, u32[]{:S(2)}, u32[]{:S(2)}) collective-permute-start(bf16[208,256]{1,0:T(8,128)(2,1)S(1)} %gate_up_2.1.refs_0_), channel_id=1, source_target_pairs={{0,2},{2,0},{1,3},{3,1},{4,6},{6,4},{5,7},{7,5},{8,10},{10,8},{9,1... | collective-permute-start | bytes 319496 | tf_op jit(solution)/shard_map/ppermute | solution.py:671
  36.4 4.7 %collective-permute-start.14 = (bf16[4,1024]{1,0:T(4,128)(2,1)S(1)}, bf16[4,1024]{1,0:T(4,128)(2,1)S(1)}, u32[]{:S(2)}, u32[]{:S(2)}) collective-permute-start(bf16[4,1024]{1,0:T(4,128)(2,1)S(1)} %get-tuple-element.212), channel_id=1, source_target_pairs={{0,2},{2,0},{1,3},{3,1},{4,6},{6,4},{5,7},{7,5},{8,10},{10,8},{9,1... | collective-permute-start | bytes 24584 | tf_op jit(solution)/shard_map/ppermute | solution.py:636
  41.1 1.4 %collective-permute-start.18 = (f32[64,512]{1,0:T(8,128)S(1)}, f32[64,512]{1,0:T(8,128)S(1)}, u32[]{:S(2)}, u32[]{:S(2)}) collective-permute-start(f32[64,512]{1,0:T(8,128)S(1)} %get-tuple-element.220), channel_id=1, source_target_pairs={{0,1},{1,0},{2,3},{3,2},{4,5},{5,4},{6,7},{7,6},{8,9},{9,8},{10,11... | collective-permute-start | bytes 393224 | tf_op jit(solution)/shard_map/ppermute | solution.py:557
  42.5 5.9 %collective-permute-start.19 = (bf16[16,512]{1,0:T(8,128)(2,1)S(1)}, bf16[16,512]{1,0:T(8,128)(2,1)S(1)}, u32[]{:S(2)}, u32[]{:S(2)}) collective-permute-start(bf16[16,512]{1,0:T(8,128)(2,1)S(1)} %get-tuple-element.228), channel_id=1, source_target_pairs={{0,12},{4,8},{8,4},{12,0},{1,13},{5,9},{9,5},{13,1},{2,14},{6,10},... | collective-permute-start | bytes 49160 | tf_op jit(solution)/shard_map/ppermute | solution.py:557
  44.5 4.7 %collective-permute-start.20 = (bf16[16,512]{1,0:T(8,128)(2,1)S(1)}, bf16[16,512]{1,0:T(8,128)(2,1)S(1)}, u32[]{:S(2)}, u32[]{:S(2)}) collective-permute-start(bf16[16,512]{1,0:T(8,128)(2,1)S(1)} %get-tuple-element.229), channel_id=1, source_target_pairs={{0,8},{4,12},{8,0},{12,4},{1,9},{5,13},{9,1},{13,5},{2,10},{6,14},... | collective-permute-start | bytes 49160 | tf_op jit(solution)/shard_map/ppermute | solution.py:557
  44.7 4.6 %collective-permute-start.21 = (bf16[16,512]{1,0:T(8,128)(2,1)S(1)}, bf16[16,512]{1,0:T(8,128)(2,1)S(1)}, u32[]{:S(2)}, u32[]{:S(2)}) collective-permute-start(bf16[16,512]{1,0:T(8,128)(2,1)S(1)} %get-tuple-element.230), channel_id=1, source_target_pairs={{0,4},{4,0},{8,12},{12,8},{1,5},{5,1},{9,13},{13,9},{2,6},{6,2},{1... | collective-permute-start | bytes 49160 | tf_op jit(solution)/shard_map/ppermute | solution.py:557
